TPU v7x, 512 devices: a whole 4x4x16 slice. The times are simulated.
512 devices in a mesh: dp: 4 (over y), expert: 128 (over z, x, core).
Axes of the slice: x: 4, y: 4, z: 16, core: 2. Of those that a mesh axis runs over, the one named last changes fastest.
Arguments:
- grad_out: bfloat16 [16384, 4096], P(('dp', 'expert')), may hold values from -6 to 6
- expert_ids: int32 [16384, 8], P(('dp', 'expert')), may hold values from 0 to 127, all different within a row; in each aligned block of 32 rows (0 to 31, 32 to 63, ...) at most 2 rows name the same one
- route_weights: float32 [16384, 8], P(('dp', 'expert')), may hold values from 0.02 to 0.2
- hidden_act: bfloat16 [4, 128, 256, 1536], P('dp', 'expert'), may hold values from -6 to 6
- projection: bfloat16 [128, 1536, 256], P('expert', 'dp'), may hold values from -0.15625 to 0.15625
Outputs:
- projected_grad: bfloat16 [128, 4096, 256], P('expert', 'dp')
Inputs may be any that keep to these rules, and one draw needn't show every extreme that they name: `expert_ids`: each row names 8 different experts. Among the 32 tokens of one device (aligned blocks of rows), no expert is named more than 2 times, a bound that some block reaches.
All inputs are finite; a program needn't handle non-finite values.
Results may differ from a plain program's by a relative error of at most 0.0058.
Values may be sent and summed in bfloat16 or wider, within the bound.
No kernel may reach another device: no remote copies, remote signals or barrier semaphores. Data moves between devices by JAX's collectives and lax.ppermute only.
A program may use at most 64 MiB of HBM per device.

v0:
```python
import jax
import jax.numpy as jnp
from jax import lax
from jax.sharding import PartitionSpec as P


def shards(grad_out, expert_ids, route_weights, hidden_act, projection):
    token_count = grad_out.shape[0]
    width = grad_out.shape[1]
    top_count = expert_ids.shape[1]
    expert_count = lax.axis_size("expert")
    slot_count = hidden_act.shape[2]
    capacity = slot_count // expert_count
    route_total = token_count * top_count
    routed = expert_ids.reshape(-1)
    onehot = (routed[:, None] == jnp.arange(expert_count, dtype=jnp.int32)[None, :]).astype(
        jnp.int32
    )
    earlier = jnp.cumsum(onehot, axis=0) - onehot
    position = jnp.sum(earlier * onehot, axis=1)
    slot = routed * capacity + position
    table = jnp.full((expert_count * capacity,), -1, jnp.int32)
    table = table.at[slot].set(jnp.arange(route_total, dtype=jnp.int32))
    valid = table >= 0
    picked = jnp.maximum(table, 0)
    rows = grad_out[picked // top_count].astype(jnp.float32)
    weight = route_weights.reshape(-1)[picked]
    weighted = jnp.where(valid[:, None], weight[:, None] * rows, 0.0).astype(jnp.bfloat16)
    outgoing = weighted.reshape(expert_count, capacity, width)
    hidden = hidden_act[0, 0]
    reduced = jnp.dot(
        hidden,
        lax.all_gather(projection[0], "dp", axis=0, tiled=True),
        preferred_element_type=jnp.float32,
    ).astype(jnp.bfloat16)
    arrived = lax.all_to_all(outgoing, "expert", split_axis=0, concat_axis=0, tiled=True).reshape(
        slot_count, width
    )
    share = lax.psum_scatter(
        lax.dot_general(
            arrived, reduced, (((0,), (0,)), ((), ())), preferred_element_type=jnp.float32
        ),
        "dp",
        scatter_dimension=0,
        tiled=True,
    )
    return share.astype(jnp.bfloat16)[None]


def solution(mesh):
    in_specs = (
        P(("dp", "expert"), None),
        P(("dp", "expert"), None),
        P(("dp", "expert"), None),
        P("dp", "expert", None, None),
        P("expert", "dp", None),
    )
    out_specs = P("expert", "dp", None)
    return jax.shard_map(shards, mesh=mesh, in_specs=in_specs, out_specs=out_specs, check_vma=False)
```

profile of v0, /device:TPU:1, one launch (start us, length us, event | category | flops | bytes accessed | tf_op | source)
XLA Modules:
  0.0 209.0 jit_solution(662351124627535418)
XLA Ops:
  6.5 0.0 copy-start
  6.5 0.0 copy-start.1
  6.5 0.8 copy.7
  7.4 0.1 eq.29
  7.5 0.1 eq.25
  7.6 0.7 broadcast_multiply_fusion
  8.3 0.1 copy.9
  8.4 0.2 fusion.5
  8.7 0.1 copy.6
  8.8 0.1 mul.32
  8.8 0.2 fusion.7
  9.1 1.4 scatter_custom_fusion
  10.5 0.0 copy-done.1
  10.5 1.8 gather_fusion.1
  12.4 0.0 copy-start.3
  12.4 4.0 %reshape.71 = f32[128,2,4096]{2,1,0:T(2,128)} reshape(bf16[256,4096]{1,0:T(8,128)(2,1)S(1)} %gather_fusion.1) | data formatting | bytes 6291456 | tf_op jit(solution)/shard_map/convert_element_type | solution.py:26
  16.4 0.0 copy-done.3
  16.4 0.1 copy.11
  16.4 0.1 reshape.69
  16.5 1.9 gather_fusion
  18.5 0.1 mul.34
  18.6 0.2 broadcast_in_dim.31
  18.8 6.9 %select_convert_fusion = bf16[128,2,4096]{2,1,0:T(2,128)(2,1)} fusion(f32[128,2,4096]{2,1,0:T(2,128)} %reshape.71, pred[128,2]{1,0:T(8,128)(4,1)S(1)} %broadcast_in_dim.31, f32[128,2]{1,0:T(8,128)S(1)} %mul.34), kind=kLoop, calls=%fused_computation.3 | loop fusion | flops 3145728 | bytes 6292736 | tf_op jit(solution)/shard_map/convert_element_type | solution.py:28
  25.7 0.0 copy-start.2
  25.7 20.5 %all-to-all-start = ((bf16[128,2,4096]{2,1,0:T(2,128)(2,1)}), bf16[128,2,4096]{2,1,0:T(2,128)(2,1)S(1)}, u32[]{:S(2)}, u32[]{:S(2)}) async-start(bf16[128,2,4096]{2,1,0:T(2,128)(2,1)} %select_convert_fusion), calls=%async_computation | async-start | bytes 4194304 | tf_op jit(solution)/shard_map/all_to_all | solution.py:36
  46.3 0.0 reduce-scatter.2.cloned.1.call-start
  46.3 0.0 copy-done.2
  46.3 13.2 %all-gather = bf16[1,1536,256]{2,1,0:T(8,128)(2,1)} all-gather(bf16[1,384,256]{2,1,0:T(8,128)(2,1)S(1)} %copy-done.2), channel_id=2, replica_groups=mesh['dp'=4,'expert'=128] {'dp'}, dimensions={1}, use_global_device_ids=true | all-gather | bytes 983040 | tf_op jit(solution)/shard_map/all_gather | solution.py:33
  59.5 82.7 %all-to-all-done = bf16[128,2,4096]{2,1,0:T(2,128)(2,1)S(1)} async-done(((bf16[128,2,4096]{2,1,0:T(2,128)(2,1)}), bf16[128,2,4096]{2,1,0:T(2,128)(2,1)S(1)}, u32[]{:S(2)}, u32[]{:S(2)}) %all-to-all-start) | async-done | bytes 2097184 | tf_op jit(solution)/shard_map/all_to_all | solution.py:36
  142.2 2.2 %reshape.70 = bf16[256,4096]{1,0:T(8,128)(2,1)} reshape(bf16[128,2,4096]{2,1,0:T(2,128)(2,1)S(1)} %all-to-all-done) | data formatting | bytes 4194304 | tf_op jit(solution)/shard_map/reshape | solution.py:36
  144.4 0.0 copy-done
  144.4 5.1 %fusion = f32[4096,256]{1,0:T(8,128)} fusion(bf16[256,4096]{1,0:T(8,128)(2,1)} %reshape.70, bf16[1,1536,256]{2,1,0:T(8,128)(2,1)} %all-gather, bf16[1,1,256,1536]{3,2,1,0:T(8,128)(2,1)S(1)} %copy-done), kind=kOutput, calls=%fused_computation.5 | convolution fusion | flops 738263040 | bytes 7864320 | tf_op jit(solution)/shard_map/dot_general | solution.py:40
  149.5 0.0 reduce-scatter.2.cloned.1.call-update
  149.5 50.6 %reduce-scatter.2.cloned.1.call-done = f32[1024,256]{1,0:T(8,128)} async-done(((f32[4096,256]{1,0:T(8,128)}), f32[1024,256]{1,0:T(8,128)}) %reduce-scatter.2.cloned.1.call-update) | async-done | bytes 1048592 | tf_op jit(solution)/shard_map/reduce_scatter | solution.py:39
  200.1 2.1 convert_bitcast_fusion
  (11 shorter events, 0.1 us)
Async XLA Ops:
  6.5 137.9 %copy-start = (bf16[1,1,256,1536]{3,2,1,0:T(8,128)(2,1)S(1)}, bf16[1,1,256,1536]{3,2,1,0:T(8,128)(2,1)}, u32[]{:S(2)}) copy-start(bf16[1,1,256,1536]{3,2,1,0:T(8,128)(2,1)} %param.8) | copy-start | bytes 2359300
  6.5 4.0 %copy-start.1 = (bf16[32,4096]{1,0:T(8,128)(2,1)S(1)}, bf16[32,4096]{1,0:T(8,128)(2,1)}, u32[]{:S(2)}) copy-start(bf16[32,4096]{1,0:T(8,128)(2,1)} %param.5) | copy-start | bytes 786436
  12.4 4.0 %copy-start.3 = (f32[32,8]{0,1:T(8,128)S(1)}, f32[32,8]{0,1:T(8,128)}, u32[]{:S(2)}) copy-start(f32[32,8]{0,1:T(8,128)} %param.7) | copy-start | bytes 3076
  25.7 20.6 %copy-start.2 = (bf16[1,384,256]{2,1,0:T(8,128)(2,1)S(1)}, bf16[1,384,256]{2,1,0:T(8,128)(2,1)}, u32[]{:S(2)}) copy-start(bf16[1,384,256]{2,1,0:T(8,128)(2,1)} %param.9) | copy-start | bytes 589828
  25.7 116.4 %all-to-all-start = ((bf16[128,2,4096]{2,1,0:T(2,128)(2,1)}), bf16[128,2,4096]{2,1,0:T(2,128)(2,1)S(1)}, u32[]{:S(2)}, u32[]{:S(2)}) async-start(bf16[128,2,4096]{2,1,0:T(2,128)(2,1)} %select_convert_fusion), calls=%async_computation | async-start | bytes 4194304 | tf_op jit(solution)/shard_map/all_to_all | solution.py:36
  46.3 153.9 %reduce-scatter.2.cloned.1.call-start = ((), (), s32[]{:S(2)}) async-start(), calls=%async_computation.2 | async-start | bytes 5242880 | tf_op jit(solution)/shard_map/reduce_scatter | solution.py:39
Sparse Core Ops, SparseCore 0:
  149.7 50.4 reduce-scatter.1
where the time goes:
time: 209 us
  waiting for transfers between devices  133 us (64%)
  starting transfers between devices  20.6 us (10%)
  between operations  13.5 us (6%)
  local copies, waits for them, and re-layouts  13.2 us (6%)
  blocking collectives  13.2 us (6%)
  other arithmetic  10.2 us (5%)
  matrix products  5.11 us (2%)
    all_to_all x1, waiting for transfers between devices, shards(): lax.all_to_all(outgoing, 'expert', split_axis=0, concat_axis=0, tiled=True)  82.7 us
    reduce_scatter x1, waiting for transfers between devices, shards(): lax.psum_scatter(lax.dot_general(arrived, reduced, (((0,), (0,)), ((), ()...  50.6 us
    all_to_all x1, starting transfers between devices, shards(): lax.all_to_all(outgoing, 'expert', split_axis=0, concat_axis=0, tiled=True)  20.5 us
    all_gather x1, blocking collectives, shards(): lax.all_gather(projection[0], 'dp', axis=0, tiled=True)  13.2 us
    convert_element_type x1, other arithmetic, shards(): jnp.where(valid[:, None], weight[:, None] * rows, 0.0).astype(jnp.bfloat16)  6.93 us
    dot_general x1, matrix products, shards(): lax.dot_general(arrived, reduced, (((0,), (0,)), ((), ())), preferred_ele...  5.11 us
  transfers between devices with their start and end apart: 2, of which 2 were waited for; matrix products, arithmetic and copies ran while one was open for 0% of the time, Pallas kernels for 0%

commit v1 on v0

v1 whole, which is shorter than its diff:
```python
import jax
import jax.numpy as jnp
from jax import lax
from jax.experimental import pallas as pl
from jax.experimental.pallas import tpu as pltpu
from jax.sharding import PartitionSpec as P


def weigh_kernel(grad_ref, ids_ref, weight_ref, out_ref):
    tokens = grad_ref.shape[0]
    top_count = ids_ref.shape[0]
    parts, slots, width = out_ref.shape
    row = lax.broadcasted_iota(jnp.int32, (slots, tokens), 0)
    expert = row // 2
    hit = jnp.zeros((slots, tokens), jnp.float32)
    scale = jnp.zeros((slots, tokens), jnp.float32)
    for k in range(top_count):
        same = ids_ref[k : k + 1, :] == expert
        hit = jnp.where(same, 1.0, hit)
        scale = jnp.where(same, weight_ref[k : k + 1, :], scale)
    before = lax.broadcasted_iota(jnp.int32, (tokens, tokens), 0) < lax.broadcasted_iota(
        jnp.int32, (tokens, tokens), 1
    )
    rank = jnp.dot(
        hit.astype(jnp.bfloat16),
        before.astype(jnp.float32).astype(jnp.bfloat16),
        preferred_element_type=jnp.float32,
    )
    wanted = (row % 2).astype(jnp.float32)
    chosen = jnp.where((hit > 0.5) & (jnp.abs(rank - wanted) < 0.5), 1.0, 0.0)
    weight = jnp.sum(chosen * scale, axis=1, keepdims=True)
    chosen = chosen.astype(jnp.bfloat16)
    for part in range(parts):
        rows = jnp.dot(
            chosen, grad_ref[:, part * width : (part + 1) * width], preferred_element_type=jnp.float32
        )
        out_ref[part] = (weight * rows).astype(jnp.bfloat16)


def shards(grad_out, expert_ids, route_weights, hidden_act, projection):
    replicas = lax.axis_size("dp")
    expert_count = lax.axis_size("expert")
    width = grad_out.shape[1] // replicas
    slot_count = hidden_act.shape[2]
    capacity = slot_count // expert_count
    weighted = pl.pallas_call(
        weigh_kernel,
        out_shape=jax.ShapeDtypeStruct((replicas, slot_count, width), jnp.bfloat16),
    )(grad_out, expert_ids.T, route_weights.T)
    outgoing = weighted.reshape(replicas * expert_count, capacity, width)
    arrived = lax.all_to_all(
        outgoing, ("dp", "expert"), split_axis=0, concat_axis=0, tiled=True
    ).reshape(replicas * slot_count, width)
    reduced = jnp.dot(
        hidden_act[0, 0],
        lax.all_gather(projection[0], "dp", axis=0, tiled=True),
        preferred_element_type=jnp.float32,
    ).astype(jnp.bfloat16)
    reduced = lax.all_gather(reduced, "dp", axis=0, tiled=True)
    share = lax.dot_general(
        arrived, reduced, (((0,), (0,)), ((), ())), preferred_element_type=jnp.float32
    )
    return share.astype(jnp.bfloat16)[None]


def solution(mesh):
    in_specs = (
        P(("dp", "expert"), None),
        P(("dp", "expert"), None),
        P(("dp", "expert"), None),
        P("dp", "expert", None, None),
        P("expert", "dp", None),
    )
    out_specs = P("expert", "dp", None)
    return jax.shard_map(shards, mesh=mesh, in_specs=in_specs, out_specs=out_specs, check_vma=False)
```

time: 209 us -> 140 us (0.67)
  waiting for transfers between devices: 133 us -> 76.2 us
  between operations: 13.5 us -> 0.03 us
  blocking collectives: 13.2 us -> 25.8 us
  other arithmetic: 10.2 us -> 0 us
  local copies, waits for them, and re-layouts: 13.2 us -> 6.31 us
  starting transfers between devices: 20.6 us -> 24.3 us
  Pallas kernels: 0 us -> 3.29 us
    reduce_scatter x1 -> x0, waiting for transfers between devices: 50.6 us -> none  [shards(): lax.psum_scatter(lax.dot_general(arrived, reduced, (((0,), (0,)), ((), ()...]
    all_gather x0 -> x1, blocking collectives: none -> 11.9 us  [shards(): reduced = lax.all_gather(reduced, 'dp', axis=0, tiled=True)]
    convert_element_type x1 -> x0, other arithmetic: 6.93 us -> none  [shards(): jnp.where(valid[:, None], weight[:, None] * rows, 0.0).astype(jnp.bfloat16)]
    all_to_all x1, waiting for transfers between devices: 82.7 us -> 76.2 us  [shards(): lax.all_to_all(outgoing, ('dp', 'expert'), split_axis=0, concat_axis=0, t...]
    convert_element_type x1 -> x0, local copies, waits for them, and re-layouts: 4 us -> none  [shards(): rows = grad_out[picked // top_count].astype(jnp.float32)]
    reshape x2, local copies, waits for them, and re-layouts: 2.32 us -> 6.3 us  [the longest x1 4.1 us: shards(): outgoing = weighted.reshape(replicas * expert_count, capacity, width)]
    gather x2 -> x0, local copies, waits for them, and re-layouts: 3.79 us -> none  [the longest x1 1.95 us: shards(): weight = route_weights.reshape(-1)[picked]]
    all_to_all x1, starting transfers between devices: 20.5 us -> 24.3 us  [shards(): lax.all_to_all(outgoing, ('dp', 'expert'), split_axis=0, concat_axis=0, t...]
  transfers between devices with their start and end apart: 2 -> 1, of which waited for: 2 -> 1; matrix products, arithmetic and copies ran while one was open for 0% -> 0% of each run, Pallas kernels for 0% -> 0%
where the time goes in v1:
time: 140 us; the launch traced here: 139 us
  waiting for transfers between devices  76.2 us (54%)
  blocking collectives  25.8 us (18%)
  starting transfers between devices  24.3 us (17%)
  local copies, waits for them, and re-layouts  6.31 us (5%)
  matrix products  3.52 us (3%)
  Pallas kernels  3.29 us (2%)
    all_to_all x1, waiting for transfers between devices, shards(): lax.all_to_all(outgoing, ('dp', 'expert'), split_axis=0, concat_axis=0, t...  76.2 us
    all_to_all x1, starting transfers between devices, shards(): lax.all_to_all(outgoing, ('dp', 'expert'), split_axis=0, concat_axis=0, t...  24.3 us
    all_gather x1, blocking collectives, shards(): lax.all_gather(projection[0], 'dp', axis=0, tiled=True)  13.9 us
    all_gather x1, blocking collectives, shards(): reduced = lax.all_gather(reduced, 'dp', axis=0, tiled=True)  11.9 us
    reshape x1, local copies, waits for them, and re-layouts, shards(): outgoing = weighted.reshape(replicas * expert_count, capacity, width)  4.1 us
    pallas_call x1, Pallas kernels, shards(): pl.pallas_call(weigh_kernel, out_shape=jax.ShapeDtypeStruct((replicas, sl...  3.29 us
    dot_general x1, matrix products, shards(): lax.dot_general(arrived, reduced, (((0,), (0,)), ((), ())), preferred_ele...  3.15 us
  transfers between devices with their start and end apart: 1, of which 1 were waited for; matrix products, arithmetic and copies ran while one was open for 0% of the time, Pallas kernels for 0%

profile of v1, /device:TPU:1, one launch (start us, length us, event | category | flops | bytes accessed | tf_op | source)
XLA Modules:
  0.0 139.4 jit_solution(6451455223477363354)
XLA Ops:
  0.0 0.0 copy-start
  0.0 3.3 %shard_map.55 = bf16[4,256,1024]{2,1,0:T(8,128)(2,1)} custom-call(bf16[32,4096]{1,0:T(8,128)(2,1)} %grad_ref.1, s32[8,32]{1,0:T(8,128)} %bitcast.12, f32[8,32]{1,0:T(8,128)} %bitcast.13), custom_call_target="tpu_custom_call" | custom-call | tf_op jit(solution)/shard_map/pallas_call | solution.py:46
  3.3 4.1 %reshape.6 = bf16[512,2,1024]{2,1,0:T(2,128)(2,1)} reshape(bf16[4,256,1024]{2,1,0:T(8,128)(2,1)} %shard_map.55) | data formatting | bytes 4194304 | tf_op jit(solution)/shard_map/reshape | solution.py:50
  7.4 0.0 copy-start.1
  7.4 24.3 %all-to-all-start = ((bf16[512,2,1024]{2,1,0:T(2,128)(2,1)}), bf16[512,2,1024]{2,1,0:T(2,128)(2,1)S(1)}, u32[]{:S(2)}, u32[]{:S(2)}) async-start(bf16[512,2,1024]{2,1,0:T(2,128)(2,1)} %reshape.6), calls=%async_computation | async-start | bytes 4194304 | tf_op jit(solution)/shard_map/all_to_all | solution.py:51
  31.7 0.0 copy-done.1
  31.7 13.9 %all-gather = bf16[1,1536,256]{2,1,0:T(8,128)(2,1)S(1)} all-gather(bf16[1,384,256]{2,1,0:T(8,128)(2,1)S(1)} %copy-done.1), channel_id=2, replica_groups=mesh['dp'=4,'expert'=128] {'dp'}, dimensions={1}, use_global_device_ids=true | all-gather | bytes 983040 | tf_op jit(solution)/shard_map/all_gather | solution.py:56
  45.7 0.0 copy-done
  45.7 0.4 convolution_convert_fusion.1
  46.0 11.9 %all_gather.7 = bf16[1024,256]{1,0:T(8,128)(2,1)S(1)} all-gather(bf16[256,256]{1,0:T(8,128)(2,1)S(1)} %convolution_convert_fusion.1), channel_id=1, replica_groups=mesh['dp'=4,'expert'=128] {'dp'}, dimensions={0}, use_global_device_ids=true | all-gather | bytes 655360 | tf_op jit(solution)/shard_map/all_gather | solution.py:59
  57.9 76.2 %all-to-all-done = bf16[512,2,1024]{2,1,0:T(2,128)(2,1)S(1)} async-done(((bf16[512,2,1024]{2,1,0:T(2,128)(2,1)}), bf16[512,2,1024]{2,1,0:T(2,128)(2,1)S(1)}, u32[]{:S(2)}, u32[]{:S(2)}) %all-to-all-start) | async-done | bytes 2097184 | tf_op jit(solution)/shard_map/all_to_all | solution.py:51
  134.1 2.2 %reshape.7 = bf16[1024,1024]{1,0:T(8,128)(2,1)} reshape(bf16[512,2,1024]{2,1,0:T(2,128)(2,1)S(1)} %all-to-all-done) | data formatting | bytes 4194304 | tf_op jit(solution)/shard_map/reshape | solution.py:53
  136.3 3.1 %fusion = bf16[1,1024,256]{2,1,0:T(8,128)(2,1)} fusion(bf16[1024,1024]{1,0:T(8,128)(2,1)} %reshape.7, bf16[1024,256]{1,0:T(8,128)(2,1)S(1)} %all_gather.7), kind=kOutput, calls=%fused_computation.1 | convolution fusion | flops 537133056 | bytes 3145728 | tf_op jit(solution)/shard_map/dot_general | solution.py:60
Async XLA Ops:
  0.0 45.7 %copy-start = (bf16[1,1,256,1536]{3,2,1,0:T(8,128)(2,1)S(1)}, bf16[1,1,256,1536]{3,2,1,0:T(8,128)(2,1)}, u32[]{:S(2)}) copy-start(bf16[1,1,256,1536]{3,2,1,0:T(8,128)(2,1)} %param.8) | copy-start | bytes 2359300
  7.4 24.3 %copy-start.1 = (bf16[1,384,256]{2,1,0:T(8,128)(2,1)S(1)}, bf16[1,384,256]{2,1,0:T(8,128)(2,1)}, u32[]{:S(2)}) copy-start(bf16[1,384,256]{2,1,0:T(8,128)(2,1)} %param.9) | copy-start | bytes 589828
  7.4 126.7 %all-to-all-start = ((bf16[512,2,1024]{2,1,0:T(2,128)(2,1)}), bf16[512,2,1024]{2,1,0:T(2,128)(2,1)S(1)}, u32[]{:S(2)}, u32[]{:S(2)}) async-start(bf16[512,2,1024]{2,1,0:T(2,128)(2,1)} %reshape.6), calls=%async_computation | async-start | bytes 4194304 | tf_op jit(solution)/shard_map/all_to_all | solution.py:51

commit v2 on v0

v2 whole, which is shorter than its diff:
```python
import numpy as np

import jax
import jax.numpy as jnp
from jax import lax
from jax.experimental import pallas as pl
from jax.experimental.pallas import tpu as pltpu
from jax.sharding import Mesh, PartitionSpec as P


PLANES = 16
LEAP = 4
META = 128
GROUP = 16
F32, BF16 = jnp.float32, jnp.bfloat16

STAY = (0, (0, 1, 2))
UP1, DOWN1 = (1, (0, 1, 2)), (-1, (0, 1, 2))
UP2, DOWN2 = (2, (0, 1)), (-2, (0, 2))
UP3, DOWN3 = (3, (1,)), (-3, (2,))
UP4 = (4, (1,))
MESSAGES = (STAY, UP1, DOWN1, UP2, DOWN2, UP3, DOWN3, UP4)
SMALL = pltpu.CompilerParams(vmem_limit_bytes=12 * 1024 * 1024)
START = (0, -LEAP, LEAP)


def origin(step, block):
    return START[block] - step


ORDER = [origin(step, block) for step, blocks in MESSAGES for block in blocks]


def pack_kernel(grad_ref, ids_ref, weight_ref, out_ref):
    tokens, width = grad_ref.shape
    high = weight_ref[...].astype(BF16).astype(F32)
    rest = weight_ref[...] - high
    middle = rest.astype(BF16).astype(F32)
    low = rest - middle
    parts = [ids_ref[...].astype(F32), high, middle, low]
    used = sum(part.shape[0] for part in parts)
    meta = jnp.concatenate(parts + [jnp.zeros((META - used, tokens), F32)], axis=0)
    same = lax.broadcasted_iota(jnp.int32, (tokens, tokens), 0) == lax.broadcasted_iota(
        jnp.int32, (tokens, tokens), 1
    )
    turned = lax.dot_general(
        same.astype(F32).astype(BF16),
        meta.astype(BF16),
        (((1,), (1,)), ((), ())),
        preferred_element_type=F32,
    )
    out_ref[:, :width] = grad_ref[...]
    out_ref[:, width:] = turned.astype(BF16)


def pick_kernel(place_ref, own_ref, behind_ref, ahead_ref, *out_refs):
    tokens = own_ref.shape[0]
    width = own_ref.shape[1] - META
    top_count = 8
    plane, sign = place_ref[0], place_ref[1]
    square = (META, META)
    same = lax.broadcasted_iota(jnp.int32, square, 0) == lax.broadcasted_iota(jnp.int32, square, 1)
    same = same.astype(F32).astype(BF16)
    before = lax.broadcasted_iota(jnp.int32, (tokens, tokens), 0) < lax.broadcasted_iota(
        jnp.int32, (tokens, tokens), 1
    )
    before = before.astype(F32).astype(BF16)
    row = lax.broadcasted_iota(jnp.int32, (GROUP, tokens), 0)
    for block, ref in enumerate((own_ref, behind_ref, ahead_ref)):
        meta = lax.dot_general(
            same, ref[:, width:], (((1,), (1,)), ((), ())), preferred_element_type=F32
        )
        ids = meta[:top_count].astype(jnp.int32)
        weights = (
            meta[top_count : 2 * top_count] + meta[2 * top_count : 3 * top_count]
        ) + meta[3 * top_count : 4 * top_count]
        places, hits, scales = [], [], []
        for (step, blocks), out_ref in zip(MESSAGES, out_refs, strict=True):
            if block not in blocks:
                continue
            places.append((out_ref, blocks.index(block) * GROUP))
            goal = lax.rem(plane + sign * step + PLANES, PLANES)
            expert = goal * (GROUP // 2) + row // 2
            hit = jnp.zeros((GROUP, tokens), F32)
            scale = jnp.zeros((GROUP, tokens), F32)
            for k in range(top_count):
                found = ids[k : k + 1, :] == expert
                hit = jnp.where(found, 1.0, hit)
                scale = jnp.where(found, weights[k : k + 1, :], scale)
            hits.append(hit)
            scales.append(scale)
        hit, scale = jnp.concatenate(hits, axis=0), jnp.concatenate(scales, axis=0)
        rank = jnp.dot(hit.astype(BF16), before, preferred_element_type=F32)
        wanted = (lax.broadcasted_iota(jnp.int32, hit.shape, 0) % 2).astype(F32)
        chosen = jnp.where((hit > 0.5) & (jnp.abs(rank - wanted) < 0.5), 1.0, 0.0)
        weight = jnp.sum(chosen * scale, axis=1, keepdims=True)
        chosen = chosen.astype(BF16)
        chunk = 1024
        for start in range(0, width, chunk):
            rows = jnp.dot(chosen, ref[:, start : start + chunk], preferred_element_type=F32)
            rows = (weight * rows).astype(BF16)
            for i, (out_ref, at) in enumerate(places):
                out_ref[at : at + GROUP, start : start + chunk] = rows[i * GROUP : (i + 1) * GROUP]


def join_kernel(spans, *refs):
    *in_refs, out_ref = refs
    parts, count, width = out_ref.shape
    blocks = count // GROUP
    shape = (count, count)
    to = lax.broadcasted_iota(jnp.int32, shape, 0)
    at = lax.broadcasted_iota(jnp.int32, shape, 1)
    device, rest = to // (2 * blocks), to % (2 * blocks)
    move = (at == (rest // 2) * GROUP + device * 2 + rest % 2).astype(F32).astype(BF16)
    for part in range(parts):
        cut = pl.ds(part * width, width)
        rows = jnp.concatenate(
            [ref[low:high, cut] for ref, (low, high) in zip(in_refs, spans, strict=True)], axis=0
        )
        out_ref[part] = jnp.dot(move, rows, preferred_element_type=F32).astype(BF16)


def join(pieces, parts):
    spans = tuple((low, high) for _, low, high in pieces)
    rows = sum(high - low for low, high in spans)
    width = pieces[0][0].shape[1] // parts

    def kernel(*refs):
        join_kernel(spans, *refs)

    return pl.pallas_call(
        kernel,
        out_shape=jax.ShapeDtypeStruct((parts, rows, width), BF16),
        compiler_params=SMALL,
    )(*[array for array, _, _ in pieces])


def shift(array, step):
    pairs = []
    for z in range(PLANES):
        for core in range(2):
            goal = (z + (step if core == 0 else -step)) % PLANES
            pairs.append((z * 2 + core, goal * 2 + core))
    return lax.ppermute(array, ("z", "core"), pairs)


def gathered(array, axis):
    count = lax.axis_size(axis)
    copies = jnp.broadcast_to(array[None], (count, *array.shape))
    return lax.all_to_all(copies, axis, split_axis=0, concat_axis=0, tiled=True)


def picked(plane, sign, own, behind, ahead):
    width = own.shape[1] - META
    return pl.pallas_call(
        pick_kernel,
        in_specs=[pl.BlockSpec(memory_space=pltpu.SMEM)] + [pl.BlockSpec(memory_space=pltpu.VMEM)] * 3,
        out_shape=[
            jax.ShapeDtypeStruct((len(blocks) * GROUP, width), BF16) for _, blocks in MESSAGES
        ],
        compiler_params=SMALL,
    )(jnp.stack([plane, sign]).astype(jnp.int32), own, behind, ahead)


def layer(grad_out, expert_ids, route_weights, hidden_act, projection):
    parts = lax.axis_size("dp")
    tokens, width = grad_out.shape
    plane, core = lax.axis_index("z"), lax.axis_index("core")
    sign = 1 - 2 * core
    own = pl.pallas_call(
        pack_kernel,
        out_shape=jax.ShapeDtypeStruct((tokens, width + META), BF16),
        compiler_params=SMALL,
    )(grad_out, expert_ids.T, route_weights.T)
    behind, ahead = shift(own, LEAP), shift(own, -LEAP)

    basis = gathered(projection[0], "dp").reshape(-1, projection.shape[2])
    reduced = jnp.dot(hidden_act[0, 0], basis, preferred_element_type=F32).astype(BF16)
    slots = reduced.shape[0]
    to = jnp.arange(slots, dtype=jnp.int32)
    batch, seat, block, copy = to // 128, (to // 16) % 8, (to // 2) % 8, to % 2
    offset = jnp.asarray(np.array(ORDER, np.int32))
    offset = jnp.sum(
        jnp.where((batch * 8 + block)[:, None] == jnp.arange(PLANES)[None, :], offset[None, :], 0),
        axis=1,
    )
    source = (plane + (1 - 2 * (seat % 2)) * offset) % PLANES
    slot = source * 16 + seat * 2 + copy
    move = (slot[:, None] == jnp.arange(slots, dtype=jnp.int32)[None, :]).astype(BF16)
    reduced = jnp.dot(move, reduced, preferred_element_type=F32).astype(BF16)
    reduced = gathered(reduced, "dp")

    sent = picked(plane, sign, own, behind, ahead)
    came = [
        array if step == 0 else shift(array, step)
        for array, (step, _) in zip(sent, MESSAGES, strict=True)
    ]
    stay, up1, down1, up2, down2, up3, down3, up4 = came
    two = 2 * GROUP
    first = join([(stay, 0, 3 * GROUP), (up1, 0, 3 * GROUP), (down1, 0, two)], parts)
    first, up2 = lax.optimization_barrier((first, up2))
    second = join(
        [
            (down1, two, 3 * GROUP),
            (up2, 0, two),
            (down2, 0, two),
            (up3, 0, GROUP),
            (down3, 0, GROUP),
            (up4, 0, GROUP),
        ],
        parts,
    )
    total = None
    for i, batch in enumerate((first, second)):
        arrived = lax.all_to_all(
            batch.reshape(-1, GROUP, batch.shape[2]),
            ("dp", "x", "core"),
            split_axis=0,
            concat_axis=0,
            tiled=True,
        ).reshape(-1, batch.shape[2])
        half = slots // 2
        factor = reduced[:, i * half : (i + 1) * half].reshape(-1, reduced.shape[2])
        share = lax.dot_general(
            arrived, factor, (((0,), (0,)), ((), ())), preferred_element_type=F32
        )
        total = share if total is None else total + share
    return total.astype(BF16)[None]


def solution(mesh):
    names = ("dp", "z", "x", "core")
    fine = Mesh(mesh.devices.reshape(mesh.shape["dp"], PLANES, -1, 2), names)
    devices = ("z", "x", "core")
    in_specs = (
        P(names, None),
        P(names, None),
        P(names, None),
        P("dp", devices, None, None),
        P(devices, "dp", None),
    )
    out_specs = P(devices, "dp", None)
    return jax.shard_map(layer, mesh=fine, in_specs=in_specs, out_specs=out_specs, check_vma=False)
```

time: 209 us -> 137 us (0.66)
  waiting for transfers between devices: 133 us -> 43.9 us
  starting transfers between devices: 20.6 us -> 75.5 us
  between operations: 13.5 us -> 0.22 us
  blocking collectives: 13.2 us -> 0 us
  other arithmetic: 10.2 us -> 0.19 us
  local copies, waits for them, and re-layouts: 13.2 us -> 6.46 us
  Pallas kernels: 0 us -> 4.9 us
    all_to_all x1 -> x4, waiting for transfers between devices: 82.7 us -> 14.6 us  [the longest x2 14.3 us: layer(): lax.all_to_all(batch.reshape(-1, GROUP, batch.shape[2]), ('dp', 'x', 'cor...]
    reduce_scatter x1 -> x0, waiting for transfers between devices: 50.6 us -> none  [shards(): lax.psum_scatter(lax.dot_general(arrived, reduced, (((0,), (0,)), ((), ()...]
    ppermute x0 -> x9, starting transfers between devices: none -> 48.5 us  [shift(): return lax.ppermute(array, ('z', 'core'), pairs)]
    ppermute x0 -> x9, waiting for transfers between devices: none -> 29.3 us  [shift(): return lax.ppermute(array, ('z', 'core'), pairs)]
    all_gather x1 -> x0, blocking collectives: 13.2 us -> none  [shards(): lax.all_gather(projection[0], 'dp', axis=0, tiled=True)]
    convert_element_type x1 -> x0, other arithmetic: 6.93 us -> none  [shards(): jnp.where(valid[:, None], weight[:, None] * rows, 0.0).astype(jnp.bfloat16)]
    all_to_all x1 -> x4, starting transfers between devices: 20.5 us -> 27 us  [the longest x2 17.3 us: layer(): lax.all_to_all(batch.reshape(-1, GROUP, batch.shape[2]), ('dp', 'x', 'cor...]
    pallas_call x0 -> x4, Pallas kernels: none -> 4.9 us  [the longest x2 2.79 us: join(): pl.pallas_call(kernel, out_shape=jax.ShapeDtypeStruct((parts, rows, width...]
  transfers between devices with their start and end apart: 2 -> 13, of which waited for: 2 -> 6; matrix products, arithmetic and copies ran while one was open for 0% -> 4% of each run, Pallas kernels for 0% -> 4%
where the time goes in v2:
time: 137 us; the launch traced here: 136 us
  starting transfers between devices  75.5 us (55%)
  waiting for transfers between devices  43.9 us (32%)
  local copies, waits for them, and re-layouts  6.46 us (5%)
  Pallas kernels  4.9 us (4%)
  matrix products  4.72 us (3%)
    ppermute x9, starting transfers between devices, shift(): return lax.ppermute(array, ('z', 'core'), pairs)  48.5 us
    ppermute x9, waiting for transfers between devices, shift(): return lax.ppermute(array, ('z', 'core'), pairs)  29.3 us
    all_to_all x2, starting transfers between devices, layer(): lax.all_to_all(batch.reshape(-1, GROUP, batch.shape[2]), ('dp', 'x', 'cor...  17.3 us
    all_to_all x2, waiting for transfers between devices, layer(): lax.all_to_all(batch.reshape(-1, GROUP, batch.shape[2]), ('dp', 'x', 'cor...  14.3 us
    all_to_all x2, starting transfers between devices, gathered(): return lax.all_to_all(copies, axis, split_axis=0, concat_axis=0, tiled=True)  9.67 us
    dot_general x2, matrix products, layer(): lax.dot_general(arrived, factor, (((0,), (0,)), ((), ())), preferred_elem...  3 us
    broadcast_in_dim x2, local copies, waits for them, and re-layouts, gathered(): copies = jnp.broadcast_to(array[None], (count, *array.shape))  2.81 us
    pallas_call x2, Pallas kernels, join(): pl.pallas_call(kernel, out_shape=jax.ShapeDtypeStruct((parts, rows, width...  2.79 us
  transfers between devices with their start and end apart: 13, of which 6 were waited for; matrix products, arithmetic and copies ran while one was open for 4% of the time, Pallas kernels for 4%

profile of v2, /device:TPU:1, one launch (start us, length us, event | category | flops | bytes accessed | tf_op | source)
XLA Modules:
  0.0 135.9 jit_solution(10031910856498444519)
XLA Ops:
  0.0 0.0 copy-start
  0.0 2.0 %broadcast_in_dim.36 = bf16[4,384,256]{2,1,0:T(8,128)(2,1)} broadcast(bf16[384,256]{1,0:T(8,128)(2,1)} %bitcast.28), dimensions={1,2} | broadcast | bytes 983040 | tf_op jit(solution)/shard_map/broadcast_in_dim | solution.py:149
  2.0 5.1 %all-to-all-start.1 = ((bf16[4,384,256]{2,1,0:T(8,128)(2,1)}), bf16[4,384,256]{2,1,0:T(8,128)(2,1)}, u32[]{:S(2)}, u32[]{:S(2)}) async-start(bf16[4,384,256]{2,1,0:T(8,128)(2,1)} %broadcast_in_dim.36), calls=%async_computation.1 | async-start | bytes 1572864 | tf_op jit(solution)/shard_map/all_to_all | solution.py:150
  7.1 0.0 copy-done.1
  7.1 0.1 shard_map.64.own_ref
  7.3 12.5 %collective-permute-start = (bf16[32,4224]{1,0:T(8,128)(2,1)S(1)}, bf16[32,4224]{1,0:T(8,128)(2,1)S(1)}, u32[]{:S(2)}, u32[]{:S(2)}) collective-permute-start(bf16[32,4224]{1,0:T(8,128)(2,1)S(1)} %shard_map.64.own_ref), channel_id=1, source_target_pairs={{0,32},{1,97},{8,40},{9,105},{16,48},{17,113},{24,56},{25,121},{32... | collective-permute-start | bytes 811016 | tf_op jit(solution)/shard_map/ppermute | solution.py:144
  19.7 1.9 %collective-permute-start.1 = (bf16[32,4224]{1,0:T(8,128)(2,1)S(1)}, bf16[32,4224]{1,0:T(8,128)(2,1)S(1)}, u32[]{:S(2)}, u32[]{:S(2)}) collective-permute-start(bf16[32,4224]{1,0:T(8,128)(2,1)S(1)} %shard_map.64.own_ref), channel_id=1, source_target_pairs={{0,96},{1,33},{8,104},{9,41},{16,112},{17,49},{24,120},{25,57},{32... | collective-permute-start | bytes 811016 | tf_op jit(solution)/shard_map/ppermute | solution.py:144
  21.7 0.0 copy-start.10
  21.7 0.6 copy-done.10
  22.3 0.1 select_reduce_fusion
  22.4 0.1 pad_add_fusion.place_ref
  22.5 14.9 %collective-permute-done.behind_ref = bf16[32,4224]{1,0:T(8,128)(2,1)S(1)} collective-permute-done((bf16[32,4224]{1,0:T(8,128)(2,1)S(1)}, bf16[32,4224]{1,0:T(8,128)(2,1)S(1)}, u32[]{:S(2)}, u32[]{:S(2)}) %collective-permute-start) | collective-permute-done | bytes 270368 | tf_op jit(solution)/shard_map/ppermute | solution.py:144
  37.4 0.0 collective-permute-done.1.ahead_ref
  37.4 2.0 %shard_map.65 = (bf16[48,4096]{1,0:T(8,128)(2,1)S(1)}, bf16[48,4096]{1,0:T(8,128)(2,1)S(1)}, bf16[48,4096]{1,0:T(8,128)(2,1)S(1)}, bf16[32,4096]{1,0:T(8,128)(2,...) custom-call(s32[2]{0:T(128)S(1)} %pad_add_fusion.place_ref, ...), custom_call_target="tpu_custom_call" | custom-call | tf_op jit(solution)/shard_map/pallas_call | solution.py:155
  39.4 0.0 copy-start.4
  39.4 0.6 copy-done.4
  40.0 0.6 copy-done.6
  40.7 0.7 copy-done.8
  41.3 1.9 %collective-permute-start.3 = (bf16[48,4096]{1,0:T(8,128)(2,1)S(1)}, bf16[48,4096]{1,0:T(8,128)(2,1)S(1)}, u32[]{:S(2)}, u32[]{:S(2)}) collective-permute-start(bf16[48,4096]{1,0:T(8,128)(2,1)S(1)} %get-tuple-element.17), channel_id=1, source_target_pairs={{0,120},{1,9},{8,0},{9,17},{16,8},{17,25},{24,16},{25,33},{32,24},... | collective-permute-start | bytes 1179656 | tf_op jit(solution)/shard_map/ppermute | solution.py:144
  43.2 13.8 %collective-permute-start.2 = (bf16[48,4096]{1,0:T(8,128)(2,1)S(1)}, bf16[48,4096]{1,0:T(8,128)(2,1)S(1)}, u32[]{:S(2)}, u32[]{:S(2)}) collective-permute-start(bf16[48,4096]{1,0:T(8,128)(2,1)S(1)} %get-tuple-element.16), channel_id=1, source_target_pairs={{0,8},{1,121},{8,16},{9,1},{16,24},{17,9},{24,32},{25,17},{32,40},... | collective-permute-start | bytes 1179656 | tf_op jit(solution)/shard_map/ppermute | solution.py:144
  57.0 0.0 all-to-all-done.1
  57.0 1.7 %convolution_convert_fusion = bf16[256,256]{1,0:T(8,128)(2,1)S(1)} fusion(bf16[1536,256]{1,0:T(8,128)(2,1)} %bitcast.8, bf16[1,1,256,1536]{3,2,1,0:T(8,128)(2,1)S(1)} %copy-done, s32[256]{0:T(256)S(1)} %fusion.7), kind=kOutput, calls=%fused_computation.3 | convolution fusion | flops 235077632 | bytes 1704960 | tf_op jit(solution)/shard_map/dot_general | solution.py:190
  58.7 0.8 broadcast_in_dim.37
  59.6 4.5 %all-to-all-start.2 = ((bf16[4,256,256]{2,1,0:T(8,128)(2,1)}), bf16[4,256,256]{2,1,0:T(8,128)(2,1)}, u32[]{:S(2)}, u32[]{:S(2)}) async-start(bf16[4,256,256]{2,1,0:T(8,128)(2,1)} %broadcast_in_dim.37), calls=%async_computation.2 | async-start | bytes 1048576 | tf_op jit(solution)/shard_map/all_to_all | solution.py:150
  64.1 3.1 %collective-permute-start.4 = (bf16[32,4096]{1,0:T(8,128)(2,1)S(1)}, bf16[32,4096]{1,0:T(8,128)(2,1)S(1)}, u32[]{:S(2)}, u32[]{:S(2)}) collective-permute-start(bf16[32,4096]{1,0:T(8,128)(2,1)S(1)} %get-tuple-element.18), channel_id=1, source_target_pairs={{0,16},{1,113},{8,24},{9,121},{16,32},{17,1},{24,40},{25,9},{32,48... | collective-permute-start | bytes 786440 | tf_op jit(solution)/shard_map/ppermute | solution.py:144
  67.2 0.0 collective-permute-done.3.refs_2_.refs_0_
  67.2 0.0 collective-permute-done.2.refs_1_
  67.2 1.4 %shard_map.66 = bf16[4,128,1024]{2,1,0:T(8,128)(2,1)} custom-call(bf16[48,4096]{1,0:T(8,128)(2,1)S(1)} %get-tuple-element.15.refs_0_, bf16[48,4096]{1,0:T(8,128)(2,1)S(1)} %collective-permute-done.2.refs_1_, bf16[48,4096]{1,0:T(8,128)(2,1)S(1)} %collective-permute-done.3.refs_2_.refs_0_), custom_call_target="tpu_custom_call" | custom-call | tf_op jit(solution)/shard_map/pallas_call | solution.py:131
  68.6 4.3 %collective-permute-done.4.refs_1_ = bf16[32,4096]{1,0:T(8,128)(2,1)S(1)} collective-permute-done((bf16[32,4096]{1,0:T(8,128)(2,1)S(1)}, bf16[32,4096]{1,0:T(8,128)(2,1)S(1)}, u32[]{:S(2)}, u32[]{:S(2)}) %collective-permute-start.4) | collective-permute-done | bytes 262176 | tf_op jit(solution)/shard_map/ppermute | solution.py:144
  72.9 0.4 all-to-all-done.2
  73.3 10.1 %all-to-all-start = ((bf16[32,16,1024]{2,1,0:T(8,128)(2,1)}), bf16[32,16,1024]{2,1,0:T(8,128)(2,1)}, u32[]{:S(2)}, u32[]{:S(2)}) async-start(bf16[32,16,1024]{2,1,0:T(8,128)(2,1)} %bitcast.4), calls=%async_computation | async-start | bytes 2097152 | tf_op jit(solution)/shard_map/all_to_all | solution.py:215
  83.4 1.9 %collective-permute-start.5 = (bf16[32,4096]{1,0:T(8,128)(2,1)S(1)}, bf16[32,4096]{1,0:T(8,128)(2,1)S(1)}, u32[]{:S(2)}, u32[]{:S(2)}) collective-permute-start(bf16[32,4096]{1,0:T(8,128)(2,1)S(1)} %get-tuple-element.21), channel_id=1, source_target_pairs={{0,112},{1,17},{8,120},{9,25},{16,0},{17,33},{24,8},{25,41},{32,16... | collective-permute-start | bytes 786440 | tf_op jit(solution)/shard_map/ppermute | solution.py:144
  85.3 0.0 copy-done.9
  85.3 6.6 %collective-permute-start.6 = (bf16[16,4096]{1,0:T(8,128)(2,1)S(1)}, bf16[16,4096]{1,0:T(8,128)(2,1)S(1)}, u32[]{:S(2)}, u32[]{:S(2)}) collective-permute-start(bf16[16,4096]{1,0:T(8,128)(2,1)S(1)} %copy-done.9), channel_id=1, source_target_pairs={{0,24},{1,105},{8,32},{9,113},{16,40},{17,121},{24,48},{25,1},{32,... | collective-permute-start | bytes 393224 | tf_op jit(solution)/shard_map/ppermute | solution.py:144
  91.9 1.9 %collective-permute-start.7 = (bf16[16,4096]{1,0:T(8,128)(2,1)S(1)}, bf16[16,4096]{1,0:T(8,128)(2,1)S(1)}, u32[]{:S(2)}, u32[]{:S(2)}) collective-permute-start(bf16[16,4096]{1,0:T(8,128)(2,1)S(1)} %copy-done.7), channel_id=1, source_target_pairs={{0,104},{1,25},{8,112},{9,33},{16,120},{17,41},{24,0},{25,49},{32,... | collective-permute-start | bytes 393224 | tf_op jit(solution)/shard_map/ppermute | solution.py:144
  93.9 0.0 copy-done.5
  93.9 4.9 %collective-permute-start.8 = (bf16[16,4096]{1,0:T(8,128)(2,1)S(1)}, bf16[16,4096]{1,0:T(8,128)(2,1)S(1)}, u32[]{:S(2)}, u32[]{:S(2)}) collective-permute-start(bf16[16,4096]{1,0:T(8,128)(2,1)S(1)} %copy-done.5), channel_id=1, source_target_pairs={{0,32},{1,97},{8,40},{9,105},{16,48},{17,113},{24,56},{25,121},{32... | collective-permute-start | bytes 393224 | tf_op jit(solution)/shard_map/ppermute | solution.py:144
  98.8 0.0 collective-permute-done.6.refs_3_
  98.8 3.3 %collective-permute-done.7.refs_4_ = bf16[16,4096]{1,0:T(8,128)(2,1)S(1)} collective-permute-done((bf16[16,4096]{1,0:T(8,128)(2,1)S(1)}, bf16[16,4096]{1,0:T(8,128)(2,1)S(1)}, u32[]{:S(2)}, u32[]{:S(2)}) %collective-permute-start.7) | collective-permute-done | bytes 131104 | tf_op jit(solution)/shard_map/ppermute | solution.py:144
  102.1 6.7 %collective-permute-done.8.refs_5_ = bf16[16,4096]{1,0:T(8,128)(2,1)S(1)} collective-permute-done((bf16[16,4096]{1,0:T(8,128)(2,1)S(1)}, bf16[16,4096]{1,0:T(8,128)(2,1)S(1)}, u32[]{:S(2)}, u32[]{:S(2)}) %collective-permute-start.8) | collective-permute-done | bytes 131104 | tf_op jit(solution)/shard_map/ppermute | solution.py:144
  108.9 0.0 collective-permute-done.5.refs_2_
  108.9 1.4 %shard_map.67 = bf16[4,128,1024]{2,1,0:T(8,128)(2,1)} custom-call(bf16[48,4096]{1,0:T(8,128)(2,1)S(1)} %collective-permute-done.3.refs_2_.refs_0_, bf16[32,4096]{1,0:T(8,128)(2,1)S(1)} %collective-permute-done.4.refs_1_, bf16[32,4096]{1,0:T(8,128)(2,1)S(1)} %collective-permute-done.5.refs_2_, bf16[16,4096]{1,0:T(8,128)(2,1)S(1)} %collective-permute-done.6.refs_3_, ...), custom_call_target="tpu_custom_call" | custom-call | tf_op jit(solution)/shard_map/pallas_call | solution.py:131
  110.3 0.0 all-to-all-done
  110.3 7.2 %all-to-all-start.3 = ((bf16[32,16,1024]{2,1,0:T(8,128)(2,1)}), bf16[32,16,1024]{2,1,0:T(8,128)(2,1)S(1)}, u32[]{:S(2)}, u32[]{:S(2)}) async-start(bf16[32,16,1024]{2,1,0:T(8,128)(2,1)} %bitcast.10), calls=%async_computation.3 | async-start | bytes 2097152 | tf_op jit(solution)/shard_map/all_to_all | solution.py:215
  117.5 1.1 fusion.20
  118.6 1.7 %fusion.21 = f32[1024,256]{1,0:T(8,128)S(1)} fusion(bf16[512,1024]{1,0:T(8,128)(2,1)} %bitcast.5, bf16[512,256]{1,0:T(8,128)(2,1)S(1)} %bitcast.26), kind=kOutput, calls=%fused_computation.50 | convolution fusion | flops 268435456 | bytes 2359296 | tf_op jit(solution)/shard_map/dot_general | solution.py:224
  120.3 14.3 %all-to-all-done.3 = bf16[32,16,1024]{2,1,0:T(8,128)(2,1)S(1)} async-done(((bf16[32,16,1024]{2,1,0:T(8,128)(2,1)}), bf16[32,16,1024]{2,1,0:T(8,128)(2,1)S(1)}, u32[]{:S(2)}, u32[]{:S(2)}) %all-to-all-start.3) | async-done | bytes 1048608 | tf_op jit(solution)/shard_map/all_to_all | solution.py:215
  134.6 1.3 fusion.1
  (14 shorter events, 0.0 us)
Async XLA Ops:
  0.0 57.0 %copy-start = (bf16[1,1,256,1536]{3,2,1,0:T(8,128)(2,1)S(1)}, bf16[1,1,256,1536]{3,2,1,0:T(8,128)(2,1)}, u32[]{:S(2)}) copy-start(bf16[1,1,256,1536]{3,2,1,0:T(8,128)(2,1)} %param.9) | copy-start | bytes 2359300
  2.0 5.1 %copy-start.1 = (bf16[32,4096]{1,0:T(8,128)(2,1)S(1)}, bf16[32,4096]{1,0:T(8,128)(2,1)}, u32[]{:S(2)}) copy-start(bf16[32,4096]{1,0:T(8,128)(2,1)} %grad_ref.1) | copy-start | bytes 786436
  2.0 5.1 %copy-start.2 = (s32[32,8]{0,1:T(8,128)S(1)}, s32[32,8]{0,1:T(8,128)}, u32[]{:S(2)}) copy-start(s32[32,8]{0,1:T(8,128)} %param.7) | copy-start | bytes 3076
  2.0 5.1 %copy-start.3 = (f32[32,8]{0,1:T(8,128)S(1)}, f32[32,8]{0,1:T(8,128)}, u32[]{:S(2)}) copy-start(f32[32,8]{0,1:T(8,128)} %param.8) | copy-start | bytes 3076
  2.0 55.0 %all-to-all-start.1 = ((bf16[4,384,256]{2,1,0:T(8,128)(2,1)}), bf16[4,384,256]{2,1,0:T(8,128)(2,1)}, u32[]{:S(2)}, u32[]{:S(2)}) async-start(bf16[4,384,256]{2,1,0:T(8,128)(2,1)} %broadcast_in_dim.36), calls=%async_computation.1 | async-start | bytes 1572864 | tf_op jit(solution)/shard_map/all_to_all | solution.py:150
  7.3 30.1 %collective-permute-start = (bf16[32,4224]{1,0:T(8,128)(2,1)S(1)}, bf16[32,4224]{1,0:T(8,128)(2,1)S(1)}, u32[]{:S(2)}, u32[]{:S(2)}) collective-permute-start(bf16[32,4224]{1,0:T(8,128)(2,1)S(1)} %shard_map.64.own_ref), channel_id=1, source_target_pairs={{0,32},{1,97},{8,40},{9,105},{16,48},{17,113},{24,56},{25,121},{32... | collective-permute-start | bytes 811016 | tf_op jit(solution)/shard_map/ppermute | solution.py:144
  19.7 17.7 %collective-permute-start.1 = (bf16[32,4224]{1,0:T(8,128)(2,1)S(1)}, bf16[32,4224]{1,0:T(8,128)(2,1)S(1)}, u32[]{:S(2)}, u32[]{:S(2)}) collective-permute-start(bf16[32,4224]{1,0:T(8,128)(2,1)S(1)} %shard_map.64.own_ref), channel_id=1, source_target_pairs={{0,96},{1,33},{8,104},{9,41},{16,112},{17,49},{24,120},{25,57},{32... | collective-permute-start | bytes 811016 | tf_op jit(solution)/shard_map/ppermute | solution.py:144
  21.7 0.7 copy-start.10
  39.4 0.6 copy-start.4
  40.0 0.6 copy-start.6
  40.7 0.7 copy-start.8
  41.3 25.9 %collective-permute-start.3 = (bf16[48,4096]{1,0:T(8,128)(2,1)S(1)}, bf16[48,4096]{1,0:T(8,128)(2,1)S(1)}, u32[]{:S(2)}, u32[]{:S(2)}) collective-permute-start(bf16[48,4096]{1,0:T(8,128)(2,1)S(1)} %get-tuple-element.17), channel_id=1, source_target_pairs={{0,120},{1,9},{8,0},{9,17},{16,8},{17,25},{24,16},{25,33},{32,24},... | collective-permute-start | bytes 1179656 | tf_op jit(solution)/shard_map/ppermute | solution.py:144
  43.2 24.0 %collective-permute-start.2 = (bf16[48,4096]{1,0:T(8,128)(2,1)S(1)}, bf16[48,4096]{1,0:T(8,128)(2,1)S(1)}, u32[]{:S(2)}, u32[]{:S(2)}) collective-permute-start(bf16[48,4096]{1,0:T(8,128)(2,1)S(1)} %get-tuple-element.16), channel_id=1, source_target_pairs={{0,8},{1,121},{8,16},{9,1},{16,24},{17,9},{24,32},{25,17},{32,40},... | collective-permute-start | bytes 1179656 | tf_op jit(solution)/shard_map/ppermute | solution.py:144
  59.6 13.7 %all-to-all-start.2 = ((bf16[4,256,256]{2,1,0:T(8,128)(2,1)}), bf16[4,256,256]{2,1,0:T(8,128)(2,1)}, u32[]{:S(2)}, u32[]{:S(2)}) async-start(bf16[4,256,256]{2,1,0:T(8,128)(2,1)} %broadcast_in_dim.37), calls=%async_computation.2 | async-start | bytes 1048576 | tf_op jit(solution)/shard_map/all_to_all | solution.py:150
  64.1 8.8 %collective-permute-start.4 = (bf16[32,4096]{1,0:T(8,128)(2,1)S(1)}, bf16[32,4096]{1,0:T(8,128)(2,1)S(1)}, u32[]{:S(2)}, u32[]{:S(2)}) collective-permute-start(bf16[32,4096]{1,0:T(8,128)(2,1)S(1)} %get-tuple-element.18), channel_id=1, source_target_pairs={{0,16},{1,113},{8,24},{9,121},{16,32},{17,1},{24,40},{25,9},{32,48... | collective-permute-start | bytes 786440 | tf_op jit(solution)/shard_map/ppermute | solution.py:144
  73.3 12.0 %copy-start.9 = (bf16[16,4096]{1,0:T(8,128)(2,1)S(1)}, bf16[16,4096]{1,0:T(8,128)(2,1)}, u32[]{:S(2)}) copy-start(bf16[16,4096]{1,0:T(8,128)(2,1)} %copy-done.8) | copy-start | bytes 393220
  73.3 18.6 %copy-start.7 = (bf16[16,4096]{1,0:T(8,128)(2,1)S(1)}, bf16[16,4096]{1,0:T(8,128)(2,1)}, u32[]{:S(2)}) copy-start(bf16[16,4096]{1,0:T(8,128)(2,1)} %copy-done.6) | copy-start | bytes 393220
  73.3 20.6 %copy-start.5 = (bf16[16,4096]{1,0:T(8,128)(2,1)S(1)}, bf16[16,4096]{1,0:T(8,128)(2,1)}, u32[]{:S(2)}) copy-start(bf16[16,4096]{1,0:T(8,128)(2,1)} %copy-done.4) | copy-start | bytes 393220
  73.3 37.0 %all-to-all-start = ((bf16[32,16,1024]{2,1,0:T(8,128)(2,1)}), bf16[32,16,1024]{2,1,0:T(8,128)(2,1)}, u32[]{:S(2)}, u32[]{:S(2)}) async-start(bf16[32,16,1024]{2,1,0:T(8,128)(2,1)} %bitcast.4), calls=%async_computation | async-start | bytes 2097152 | tf_op jit(solution)/shard_map/all_to_all | solution.py:215
  83.4 25.5 %collective-permute-start.5 = (bf16[32,4096]{1,0:T(8,128)(2,1)S(1)}, bf16[32,4096]{1,0:T(8,128)(2,1)S(1)}, u32[]{:S(2)}, u32[]{:S(2)}) collective-permute-start(bf16[32,4096]{1,0:T(8,128)(2,1)S(1)} %get-tuple-element.21), channel_id=1, source_target_pairs={{0,112},{1,17},{8,120},{9,25},{16,0},{17,33},{24,8},{25,41},{32,16... | collective-permute-start | bytes 786440 | tf_op jit(solution)/shard_map/ppermute | solution.py:144
  85.3 13.5 %collective-permute-start.6 = (bf16[16,4096]{1,0:T(8,128)(2,1)S(1)}, bf16[16,4096]{1,0:T(8,128)(2,1)S(1)}, u32[]{:S(2)}, u32[]{:S(2)}) collective-permute-start(bf16[16,4096]{1,0:T(8,128)(2,1)S(1)} %copy-done.9), channel_id=1, source_target_pairs={{0,24},{1,105},{8,32},{9,113},{16,40},{17,121},{24,48},{25,1},{32,... | collective-permute-start | bytes 393224 | tf_op jit(solution)/shard_map/ppermute | solution.py:144
  91.9 10.2 %collective-permute-start.7 = (bf16[16,4096]{1,0:T(8,128)(2,1)S(1)}, bf16[16,4096]{1,0:T(8,128)(2,1)S(1)}, u32[]{:S(2)}, u32[]{:S(2)}) collective-permute-start(bf16[16,4096]{1,0:T(8,128)(2,1)S(1)} %copy-done.7), channel_id=1, source_target_pairs={{0,104},{1,25},{8,112},{9,33},{16,120},{17,41},{24,0},{25,49},{32,... | collective-permute-start | bytes 393224 | tf_op jit(solution)/shard_map/ppermute | solution.py:144
  93.9 15.0 %collective-permute-start.8 = (bf16[16,4096]{1,0:T(8,128)(2,1)S(1)}, bf16[16,4096]{1,0:T(8,128)(2,1)S(1)}, u32[]{:S(2)}, u32[]{:S(2)}) collective-permute-start(bf16[16,4096]{1,0:T(8,128)(2,1)S(1)} %copy-done.5), channel_id=1, source_target_pairs={{0,32},{1,97},{8,40},{9,105},{16,48},{17,113},{24,56},{25,121},{32... | collective-permute-start | bytes 393224 | tf_op jit(solution)/shard_map/ppermute | solution.py:144
  110.3 24.3 %all-to-all-start.3 = ((bf16[32,16,1024]{2,1,0:T(8,128)(2,1)}), bf16[32,16,1024]{2,1,0:T(8,128)(2,1)S(1)}, u32[]{:S(2)}, u32[]{:S(2)}) async-start(bf16[32,16,1024]{2,1,0:T(8,128)(2,1)} %bitcast.10), calls=%async_computation.3 | async-start | bytes 2097152 | tf_op jit(solution)/shard_map/all_to_all | solution.py:215

commit v3 on v0

v3 whole, which is shorter than its diff:
```python
import numpy as np

import jax
import jax.numpy as jnp
from jax import lax
from jax.experimental import pallas as pl
from jax.experimental.pallas import tpu as pltpu
from jax.sharding import Mesh, PartitionSpec as P


PLANES = 16
SEATS = 8
LEAP = 5
META = 128
TOPK = 8
GROUP = 2 * SEATS
F32, BF16 = jnp.float32, jnp.bfloat16
SMALL = pltpu.CompilerParams(vmem_limit_bytes=12 * 1024 * 1024)

START = (0, -LEAP, LEAP)
NEAR = ((1, 0), (1, 1), (1, 2), (0, 0), (-1, 0), (-1, 1), (-1, 2), (0, 1))
FAR = ((0, 2), (2, 0), (2, 1), (2, 2), (-2, 0), (-2, 1), (-2, 2), (3, 1))
CUTS = (GROUP, 3 * GROUP, 3 * GROUP, GROUP)


def origins(table, moved):
    return [(START[block], step) if step == moved else None for step, block in table]


SLOTS = (
    origins(NEAR, 0)
    + origins(NEAR[:4], 1)
    + origins(NEAR[4:], -1)
    + [(START[block] - step, 0) for step, block in FAR]
)


def pack_kernel(grad_ref, ids_ref, weight_ref, out_ref):
    tokens, width = grad_ref.shape
    high = weight_ref[...].astype(BF16).astype(F32)
    rest = weight_ref[...] - high
    middle = rest.astype(BF16).astype(F32)
    low = rest - middle
    parts = [ids_ref[...].astype(F32), high, middle, low]
    used = sum(part.shape[0] for part in parts)
    meta = jnp.concatenate(parts + [jnp.zeros((META - used, tokens), F32)], axis=0)
    same = lax.broadcasted_iota(jnp.int32, (tokens, tokens), 0) == lax.broadcasted_iota(
        jnp.int32, (tokens, tokens), 1
    )
    turned = lax.dot_general(
        same.astype(F32).astype(BF16),
        meta.astype(BF16),
        (((1,), (1,)), ((), ())),
        preferred_element_type=F32,
    )
    out_ref[:, :width] = grad_ref[...]
    out_ref[:, width:] = turned.astype(BF16)


def pick_kernel(place_ref, own_ref, behind_ref, ahead_ref, near_ref, *far_refs):
    refs = (own_ref, behind_ref, ahead_ref)
    tokens = own_ref.shape[0]
    width = own_ref.shape[1] - META
    lanes = tokens * len(refs)
    parts, count, part_width = near_ref.shape
    plane, sign = place_ref[0], place_ref[1]

    same = lax.broadcasted_iota(jnp.int32, (META, META), 0) == lax.broadcasted_iota(
        jnp.int32, (META, META), 1
    )
    meta = lax.dot_general(
        same.astype(F32).astype(BF16),
        jnp.concatenate([ref[:, width:] for ref in refs], axis=0),
        (((1,), (1,)), ((), ())),
        preferred_element_type=F32,
    )
    ids = meta[:TOPK]
    weights = (meta[TOPK : 2 * TOPK] + meta[2 * TOPK : 3 * TOPK]) + meta[3 * TOPK : 4 * TOPK]
    early = lax.broadcasted_iota(jnp.int32, (lanes, lanes), 0)
    late = lax.broadcasted_iota(jnp.int32, (lanes, lanes), 1)
    before = ((early // tokens == late // tokens) & (early < late)).astype(F32).astype(BF16)

    row = lax.broadcasted_iota(jnp.int32, (count, lanes), 0)
    block = lax.broadcasted_iota(jnp.int32, (count, lanes), 1) // tokens
    copy = (row % 2).astype(F32)

    def choose(table, entry, seat, senses):
        base = jnp.zeros((count, lanes), jnp.int32)
        wanted = jnp.zeros((count, lanes), jnp.int32)
        for i, (step, source) in enumerate(table):
            goals = [lax.rem(plane + sense * step + PLANES, PLANES) * SEATS for sense in senses]
            goal = goals[0] if len(goals) == 1 else jnp.where(seat % 2 == 0, goals[0], goals[1])
            base = jnp.where(entry == i, goal, base)
            wanted = jnp.where(entry == i, source, wanted)
        expert = (base + seat).astype(F32)
        hit = jnp.zeros((count, lanes), F32)
        scale = jnp.zeros((count, lanes), F32)
        for k in range(TOPK):
            found = ids[k : k + 1, :] == expert
            hit = jnp.where(found, 1.0, hit)
            scale = jnp.where(found, weights[k : k + 1, :], scale)
        rank = jnp.dot(hit.astype(BF16), before, preferred_element_type=F32)
        chosen = (hit > 0.5) & (jnp.abs(rank - copy) < 0.5) & (block == wanted)
        chosen = jnp.where(chosen, 1.0, 0.0)
        return chosen.astype(BF16), jnp.sum(chosen * scale, axis=1, keepdims=True)

    near, near_weight = choose(NEAR, (row // 2) % 8, row // GROUP, (1, -1))
    far, far_weight = choose(FAR, row // GROUP, (row // 2) % SEATS, (sign,))
    for part in range(parts):
        cut = pl.ds(part * part_width, part_width)
        tile = jnp.concatenate([ref[:, cut] for ref in refs], axis=0)
        rows = jnp.dot(far, tile, preferred_element_type=F32)
        rows = (far_weight * rows).astype(BF16)
        at = 0
        for ref, size in zip(far_refs, CUTS, strict=True):
            ref[:, cut] = rows[at : at + size]
            at += size
        rows = jnp.dot(near, tile, preferred_element_type=F32)
        near_ref[part] = (near_weight * rows).astype(BF16)


def picked(plane, sign, own, behind, ahead, parts):
    width = own.shape[1] - META
    shapes = [(parts, SEATS * GROUP, width // parts)] + [(size, width) for size in CUTS]
    return pl.pallas_call(
        pick_kernel,
        in_specs=[pl.BlockSpec(memory_space=pltpu.SMEM)] + [pl.BlockSpec(memory_space=pltpu.VMEM)] * 3,
        out_shape=[jax.ShapeDtypeStruct(shape, BF16) for shape in shapes],
        compiler_params=SMALL,
    )(jnp.stack([plane, sign]).astype(jnp.int32), own, behind, ahead)


def join_kernel(*refs):
    *in_refs, out_ref = refs
    parts, count, width = out_ref.shape
    to = lax.broadcasted_iota(jnp.int32, (count, count), 0)
    at = lax.broadcasted_iota(jnp.int32, (count, count), 1)
    seat, entry, copy = to // GROUP, (to // 2) % 8, to % 2
    move = (at == entry * GROUP + seat * 2 + copy).astype(F32).astype(BF16)
    for part in range(parts):
        cut = pl.ds(part * width, width)
        rows = jnp.concatenate([ref[:, cut] for ref in in_refs], axis=0)
        out_ref[part] = jnp.dot(move, rows, preferred_element_type=F32).astype(BF16)


def join(pieces, parts):
    rows = sum(piece.shape[0] for piece in pieces)
    return pl.pallas_call(
        join_kernel,
        out_shape=jax.ShapeDtypeStruct((parts, rows, pieces[0].shape[1] // parts), BF16),
        compiler_params=SMALL,
    )(*pieces)


def shift(array, step):
    pairs = []
    for z in range(PLANES):
        for core in range(2):
            goal = (z + (step if core == 0 else -step)) % PLANES
            pairs.append((z * 2 + core, goal * 2 + core))
    return lax.ppermute(array, ("z", "core"), pairs)


def gathered(array, axis):
    count = lax.axis_size(axis)
    copies = jnp.broadcast_to(array[None], (count, *array.shape))
    return lax.all_to_all(copies, axis, split_axis=0, concat_axis=0, tiled=True)


def exchanged(array):
    array = array.reshape(-1, GROUP, array.shape[2])
    return lax.all_to_all(array, ("dp", "x", "core"), split_axis=0, concat_axis=0, tiled=True)


def factor_moves(plane, sign, slots):
    moves = []
    for low, high in ((0, 8), (8, 12), (12, 16), (16, 24)):
        span = SLOTS[low:high]
        size = len(span)
        to = np.arange(SEATS * size * 2)
        seat, entry, copy = to // (size * 2), (to // 2) % size, to % 2
        ahead = np.array([0 if s is None else s[0] for s in span])[entry] * (1 - 2 * (seat % 2))
        behind = np.array([0 if s is None else s[1] for s in span])[entry]
        real = np.array([s is not None for s in span])[entry]
        moves.append(np.stack([ahead, behind, seat * 2 + copy, real]))
    ahead, behind, within, real = np.concatenate(moves, axis=1).astype(np.int32)
    slot = (plane + ahead - sign * behind + 2 * PLANES) % PLANES * GROUP + within
    same = slot[:, None] == jnp.arange(slots, dtype=jnp.int32)[None, :]
    return (same & (real[:, None] > 0)).astype(BF16)


def layer(grad_out, expert_ids, route_weights, hidden_act, projection):
    parts = lax.axis_size("dp")
    tokens, width = grad_out.shape
    rank = projection.shape[2]
    plane, core = lax.axis_index("z"), lax.axis_index("core")
    sign = 1 - 2 * core
    own = pl.pallas_call(
        pack_kernel,
        out_shape=jax.ShapeDtypeStruct((tokens, width + META), BF16),
    )(grad_out, expert_ids.T, route_weights.T)
    behind, ahead = shift(own, LEAP), shift(own, -LEAP)

    basis = gathered(projection[0], "dp").reshape(-1, rank)
    reduced = jnp.dot(hidden_act[0, 0], basis, preferred_element_type=F32).astype(BF16)
    reduced = gathered(reduced, "dp")
    moves = factor_moves(plane, sign, reduced.shape[1])
    factor = jnp.einsum("as,rsk->rak", moves, reduced, preferred_element_type=F32).astype(BF16)

    near, stay, up2, down2, up3 = picked(plane, sign, own, behind, ahead, parts)
    up2, down2, up3 = shift(up2, 2), shift(down2, -2), shift(up3, 3)
    near = exchanged(near)
    far = join([stay, up2, down2, up3], parts)
    far = exchanged(far)
    up1 = shift(near[:, :8], 1)
    down1 = shift(near[:, 8:], -1)
    total = None
    at = 0
    for piece in (near, up1, down1, far):
        size = SEATS * piece.shape[1]
        share = lax.dot_general(
            piece.reshape(-1, piece.shape[2]),
            factor[:, at : at + size].reshape(-1, rank),
            (((0,), (0,)), ((), ())),
            preferred_element_type=F32,
        )
        total = share if total is None else total + share
        at += size
    return total.astype(BF16)[None]


def solution(mesh):
    names = ("dp", "z", "x", "core")
    fine = Mesh(mesh.devices.reshape(mesh.shape["dp"], PLANES, -1, 2), names)
    devices = ("z", "x", "core")
    in_specs = (
        P(names, None),
        P(names, None),
        P(names, None),
        P("dp", devices, None, None),
        P(devices, "dp", None),
    )
    out_specs = P(devices, "dp", None)
    return jax.shard_map(layer, mesh=fine, in_specs=in_specs, out_specs=out_specs, check_vma=False)
```

time: 209 us -> 143 us (0.68)
  waiting for transfers between devices: 133 us -> 50.7 us
  starting transfers between devices: 20.6 us -> 58.1 us
  between operations: 13.5 us -> 0.23 us
  other arithmetic: 10.2 us -> 0.09 us
  Pallas kernels: 0 us -> 5.77 us
  local copies, waits for them, and re-layouts: 13.2 us -> 7.74 us
    all_to_all x1 -> x3, waiting for transfers between devices: 82.7 us -> 5.99 us  [the longest x2 5.99 us: exchanged(): lax.all_to_all(array, ('dp', 'x', 'core'), split_axis=0, concat_axis=0, t...]
    reduce_scatter x1 -> x0, waiting for transfers between devices: 50.6 us -> none  [shards(): lax.psum_scatter(lax.dot_general(arrived, reduced, (((0,), (0,)), ((), ()...]
    ppermute x0 -> x7, waiting for transfers between devices: none -> 44.7 us  [shift(): return lax.ppermute(array, ('z', 'core'), pairs)]
    ppermute x0 -> x7, starting transfers between devices: none -> 39.7 us  [shift(): return lax.ppermute(array, ('z', 'core'), pairs)]
    all_gather x1 -> x0, blocking collectives: 13.2 us -> none  [shards(): lax.all_gather(projection[0], 'dp', axis=0, tiled=True)]
    all_to_all x0 -> x1, blocking collectives: none -> 13.1 us  [gathered(): return lax.all_to_all(copies, axis, split_axis=0, concat_axis=0, tiled=True)]
    convert_element_type x1 -> x0, other arithmetic: 6.93 us -> none  [shards(): jnp.where(valid[:, None], weight[:, None] * rows, 0.0).astype(jnp.bfloat16)]
    pallas_call x0 -> x3, Pallas kernels: none -> 5.77 us  [the longest x1 2.55 us: picked(): pl.pallas_call(pick_kernel, in_specs=[pl.BlockSpec(memory_space=pltpu.SME...]
  transfers between devices with their start and end apart: 2 -> 10, of which waited for: 2 -> 6; matrix products, arithmetic and copies ran while one was open for 0% -> 6% of each run, Pallas kernels for 0% -> 4%
where the time goes in v3:
time: 143 us
  starting transfers between devices  58.1 us (41%)
  waiting for transfers between devices  50.7 us (35%)
  blocking collectives  13.1 us (9%)
  local copies, waits for them, and re-layouts  7.74 us (5%)
  matrix products  6.79 us (5%)
  Pallas kernels  5.77 us (4%)
    ppermute x7, waiting for transfers between devices, shift(): return lax.ppermute(array, ('z', 'core'), pairs)  44.7 us
    ppermute x7, starting transfers between devices, shift(): return lax.ppermute(array, ('z', 'core'), pairs)  39.7 us
    all_to_all x2, starting transfers between devices, exchanged(): lax.all_to_all(array, ('dp', 'x', 'core'), split_axis=0, concat_axis=0, t...  14.9 us
    all_to_all x1, blocking collectives, gathered(): return lax.all_to_all(copies, axis, split_axis=0, concat_axis=0, tiled=True)  13.1 us
    all_to_all x2, waiting for transfers between devices, exchanged(): lax.all_to_all(array, ('dp', 'x', 'core'), split_axis=0, concat_axis=0, t...  5.99 us
    dot_general x4, matrix products, layer(): lax.dot_general(piece.reshape(-1, piece.shape[2]), factor[:, at:at + size...  5.79 us
    all_to_all x1, starting transfers between devices, gathered(): return lax.all_to_all(copies, axis, split_axis=0, concat_axis=0, tiled=True)  3.47 us
    slice x6, local copies, waits for them, and re-layouts, layer(): factor[:, at:at + size].reshape(-1, rank)  3.06 us
  transfers between devices with their start and end apart: 10, of which 6 were waited for; matrix products, arithmetic and copies ran while one was open for 6% of the time, Pallas kernels for 4%

profile of v3, /device:TPU:1, one launch (start us, length us, event | category | flops | bytes accessed | tf_op | source)
XLA Modules:
  0.0 142.6 jit_solution(15399885373768475271)
XLA Ops:
  0.0 0.0 copy-start
  0.0 1.1 broadcast_in_dim.9
  1.1 13.1 %all_to_all.20 = bf16[4,384,256]{2,1,0:T(8,128)(2,1)S(1)} all-to-all(bf16[4,384,256]{2,1,0:T(8,128)(2,1)S(1)} %broadcast_in_dim.9), channel_id=1, replica_groups=mesh['dp'=4,'z'=16,'x'=4,'core'=2] {'dp'}, dimensions={0} | all-to-all | bytes 1572864 | tf_op jit(solution)/shard_map/all_to_all | solution.py:167
  14.2 0.4 convolution_convert_fusion.1
  14.6 0.8 broadcast_in_dim.20
  15.5 3.5 %all-to-all-start.2 = ((bf16[4,256,256]{1,2,0:T(8,128)(2,1)}), bf16[4,256,256]{1,2,0:T(8,128)(2,1)S(1)}, u32[]{:S(2)}, u32[]{:S(2)}) async-start(bf16[4,256,256]{1,2,0:T(8,128)(2,1)} %broadcast_in_dim.20), calls=%async_computation.2 | async-start | bytes 1048576 | tf_op jit(solution)/shard_map/all_to_all | solution.py:167
  18.9 1.8 %shard_map.91.own_ref = bf16[32,4224]{1,0:T(8,128)(2,1)} custom-call(bf16[32,4096]{1,0:T(8,128)(2,1)} %grad_ref.1, s32[8,32]{1,0:T(8,128)} %bitcast.45, f32[8,32]{1,0:T(8,128)} %bitcast.46), custom_call_target="tpu_custom_call" | custom-call | tf_op jit(solution)/shard_map/pallas_call | solution.py:198
  20.7 13.3 %collective-permute-start.1 = (bf16[32,4224]{1,0:T(8,128)(2,1)}, bf16[32,4224]{1,0:T(8,128)(2,1)S(1)}, u32[]{:S(2)}, u32[]{:S(2)}) collective-permute-start(bf16[32,4224]{1,0:T(8,128)(2,1)} %shard_map.91.own_ref), channel_id=1, source_target_pairs={{0,88},{1,41},{8,96},{9,49},{16,104},{17,57},{24,112},{25,65},{32,... | collective-permute-start | bytes 811016 | tf_op jit(solution)/shard_map/ppermute | solution.py:161
  34.0 5.9 %collective-permute-start = (bf16[32,4224]{1,0:T(8,128)(2,1)}, bf16[32,4224]{1,0:T(8,128)(2,1)S(1)}, u32[]{:S(2)}, u32[]{:S(2)}) collective-permute-start(bf16[32,4224]{1,0:T(8,128)(2,1)} %shard_map.91.own_ref), channel_id=1, source_target_pairs={{0,40},{1,89},{8,48},{9,97},{16,56},{17,105},{24,64},{25,113},{32,... | collective-permute-start | bytes 811016 | tf_op jit(solution)/shard_map/ppermute | solution.py:161
  39.9 0.1 pad_add_fusion.place_ref
  39.9 2.4 %collective-permute-done.1.ahead_ref = bf16[32,4224]{1,0:T(8,128)(2,1)S(1)} collective-permute-done((bf16[32,4224]{1,0:T(8,128)(2,1)}, bf16[32,4224]{1,0:T(8,128)(2,1)S(1)}, u32[]{:S(2)}, u32[]{:S(2)}) %collective-permute-start.1) | collective-permute-done | bytes 270368 | tf_op jit(solution)/shard_map/ppermute | solution.py:161
  42.3 26.5 %collective-permute-done.behind_ref = bf16[32,4224]{1,0:T(8,128)(2,1)S(1)} collective-permute-done((bf16[32,4224]{1,0:T(8,128)(2,1)}, bf16[32,4224]{1,0:T(8,128)(2,1)S(1)}, u32[]{:S(2)}, u32[]{:S(2)}) %collective-permute-start) | collective-permute-done | bytes 270368 | tf_op jit(solution)/shard_map/ppermute | solution.py:161
  68.9 1.0 copy-done.1
  69.8 2.5 %shard_map.92 = (bf16[4,128,1024]{2,1,0:T(8,128)(2,1)}, bf16[16,4096]{1,0:T(8,128)(2,1)S(1)}, bf16[48,4096]{1,0:T(8,128)(2,1)S(1)}, bf16[48,4096]{1,0:T(8,128)(2,1)S(1)}, bf16[16,4096]{1,0:T(8,128)(2,1)S(1)}) custom-call(s32[2]{0:T(128)S(1)} %pad_add_fusion.place_ref, bf16[32,4224]{1,0:T(8,128)(2,1)S(1)} %copy-done.1, ...), custom_call_target="tpu_custom_call" | custom-call | tf_op jit(solution)/shard_map/pallas_call | solution.py:125
  72.4 0.0 all-to-all-done.2
  72.4 0.0 copy-start.7
  72.4 0.8 copy-done.2
  73.2 7.6 %all-to-all-start = ((bf16[32,16,1024]{2,1,0:T(8,128)(2,1)}), bf16[32,16,1024]{2,1,0:T(8,128)(2,1)S(1)}, u32[]{:S(2)}, u32[]{:S(2)}) async-start(bf16[32,16,1024]{2,1,0:T(8,128)(2,1)} %bitcast.4), calls=%async_computation | async-start | bytes 2097152 | tf_op jit(solution)/shard_map/all_to_all | solution.py:172
  80.8 4.8 %collective-permute-start.4 = (bf16[48,4096]{1,0:T(8,128)(2,1)S(1)}, bf16[48,4096]{1,0:T(8,128)(2,1)S(1)}, u32[]{:S(2)}, u32[]{:S(2)}) collective-permute-start(bf16[48,4096]{1,0:T(8,128)(2,1)S(1)} %get-tuple-element.12), channel_id=1, source_target_pairs={{0,16},{1,113},{8,24},{9,121},{16,32},{17,1},{24,40},{25,9},{32,48... | collective-permute-start | bytes 1179656 | tf_op jit(solution)/shard_map/ppermute | solution.py:161
  85.6 1.9 %collective-permute-start.5 = (bf16[48,4096]{1,0:T(8,128)(2,1)S(1)}, bf16[48,4096]{1,0:T(8,128)(2,1)S(1)}, u32[]{:S(2)}, u32[]{:S(2)}) collective-permute-start(bf16[48,4096]{1,0:T(8,128)(2,1)S(1)} %get-tuple-element.13), channel_id=1, source_target_pairs={{0,112},{1,17},{8,120},{9,25},{16,0},{17,33},{24,8},{25,41},{32,16... | collective-permute-start | bytes 1179656 | tf_op jit(solution)/shard_map/ppermute | solution.py:161
  87.5 7.4 %collective-permute-start.6 = (bf16[16,4096]{1,0:T(8,128)(2,1)S(1)}, bf16[16,4096]{1,0:T(8,128)(2,1)S(1)}, u32[]{:S(2)}, u32[]{:S(2)}) collective-permute-start(bf16[16,4096]{1,0:T(8,128)(2,1)S(1)} %get-tuple-element.14), channel_id=1, source_target_pairs={{0,24},{1,105},{8,32},{9,113},{16,40},{17,121},{24,48},{25,1},{32,... | collective-permute-start | bytes 393224 | tf_op jit(solution)/shard_map/ppermute | solution.py:161
  95.0 0.0 copy-done.5
  95.0 0.0 copy-done.6
  95.0 0.0 copy-done.7
  95.0 10.4 %collective-permute-done.6.refs_3_ = bf16[16,4096]{1,0:T(8,128)(2,1)S(1)} collective-permute-done((bf16[16,4096]{1,0:T(8,128)(2,1)S(1)}, bf16[16,4096]{1,0:T(8,128)(2,1)S(1)}, u32[]{:S(2)}, u32[]{:S(2)}) %collective-permute-start.6) | collective-permute-done | bytes 131104 | tf_op jit(solution)/shard_map/ppermute | solution.py:161
  105.4 0.0 collective-permute-done.4.refs_1_
  105.4 3.1 %collective-permute-done.5.refs_2_ = bf16[48,4096]{1,0:T(8,128)(2,1)S(1)} collective-permute-done((bf16[48,4096]{1,0:T(8,128)(2,1)S(1)}, bf16[48,4096]{1,0:T(8,128)(2,1)S(1)}, u32[]{:S(2)}, u32[]{:S(2)}) %collective-permute-start.5) | collective-permute-done | bytes 393248 | tf_op jit(solution)/shard_map/ppermute | solution.py:161
  108.5 1.4 %shard_map.93 = bf16[4,128,1024]{2,1,0:T(8,128)(2,1)} custom-call(bf16[16,4096]{1,0:T(8,128)(2,1)S(1)} %get-tuple-element.11.refs_0_, bf16[48,4096]{1,0:T(8,128)(2,1)S(1)} %collective-permute-done.4.refs_1_, bf16[48,4096]{1,0:T(8,128)(2,1)S(1)} %collective-permute-done.5.refs_2_, bf16[16,4096]{1,0:T(8,128)(2,1)S(1)} %collective-permute-done.6.refs_3_), custom_call_target="tpu_custom_call" | custom-call | tf_op jit(solution)/shard_map/pallas_call | solution.py:148
  110.0 0.0 copy-done.3
  110.0 0.6 fusion.2
  110.6 0.0 all-to-all-done
  110.6 7.3 %all-to-all-start.3 = ((bf16[32,16,1024]{2,1,0:T(8,128)(2,1)}), bf16[32,16,1024]{2,1,0:T(8,128)(2,1)}, u32[]{:S(2)}, u32[]{:S(2)}) async-start(bf16[32,16,1024]{2,1,0:T(8,128)(2,1)} %bitcast.16), calls=%async_computation.3 | async-start | bytes 2097152 | tf_op jit(solution)/shard_map/all_to_all | solution.py:172
  117.9 0.1 fusion.17
  118.0 0.1 copy.10
  118.1 0.8 fusion.16
  119.0 1.1 copy.12
  120.1 0.8 copy.11
  120.8 0.1 copy.13
  121.0 1.0 fusion.15
  122.0 2.7 %collective-permute-start.3 = (bf16[32,8,1024]{2,1,0:T(8,128)(2,1)}, bf16[32,8,1024]{2,1,0:T(8,128)(2,1)}, u32[]{:S(2)}, u32[]{:S(2)}) collective-permute-start(bf16[32,8,1024]{2,1,0:T(8,128)(2,1)} %get-tuple-element.15), channel_id=1, source_target_pairs={{0,120},{1,9},{8,0},{9,17},{16,8},{17,25},{24,16},{25,33},{32,24},... | collective-permute-start | bytes 1572872 | tf_op jit(solution)/shard_map/ppermute | solution.py:161
  124.7 3.8 %collective-permute-start.2 = (bf16[32,8,1024]{2,1,0:T(8,128)(2,1)}, bf16[32,8,1024]{2,1,0:T(8,128)(2,1)}, u32[]{:S(2)}, u32[]{:S(2)}) collective-permute-start(bf16[32,8,1024]{2,1,0:T(8,128)(2,1)} %get-tuple-element.16), channel_id=1, source_target_pairs={{0,8},{1,121},{8,16},{9,1},{16,24},{17,9},{24,32},{25,17},{32,40},... | collective-permute-start | bytes 1572872 | tf_op jit(solution)/shard_map/ppermute | solution.py:161
  128.5 0.5 fusion.18
  129.0 6.0 %all-to-all-done.3 = bf16[32,16,1024]{2,1,0:T(8,128)(2,1)} async-done(((bf16[32,16,1024]{2,1,0:T(8,128)(2,1)}), bf16[32,16,1024]{2,1,0:T(8,128)(2,1)}, u32[]{:S(2)}, u32[]{:S(2)}) %all-to-all-start.3) | async-done | bytes 1048608 | tf_op jit(solution)/shard_map/all_to_all | solution.py:172
  135.0 1.7 %fusion.19 = f32[1024,256]{1,0:T(8,128)S(1)} fusion(bf16[512,1024]{1,0:T(8,128)(2,1)} %bitcast.17, bf16[512,256]{1,0:T(8,128)(2,1)S(1)} %bitcast.41), kind=kOutput, calls=%fused_computation.27 | convolution fusion | flops 268435456 | bytes 2359296 | tf_op jit(solution)/shard_map/dot_general | solution.py:221
  136.7 2.2 %collective-permute-done.2 = bf16[32,8,1024]{2,1,0:T(8,128)(2,1)} collective-permute-done((bf16[32,8,1024]{2,1,0:T(8,128)(2,1)}, bf16[32,8,1024]{2,1,0:T(8,128)(2,1)}, u32[]{:S(2)}, u32[]{:S(2)}) %collective-permute-start.2) | collective-permute-done | bytes 524320 | tf_op jit(solution)/shard_map/ppermute | solution.py:161
  138.9 1.4 convolution_add_fusion.1
  140.4 0.0 collective-permute-done.3
  140.4 2.2 %fusion.3 = bf16[1,1024,256]{2,1,0:T(8,128)(2,1)} fusion(f32[1024,256]{1,0:T(8,128)S(1)} %fusion.19, f32[1024,256]{1,0:T(8,128)S(1)} %convolution_add_fusion.1, bf16[256,256]{1,0:T(8,128)(2,1)S(1)} %bitcast.42, bf16[32,8,1024]{2,1,0:T(8,128)(2,1)} %collective-permute-done.3), kind=kOutput, calls=%fused_computation.6 | convolution fusion | flops 135004160 | bytes 3276800 | tf_op jit(solution)/shard_map/dot_general | solution.py:221
  (11 shorter events, 0.0 us)
Async XLA Ops:
  0.0 14.2 %copy-start = (bf16[1,1,256,1536]{3,2,1,0:T(8,128)(2,1)S(1)}, bf16[1,1,256,1536]{3,2,1,0:T(8,128)(2,1)}, u32[]{:S(2)}) copy-start(bf16[1,1,256,1536]{3,2,1,0:T(8,128)(2,1)} %param.12) | copy-start | bytes 2359300
  15.5 56.9 %all-to-all-start.2 = ((bf16[4,256,256]{1,2,0:T(8,128)(2,1)}), bf16[4,256,256]{1,2,0:T(8,128)(2,1)S(1)}, u32[]{:S(2)}, u32[]{:S(2)}) async-start(bf16[4,256,256]{1,2,0:T(8,128)(2,1)} %broadcast_in_dim.20), calls=%async_computation.2 | async-start | bytes 1048576 | tf_op jit(solution)/shard_map/all_to_all | solution.py:167
  20.7 21.6 %collective-permute-start.1 = (bf16[32,4224]{1,0:T(8,128)(2,1)}, bf16[32,4224]{1,0:T(8,128)(2,1)S(1)}, u32[]{:S(2)}, u32[]{:S(2)}) collective-permute-start(bf16[32,4224]{1,0:T(8,128)(2,1)} %shard_map.91.own_ref), channel_id=1, source_target_pairs={{0,88},{1,41},{8,96},{9,49},{16,104},{17,57},{24,112},{25,65},{32,... | collective-permute-start | bytes 811016 | tf_op jit(solution)/shard_map/ppermute | solution.py:161
  34.0 34.9 %collective-permute-start = (bf16[32,4224]{1,0:T(8,128)(2,1)}, bf16[32,4224]{1,0:T(8,128)(2,1)S(1)}, u32[]{:S(2)}, u32[]{:S(2)}) collective-permute-start(bf16[32,4224]{1,0:T(8,128)(2,1)} %shard_map.91.own_ref), channel_id=1, source_target_pairs={{0,40},{1,89},{8,48},{9,97},{16,56},{17,105},{24,64},{25,113},{32,... | collective-permute-start | bytes 811016 | tf_op jit(solution)/shard_map/ppermute | solution.py:161
  68.9 1.0 copy-start.1
  72.4 0.8 copy-start.2
  72.4 22.6 %copy-start.5 = (s32[384]{0:T(512)S(1)}, s32[384]{0:T(512)}, u32[]{:S(2)}) copy-start(s32[384]{0:T(512)} %constant.42.clone) | copy-start | bytes 4612
  72.4 22.6 %copy-start.6 = (s32[384]{0:T(512)S(1)}, s32[384]{0:T(512)}, u32[]{:S(2)}) copy-start(s32[384]{0:T(512)} %constant.41.clone) | copy-start | bytes 4612
  72.4 22.6 %copy-start.7 = (s32[384]{0:T(512)S(1)}, s32[384]{0:T(512)}, u32[]{:S(2)}) copy-start(s32[384]{0:T(512)} %constant.40.clone) | copy-start | bytes 4612
  73.2 37.4 %all-to-all-start = ((bf16[32,16,1024]{2,1,0:T(8,128)(2,1)}), bf16[32,16,1024]{2,1,0:T(8,128)(2,1)S(1)}, u32[]{:S(2)}, u32[]{:S(2)}) async-start(bf16[32,16,1024]{2,1,0:T(8,128)(2,1)} %bitcast.4), calls=%async_computation | async-start | bytes 2097152 | tf_op jit(solution)/shard_map/all_to_all | solution.py:172
  80.8 24.6 %collective-permute-start.4 = (bf16[48,4096]{1,0:T(8,128)(2,1)S(1)}, bf16[48,4096]{1,0:T(8,128)(2,1)S(1)}, u32[]{:S(2)}, u32[]{:S(2)}) collective-permute-start(bf16[48,4096]{1,0:T(8,128)(2,1)S(1)} %get-tuple-element.12), channel_id=1, source_target_pairs={{0,16},{1,113},{8,24},{9,121},{16,32},{17,1},{24,40},{25,9},{32,48... | collective-permute-start | bytes 1179656 | tf_op jit(solution)/shard_map/ppermute | solution.py:161
  85.6 22.9 %collective-permute-start.5 = (bf16[48,4096]{1,0:T(8,128)(2,1)S(1)}, bf16[48,4096]{1,0:T(8,128)(2,1)S(1)}, u32[]{:S(2)}, u32[]{:S(2)}) collective-permute-start(bf16[48,4096]{1,0:T(8,128)(2,1)S(1)} %get-tuple-element.13), channel_id=1, source_target_pairs={{0,112},{1,17},{8,120},{9,25},{16,0},{17,33},{24,8},{25,41},{32,16... | collective-permute-start | bytes 1179656 | tf_op jit(solution)/shard_map/ppermute | solution.py:161
  87.5 17.9 %collective-permute-start.6 = (bf16[16,4096]{1,0:T(8,128)(2,1)S(1)}, bf16[16,4096]{1,0:T(8,128)(2,1)S(1)}, u32[]{:S(2)}, u32[]{:S(2)}) collective-permute-start(bf16[16,4096]{1,0:T(8,128)(2,1)S(1)} %get-tuple-element.14), channel_id=1, source_target_pairs={{0,24},{1,105},{8,32},{9,113},{16,40},{17,121},{24,48},{25,1},{32,... | collective-permute-start | bytes 393224 | tf_op jit(solution)/shard_map/ppermute | solution.py:161
  108.5 1.4 %copy-start.3 = (bf16[4,256,256]{1,2,0:T(8,128)(2,1)S(1)}, bf16[4,256,256]{1,2,0:T(8,128)(2,1)}, u32[]{:S(2)}) copy-start(bf16[4,256,256]{1,2,0:T(8,128)(2,1)} %copy-done.2) | copy-start | bytes 1572868
  108.5 1.4 %copy-start.8 = (pred[384]{0:T(512)(128)(4,1)S(1)}, pred[384]{0:T(512)(128)(4,1)}, u32[]{:S(2)}) copy-start(pred[384]{0:T(512)(128)(4,1)} %constant.49) | copy-start | bytes 1156
  110.6 24.4 %all-to-all-start.3 = ((bf16[32,16,1024]{2,1,0:T(8,128)(2,1)}), bf16[32,16,1024]{2,1,0:T(8,128)(2,1)}, u32[]{:S(2)}, u32[]{:S(2)}) async-start(bf16[32,16,1024]{2,1,0:T(8,128)(2,1)} %bitcast.16), calls=%async_computation.3 | async-start | bytes 2097152 | tf_op jit(solution)/shard_map/all_to_all | solution.py:172
  122.0 18.3 %collective-permute-start.3 = (bf16[32,8,1024]{2,1,0:T(8,128)(2,1)}, bf16[32,8,1024]{2,1,0:T(8,128)(2,1)}, u32[]{:S(2)}, u32[]{:S(2)}) collective-permute-start(bf16[32,8,1024]{2,1,0:T(8,128)(2,1)} %get-tuple-element.15), channel_id=1, source_target_pairs={{0,120},{1,9},{8,0},{9,17},{16,8},{17,25},{24,16},{25,33},{32,24},... | collective-permute-start | bytes 1572872 | tf_op jit(solution)/shard_map/ppermute | solution.py:161
  124.7 14.2 %collective-permute-start.2 = (bf16[32,8,1024]{2,1,0:T(8,128)(2,1)}, bf16[32,8,1024]{2,1,0:T(8,128)(2,1)}, u32[]{:S(2)}, u32[]{:S(2)}) collective-permute-start(bf16[32,8,1024]{2,1,0:T(8,128)(2,1)} %get-tuple-element.16), channel_id=1, source_target_pairs={{0,8},{1,121},{8,16},{9,1},{16,24},{17,9},{24,32},{25,17},{32,40},... | collective-permute-start | bytes 1572872 | tf_op jit(solution)/shard_map/ppermute | solution.py:161
  135.0 4.0 %copy-start.4 = (bf16[4,64,256]{2,1,0:T(8,128)(2,1)S(1)}, bf16[4,64,256]{2,1,0:T(8,128)(2,1)}, u32[]{:S(2)}) copy-start(bf16[4,64,256]{2,1,0:T(8,128)(2,1)} %copy.11) | copy-start | bytes 393220

commit v4 on v3

--- a/solution.py
+++ b/solution.py
@@ -189,6 +189,49 @@
     return (same & (real[:, None] > 0)).astype(BF16)
 
 
+def cut_kernel(in_ref, up_ref, down_ref):
+    half = up_ref.shape[1]
+    up_ref[...] = in_ref[:, :half]
+    down_ref[...] = in_ref[:, half:]
+
+
+def halves(array):
+    count, rows, width = array.shape
+    steps = 4
+
+    def spec(size):
+        return pl.BlockSpec((count // steps, size, width), lambda i: (i, 0, 0))
+
+    shape = jax.ShapeDtypeStruct((count, rows // 2, width), array.dtype)
+    return pl.pallas_call(
+        cut_kernel,
+        grid=(steps,),
+        in_specs=[spec(rows)],
+        out_specs=[spec(rows // 2)] * 2,
+        out_shape=[shape] * 2,
+        compiler_params=SMALL,
+    )(array)
+
+
+def order_kernel(move_ref, reduced_ref, *out_refs):
+    for replica in range(reduced_ref.shape[0]):
+        rows = jnp.dot(move_ref[...], reduced_ref[replica], preferred_element_type=F32)
+        at = 0
+        for ref in out_refs:
+            ref[replica] = rows[at : at + ref.shape[1]].astype(BF16)
+            at += ref.shape[1]
+
+
+def ordered(moves, reduced):
+    replicas, _, rank = reduced.shape
+    sizes = [2 * SEATS * count for count in (8, 4, 4, 8)]
+    return pl.pallas_call(
+        order_kernel,
+        out_shape=[jax.ShapeDtypeStruct((replicas, size, rank), BF16) for size in sizes],
+        compiler_params=SMALL,
+    )(moves, reduced)
+
+
 def layer(grad_out, expert_ids, route_weights, hidden_act, projection):
     parts = lax.axis_size("dp")
     tokens, width = grad_out.shape
@@ -202,30 +245,30 @@
     behind, ahead = shift(own, LEAP), shift(own, -LEAP)
 
     basis = gathered(projection[0], "dp").reshape(-1, rank)
+    moves = factor_moves(plane, sign, hidden_act.shape[2])
+    basis, moves = lax.optimization_barrier((basis, moves))
     reduced = jnp.dot(hidden_act[0, 0], basis, preferred_element_type=F32).astype(BF16)
     reduced = gathered(reduced, "dp")
-    moves = factor_moves(plane, sign, reduced.shape[1])
-    factor = jnp.einsum("as,rsk->rak", moves, reduced, preferred_element_type=F32).astype(BF16)
 
     near, stay, up2, down2, up3 = picked(plane, sign, own, behind, ahead, parts)
     up2, down2, up3 = shift(up2, 2), shift(down2, -2), shift(up3, 3)
+    near, reduced = lax.optimization_barrier((near, reduced))
     near = exchanged(near)
+    factors = ordered(moves, reduced)
     far = join([stay, up2, down2, up3], parts)
+    up1, down1 = halves(near)
+    far, up1 = lax.optimization_barrier((far, up1))
     far = exchanged(far)
-    up1 = shift(near[:, :8], 1)
-    down1 = shift(near[:, 8:], -1)
+    up1, down1 = shift(up1, 1), shift(down1, -1)
     total = None
-    at = 0
-    for piece in (near, up1, down1, far):
-        size = SEATS * piece.shape[1]
+    for piece, factor in zip((near, up1, down1, far), factors, strict=True):
         share = lax.dot_general(
             piece.reshape(-1, piece.shape[2]),
-            factor[:, at : at + size].reshape(-1, rank),
+            factor.reshape(-1, rank),
             (((0,), (0,)), ((), ())),
             preferred_element_type=F32,
         )
         total = share if total is None else total + share
-        at += size
     return total.astype(BF16)[None]
 
 

time: 143 us -> 141 us (0.986)
  blocking collectives: 13.1 us -> 0 us
  waiting for transfers between devices: 50.7 us -> 59.9 us
  starting transfers between devices: 58.1 us -> 62.1 us
  matrix products: 6.79 us -> 5.13 us
    all_to_all x1 -> x0, blocking collectives: 13.1 us -> none  [gathered(): return lax.all_to_all(copies, axis, split_axis=0, concat_axis=0, tiled=True)]
    all_to_all x1 -> x2, waiting for transfers between devices: 0.01 us -> 6.81 us  [gathered(): return lax.all_to_all(copies, axis, split_axis=0, concat_axis=0, tiled=True)]
    all_to_all x1 -> x2, starting transfers between devices: 3.47 us -> 8.6 us  [gathered(): return lax.all_to_all(copies, axis, split_axis=0, concat_axis=0, tiled=True)]
    slice x7 -> x0, local copies, waits for them, and re-layouts: 4.11 us -> none  [the longest x6 3.06 us: layer(): factor[:, at:at + size].reshape(-1, rank)]
    ppermute x7, waiting for transfers between devices: 44.7 us -> 48.6 us  [shift(): return lax.ppermute(array, ('z', 'core'), pairs)]
    unnamed x18 -> x16, local copies, waits for them, and re-layouts: 1.75 us -> 3.73 us
    dot_general x5 -> x4, matrix products: 6.37 us -> 4.71 us  [layer(): lax.dot_general(piece.reshape(-1, piece.shape[2]), factor.reshape(-1, ran...]
    all_to_all x2, waiting for transfers between devices: 5.99 us -> 4.48 us  [exchanged(): lax.all_to_all(array, ('dp', 'x', 'core'), split_axis=0, concat_axis=0, t...]
  transfers between devices with their start and end apart: 10 -> 11, of which waited for: 6 -> 7; matrix products, arithmetic and copies ran while one was open for 6% -> 2% of each run, Pallas kernels for 4% -> 4%
where the time goes in v4:
time: 141 us; the launch traced here: 140 us
  starting transfers between devices  62.1 us (44%)
  waiting for transfers between devices  59.9 us (42%)
  local copies, waits for them, and re-layouts  6.58 us (5%)
  Pallas kernels  6.27 us (4%)
  matrix products  5.13 us (4%)
    ppermute x7, waiting for transfers between devices, shift(): return lax.ppermute(array, ('z', 'core'), pairs)  48.6 us
    ppermute x7, starting transfers between devices, shift(): return lax.ppermute(array, ('z', 'core'), pairs)  38.5 us
    all_to_all x2, starting transfers between devices, exchanged(): lax.all_to_all(array, ('dp', 'x', 'core'), split_axis=0, concat_axis=0, t...  14.9 us
    all_to_all x2, starting transfers between devices, gathered(): return lax.all_to_all(copies, axis, split_axis=0, concat_axis=0, tiled=True)  8.6 us
    all_to_all x2, waiting for transfers between devices, gathered(): return lax.all_to_all(copies, axis, split_axis=0, concat_axis=0, tiled=True)  6.81 us
    dot_general x4, matrix products, layer(): lax.dot_general(piece.reshape(-1, piece.shape[2]), factor.reshape(-1, ran...  4.71 us
    all_to_all x2, waiting for transfers between devices, exchanged(): lax.all_to_all(array, ('dp', 'x', 'core'), split_axis=0, concat_axis=0, t...  4.48 us
    unnamed x16, local copies, waits for them, and re-layouts  3.73 us
  transfers between devices with their start and end apart: 11, of which 7 were waited for; matrix products, arithmetic and copies ran while one was open for 2% of the time, Pallas kernels for 4%

profile of v4, /device:TPU:1, one launch (start us, length us, event | category | flops | bytes accessed | tf_op | source)
XLA Modules:
  0.0 140.4 jit_solution(15163973865707612558)
XLA Ops:
  0.0 0.0 copy-start
  0.0 1.9 %broadcast_in_dim.9 = bf16[4,384,256]{2,1,0:T(8,128)(2,1)} broadcast(bf16[384,256]{1,0:T(8,128)(2,1)} %bitcast.40), dimensions={1,2} | broadcast | bytes 983040 | tf_op jit(solution)/shard_map/broadcast_in_dim | solution.py:166
  1.9 0.0 copy-start.6
  1.9 5.1 %all-to-all-start = ((bf16[4,384,256]{2,1,0:T(8,128)(2,1)}), bf16[4,384,256]{2,1,0:T(8,128)(2,1)S(1)}, u32[]{:S(2)}, u32[]{:S(2)}) async-start(bf16[4,384,256]{2,1,0:T(8,128)(2,1)} %broadcast_in_dim.9), calls=%async_computation | async-start | bytes 1572864 | tf_op jit(solution)/shard_map/all_to_all | solution.py:167
  7.1 0.0 copy-done.6
  7.1 0.7 copy-done.5
  7.7 0.0 copy-done.4
  7.8 0.6 copy-done.7
  8.4 0.2 fusion.8.move_ref
  8.6 6.8 %all-to-all-done = bf16[4,384,256]{2,1,0:T(8,128)(2,1)S(1)} async-done(((bf16[4,384,256]{2,1,0:T(8,128)(2,1)}), bf16[4,384,256]{2,1,0:T(8,128)(2,1)S(1)}, u32[]{:S(2)}, u32[]{:S(2)}) %all-to-all-start) | async-done | bytes 786464 | tf_op jit(solution)/shard_map/all_to_all | solution.py:167
  15.4 0.0 copy-done
  15.4 0.4 fusion.3
  15.8 0.1 copy.10
  15.9 0.8 broadcast_in_dim.20
  16.8 3.5 %all-to-all-start.1 = ((bf16[4,256,256]{2,1,0:T(8,128)(2,1)}), bf16[4,256,256]{2,1,0:T(8,128)(2,1)S(1)}, u32[]{:S(2)}, u32[]{:S(2)}) async-start(bf16[4,256,256]{2,1,0:T(8,128)(2,1)} %broadcast_in_dim.20), calls=%async_computation.1 | async-start | bytes 1048576 | tf_op jit(solution)/shard_map/all_to_all | solution.py:167
  20.2 1.8 %shard_map.91.own_ref = bf16[32,4224]{1,0:T(8,128)(2,1)} custom-call(bf16[32,4096]{1,0:T(8,128)(2,1)} %grad_ref.1, s32[8,32]{1,0:T(8,128)} %bitcast.41, f32[8,32]{1,0:T(8,128)} %bitcast.42), custom_call_target="tpu_custom_call" | custom-call | tf_op jit(solution)/shard_map/pallas_call | solution.py:241
  22.0 13.3 %collective-permute-start.1 = (bf16[32,4224]{1,0:T(8,128)(2,1)}, bf16[32,4224]{1,0:T(8,128)(2,1)S(1)}, u32[]{:S(2)}, u32[]{:S(2)}) collective-permute-start(bf16[32,4224]{1,0:T(8,128)(2,1)} %shard_map.91.own_ref), channel_id=1, source_target_pairs={{0,88},{1,41},{8,96},{9,49},{16,104},{17,57},{24,112},{25,65},{32,... | collective-permute-start | bytes 811016 | tf_op jit(solution)/shard_map/ppermute | solution.py:161
  35.3 5.9 %collective-permute-start = (bf16[32,4224]{1,0:T(8,128)(2,1)}, bf16[32,4224]{1,0:T(8,128)(2,1)S(1)}, u32[]{:S(2)}, u32[]{:S(2)}) collective-permute-start(bf16[32,4224]{1,0:T(8,128)(2,1)} %shard_map.91.own_ref), channel_id=1, source_target_pairs={{0,40},{1,89},{8,48},{9,97},{16,56},{17,105},{24,64},{25,113},{32,... | collective-permute-start | bytes 811016 | tf_op jit(solution)/shard_map/ppermute | solution.py:161
  41.2 0.1 pad_add_fusion.place_ref
  41.2 2.4 %collective-permute-done.1.ahead_ref = bf16[32,4224]{1,0:T(8,128)(2,1)S(1)} collective-permute-done((bf16[32,4224]{1,0:T(8,128)(2,1)}, bf16[32,4224]{1,0:T(8,128)(2,1)S(1)}, u32[]{:S(2)}, u32[]{:S(2)}) %collective-permute-start.1) | collective-permute-done | bytes 270368 | tf_op jit(solution)/shard_map/ppermute | solution.py:161
  43.6 26.5 %collective-permute-done.behind_ref = bf16[32,4224]{1,0:T(8,128)(2,1)S(1)} collective-permute-done((bf16[32,4224]{1,0:T(8,128)(2,1)}, bf16[32,4224]{1,0:T(8,128)(2,1)S(1)}, u32[]{:S(2)}, u32[]{:S(2)}) %collective-permute-start) | collective-permute-done | bytes 270368 | tf_op jit(solution)/shard_map/ppermute | solution.py:161
  70.2 1.0 copy-done.1
  71.1 2.6 %shard_map.92 = (bf16[4,128,1024]{2,1,0:T(8,128)(2,1)}, bf16[16,4096]{1,0:T(8,128)(2,1)S(1)}, bf16[48,4096]{1,0:T(8,128)(2,1)S(1)}, bf16[48,4096]{1,0:T(8,128)(2,1)S(1)}, bf16[16,4096]{1,0:T(8,128)(2,1)S(1)}) custom-call(s32[2]{0:T(128)S(1)} %pad_add_fusion.place_ref, bf16[32,4224]{1,0:T(8,128)(2,1)S(1)} %copy-done.1, ...), custom_call_target="tpu_custom_call" | custom-call | tf_op jit(solution)/shard_map/pallas_call | solution.py:125
  73.7 0.6 copy-done.3
  74.4 0.0 all-to-all-done.1.reduced_ref
  74.4 7.6 %all-to-all-start.2 = ((bf16[32,16,1024]{2,1,0:T(8,128)(2,1)}), bf16[32,16,1024]{2,1,0:T(8,128)(2,1)S(1)}, u32[]{:S(2)}, u32[]{:S(2)}) async-start(bf16[32,16,1024]{2,1,0:T(8,128)(2,1)} %bitcast.8), calls=%async_computation.2 | async-start | bytes 2097152 | tf_op jit(solution)/shard_map/all_to_all | solution.py:172
  82.0 4.8 %collective-permute-start.2 = (bf16[48,4096]{1,0:T(8,128)(2,1)S(1)}, bf16[48,4096]{1,0:T(8,128)(2,1)S(1)}, u32[]{:S(2)}, u32[]{:S(2)}) collective-permute-start(bf16[48,4096]{1,0:T(8,128)(2,1)S(1)} %get-tuple-element.29), channel_id=1, source_target_pairs={{0,16},{1,113},{8,24},{9,121},{16,32},{17,1},{24,40},{25,9},{32,48... | collective-permute-start | bytes 1179656 | tf_op jit(solution)/shard_map/ppermute | solution.py:161
  86.8 1.9 %collective-permute-start.3 = (bf16[48,4096]{1,0:T(8,128)(2,1)S(1)}, bf16[48,4096]{1,0:T(8,128)(2,1)S(1)}, u32[]{:S(2)}, u32[]{:S(2)}) collective-permute-start(bf16[48,4096]{1,0:T(8,128)(2,1)S(1)} %get-tuple-element.30), channel_id=1, source_target_pairs={{0,112},{1,17},{8,120},{9,25},{16,0},{17,33},{24,8},{25,41},{32,16... | collective-permute-start | bytes 1179656 | tf_op jit(solution)/shard_map/ppermute | solution.py:161
  88.7 7.4 %collective-permute-start.4 = (bf16[16,4096]{1,0:T(8,128)(2,1)}, bf16[16,4096]{1,0:T(8,128)(2,1)S(1)}, u32[]{:S(2)}, u32[]{:S(2)}) collective-permute-start(bf16[16,4096]{1,0:T(8,128)(2,1)} %copy-done.3), channel_id=1, source_target_pairs={{0,24},{1,105},{8,32},{9,113},{16,40},{17,121},{24,48},{25,1},{32,... | collective-permute-start | bytes 393224 | tf_op jit(solution)/shard_map/ppermute | solution.py:161
  96.2 10.4 %collective-permute-done.4.refs_3_ = bf16[16,4096]{1,0:T(8,128)(2,1)S(1)} collective-permute-done((bf16[16,4096]{1,0:T(8,128)(2,1)}, bf16[16,4096]{1,0:T(8,128)(2,1)S(1)}, u32[]{:S(2)}, u32[]{:S(2)}) %collective-permute-start.4) | collective-permute-done | bytes 131104 | tf_op jit(solution)/shard_map/ppermute | solution.py:161
  106.6 0.0 collective-permute-done.2.refs_1_
  106.6 3.1 %collective-permute-done.3.refs_2_ = bf16[48,4096]{1,0:T(8,128)(2,1)S(1)} collective-permute-done((bf16[48,4096]{1,0:T(8,128)(2,1)S(1)}, bf16[48,4096]{1,0:T(8,128)(2,1)S(1)}, u32[]{:S(2)}, u32[]{:S(2)}) %collective-permute-start.3) | collective-permute-done | bytes 393248 | tf_op jit(solution)/shard_map/ppermute | solution.py:161
  109.7 1.4 shard_map.94
  111.1 0.0 all-to-all-done.2.in_ref
  111.1 0.1 shard_map.95
  111.2 0.0 copy-start.2
  111.3 0.8 copy-done.2
  112.0 7.3 %all-to-all-start.3 = ((bf16[32,16,1024]{2,1,0:T(8,128)(2,1)}), bf16[32,16,1024]{2,1,0:T(8,128)(2,1)}, u32[]{:S(2)}, u32[]{:S(2)}) async-start(bf16[32,16,1024]{2,1,0:T(8,128)(2,1)} %bitcast.15), calls=%async_computation.3 | async-start | bytes 2097152 | tf_op jit(solution)/shard_map/all_to_all | solution.py:172
  119.4 1.9 %collective-permute-start.5 = (bf16[32,8,1024]{2,1,0:T(8,128)(2,1)}, bf16[32,8,1024]{2,1,0:T(8,128)(2,1)S(1)}, u32[]{:S(2)}, u32[]{:S(2)}) collective-permute-start(bf16[32,8,1024]{2,1,0:T(8,128)(2,1)} %copy-done.2), channel_id=1, source_target_pairs={{0,8},{1,121},{8,16},{9,1},{16,24},{17,9},{24,32},{25,17},{32,40},... | collective-permute-start | bytes 1572872 | tf_op jit(solution)/shard_map/ppermute | solution.py:161
  121.3 0.4 shard_map.93
  121.7 3.4 %collective-permute-start.6 = (bf16[32,8,1024]{2,1,0:T(8,128)(2,1)S(1)}, bf16[32,8,1024]{2,1,0:T(8,128)(2,1)}, u32[]{:S(2)}, u32[]{:S(2)}) collective-permute-start(bf16[32,8,1024]{2,1,0:T(8,128)(2,1)S(1)} %get-tuple-element.35), channel_id=1, source_target_pairs={{0,120},{1,9},{8,0},{9,17},{16,8},{17,25},{24,16},{25,33},{32,24},... | collective-permute-start | bytes 1572872 | tf_op jit(solution)/shard_map/ppermute | solution.py:161
  125.0 0.5 fusion.12
  125.5 6.1 %collective-permute-done.5 = bf16[32,8,1024]{2,1,0:T(8,128)(2,1)S(1)} collective-permute-done((bf16[32,8,1024]{2,1,0:T(8,128)(2,1)}, bf16[32,8,1024]{2,1,0:T(8,128)(2,1)S(1)}, u32[]{:S(2)}, u32[]{:S(2)}) %collective-permute-start.5) | collective-permute-done | bytes 524320 | tf_op jit(solution)/shard_map/ppermute | solution.py:161
  131.6 0.3 convolution_add_fusion.1
  132.0 4.5 %all-to-all-done.3 = bf16[32,16,1024]{2,1,0:T(8,128)(2,1)} async-done(((bf16[32,16,1024]{2,1,0:T(8,128)(2,1)}), bf16[32,16,1024]{2,1,0:T(8,128)(2,1)}, u32[]{:S(2)}, u32[]{:S(2)}) %all-to-all-start.3) | async-done | bytes 1048608 | tf_op jit(solution)/shard_map/all_to_all | solution.py:172
  136.5 1.7 %fusion.13 = f32[1024,256]{1,0:T(8,128)S(1)} fusion(bf16[512,1024]{1,0:T(8,128)(2,1)} %bitcast.16, bf16[512,256]{1,0:T(8,128)(2,1)S(1)} %bitcast.35), kind=kOutput, calls=%fused_computation.21 | convolution fusion | flops 268435456 | bytes 2359296 | tf_op jit(solution)/shard_map/dot_general | solution.py:265
  138.2 0.0 collective-permute-done.6
  138.2 2.2 %fusion.2 = bf16[1,1024,256]{2,1,0:T(8,128)(2,1)} fusion(f32[1024,256]{1,0:T(8,128)S(1)} %fusion.13, f32[1024,256]{1,0:T(8,128)S(1)} %convolution_add_fusion.1, bf16[256,256]{1,0:T(8,128)(2,1)S(1)} %bitcast.37, bf16[32,8,1024]{2,1,0:T(8,128)(2,1)} %collective-permute-done.6), kind=kOutput, calls=%fused_computation.4 | convolution fusion | flops 135004160 | bytes 3276800 | tf_op jit(solution)/shard_map/dot_general | solution.py:265
  (6 shorter events, 0.0 us)
Async XLA Ops:
  0.0 15.4 %copy-start = (bf16[1,1,256,1536]{3,2,1,0:T(8,128)(2,1)S(1)}, bf16[1,1,256,1536]{3,2,1,0:T(8,128)(2,1)}, u32[]{:S(2)}) copy-start(bf16[1,1,256,1536]{3,2,1,0:T(8,128)(2,1)} %param.12) | copy-start | bytes 2359300
  1.9 5.1 %copy-start.6 = (s32[384]{0:T(512)S(1)}, s32[384]{0:T(512)}, u32[]{:S(2)}) copy-start(s32[384]{0:T(512)} %constant.40.clone) | copy-start | bytes 4612
  1.9 13.5 %all-to-all-start = ((bf16[4,384,256]{2,1,0:T(8,128)(2,1)}), bf16[4,384,256]{2,1,0:T(8,128)(2,1)S(1)}, u32[]{:S(2)}, u32[]{:S(2)}) async-start(bf16[4,384,256]{2,1,0:T(8,128)(2,1)} %broadcast_in_dim.9), calls=%async_computation | async-start | bytes 1572864 | tf_op jit(solution)/shard_map/all_to_all | solution.py:167
  7.1 0.7 copy-start.5
  7.1 0.7 copy-start.4
  7.8 0.7 copy-start.7
  16.8 57.6 %all-to-all-start.1 = ((bf16[4,256,256]{2,1,0:T(8,128)(2,1)}), bf16[4,256,256]{2,1,0:T(8,128)(2,1)S(1)}, u32[]{:S(2)}, u32[]{:S(2)}) async-start(bf16[4,256,256]{2,1,0:T(8,128)(2,1)} %broadcast_in_dim.20), calls=%async_computation.1 | async-start | bytes 1048576 | tf_op jit(solution)/shard_map/all_to_all | solution.py:167
  22.0 21.6 %collective-permute-start.1 = (bf16[32,4224]{1,0:T(8,128)(2,1)}, bf16[32,4224]{1,0:T(8,128)(2,1)S(1)}, u32[]{:S(2)}, u32[]{:S(2)}) collective-permute-start(bf16[32,4224]{1,0:T(8,128)(2,1)} %shard_map.91.own_ref), channel_id=1, source_target_pairs={{0,88},{1,41},{8,96},{9,49},{16,104},{17,57},{24,112},{25,65},{32,... | collective-permute-start | bytes 811016 | tf_op jit(solution)/shard_map/ppermute | solution.py:161
  35.3 34.9 %collective-permute-start = (bf16[32,4224]{1,0:T(8,128)(2,1)}, bf16[32,4224]{1,0:T(8,128)(2,1)S(1)}, u32[]{:S(2)}, u32[]{:S(2)}) collective-permute-start(bf16[32,4224]{1,0:T(8,128)(2,1)} %shard_map.91.own_ref), channel_id=1, source_target_pairs={{0,40},{1,89},{8,48},{9,97},{16,56},{17,105},{24,64},{25,113},{32,... | collective-permute-start | bytes 811016 | tf_op jit(solution)/shard_map/ppermute | solution.py:161
  70.2 1.0 copy-start.1
  73.7 0.6 copy-start.3
  74.4 36.7 %all-to-all-start.2 = ((bf16[32,16,1024]{2,1,0:T(8,128)(2,1)}), bf16[32,16,1024]{2,1,0:T(8,128)(2,1)S(1)}, u32[]{:S(2)}, u32[]{:S(2)}) async-start(bf16[32,16,1024]{2,1,0:T(8,128)(2,1)} %bitcast.8), calls=%async_computation.2 | async-start | bytes 2097152 | tf_op jit(solution)/shard_map/all_to_all | solution.py:172
  82.0 24.6 %collective-permute-start.2 = (bf16[48,4096]{1,0:T(8,128)(2,1)S(1)}, bf16[48,4096]{1,0:T(8,128)(2,1)S(1)}, u32[]{:S(2)}, u32[]{:S(2)}) collective-permute-start(bf16[48,4096]{1,0:T(8,128)(2,1)S(1)} %get-tuple-element.29), channel_id=1, source_target_pairs={{0,16},{1,113},{8,24},{9,121},{16,32},{17,1},{24,40},{25,9},{32,48... | collective-permute-start | bytes 1179656 | tf_op jit(solution)/shard_map/ppermute | solution.py:161
  86.8 22.9 %collective-permute-start.3 = (bf16[48,4096]{1,0:T(8,128)(2,1)S(1)}, bf16[48,4096]{1,0:T(8,128)(2,1)S(1)}, u32[]{:S(2)}, u32[]{:S(2)}) collective-permute-start(bf16[48,4096]{1,0:T(8,128)(2,1)S(1)} %get-tuple-element.30), channel_id=1, source_target_pairs={{0,112},{1,17},{8,120},{9,25},{16,0},{17,33},{24,8},{25,41},{32,16... | collective-permute-start | bytes 1179656 | tf_op jit(solution)/shard_map/ppermute | solution.py:161
  88.7 17.9 %collective-permute-start.4 = (bf16[16,4096]{1,0:T(8,128)(2,1)}, bf16[16,4096]{1,0:T(8,128)(2,1)S(1)}, u32[]{:S(2)}, u32[]{:S(2)}) collective-permute-start(bf16[16,4096]{1,0:T(8,128)(2,1)} %copy-done.3), channel_id=1, source_target_pairs={{0,24},{1,105},{8,32},{9,113},{16,40},{17,121},{24,48},{25,1},{32,... | collective-permute-start | bytes 393224 | tf_op jit(solution)/shard_map/ppermute | solution.py:161
  111.2 0.8 copy-start.2
  112.0 24.4 %all-to-all-start.3 = ((bf16[32,16,1024]{2,1,0:T(8,128)(2,1)}), bf16[32,16,1024]{2,1,0:T(8,128)(2,1)}, u32[]{:S(2)}, u32[]{:S(2)}) async-start(bf16[32,16,1024]{2,1,0:T(8,128)(2,1)} %bitcast.15), calls=%async_computation.3 | async-start | bytes 2097152 | tf_op jit(solution)/shard_map/all_to_all | solution.py:172
  119.4 12.3 %collective-permute-start.5 = (bf16[32,8,1024]{2,1,0:T(8,128)(2,1)}, bf16[32,8,1024]{2,1,0:T(8,128)(2,1)S(1)}, u32[]{:S(2)}, u32[]{:S(2)}) collective-permute-start(bf16[32,8,1024]{2,1,0:T(8,128)(2,1)} %copy-done.2), channel_id=1, source_target_pairs={{0,8},{1,121},{8,16},{9,1},{16,24},{17,9},{24,32},{25,17},{32,40},... | collective-permute-start | bytes 1572872 | tf_op jit(solution)/shard_map/ppermute | solution.py:161
  121.7 16.5 %collective-permute-start.6 = (bf16[32,8,1024]{2,1,0:T(8,128)(2,1)S(1)}, bf16[32,8,1024]{2,1,0:T(8,128)(2,1)}, u32[]{:S(2)}, u32[]{:S(2)}) collective-permute-start(bf16[32,8,1024]{2,1,0:T(8,128)(2,1)S(1)} %get-tuple-element.35), channel_id=1, source_target_pairs={{0,120},{1,9},{8,0},{9,17},{16,8},{17,25},{24,16},{25,33},{32,24},... | collective-permute-start | bytes 1572872 | tf_op jit(solution)/shard_map/ppermute | solution.py:161

commit v5 on v4

--- a/solution.py
+++ b/solution.py
@@ -10,7 +10,7 @@
 
 PLANES = 16
 SEATS = 8
-LEAP = 5
+LEAP = 4
 META = 128
 TOPK = 8
 GROUP = 2 * SEATS
@@ -19,8 +19,8 @@
 
 START = (0, -LEAP, LEAP)
 NEAR = ((1, 0), (1, 1), (1, 2), (0, 0), (-1, 0), (-1, 1), (-1, 2), (0, 1))
-FAR = ((0, 2), (2, 0), (2, 1), (2, 2), (-2, 0), (-2, 1), (-2, 2), (3, 1))
-CUTS = (GROUP, 3 * GROUP, 3 * GROUP, GROUP)
+FAR = ((0, 2), (2, 0), (2, 1), (-2, 0), (-2, 2), (3, 1), (-3, 2), (4, 1))
+CUTS = (GROUP, 2 * GROUP, 2 * GROUP, GROUP, GROUP, GROUP)
 
 
 def origins(table, moved):
@@ -57,7 +57,8 @@
     out_ref[:, width:] = turned.astype(BF16)
 
 
-def pick_kernel(place_ref, own_ref, behind_ref, ahead_ref, near_ref, *far_refs):
+def pick_kernel(place_ref, own_ref, behind_ref, ahead_ref, near_out, *rest):
+    far_outs, (near_ref, far_ref, sems) = rest[: len(CUTS)], rest[len(CUTS) :]
     refs = (own_ref, behind_ref, ahead_ref)
     tokens = own_ref.shape[0]
     width = own_ref.shape[1] - META
@@ -106,17 +107,26 @@
 
     near, near_weight = choose(NEAR, (row // 2) % 8, row // GROUP, (1, -1))
     far, far_weight = choose(FAR, row // GROUP, (row // 2) % SEATS, (sign,))
+    copies = []
+
+    def send(source, goal):
+        copies.append(pltpu.make_async_copy(source, goal, sems.at[len(copies)]))
+        copies[-1].start()
+
     for part in range(parts):
         cut = pl.ds(part * part_width, part_width)
         tile = jnp.concatenate([ref[:, cut] for ref in refs], axis=0)
         rows = jnp.dot(far, tile, preferred_element_type=F32)
-        rows = (far_weight * rows).astype(BF16)
+        far_ref[:, cut] = (far_weight * rows).astype(BF16)
         at = 0
-        for ref, size in zip(far_refs, CUTS, strict=True):
-            ref[:, cut] = rows[at : at + size]
+        for out, size in zip(far_outs, CUTS, strict=True):
+            send(far_ref.at[pl.ds(at, size), cut], out.at[:, cut])
             at += size
         rows = jnp.dot(near, tile, preferred_element_type=F32)
         near_ref[part] = (near_weight * rows).astype(BF16)
+        send(near_ref.at[part], near_out.at[part])
+    for copy_out in copies:
+        copy_out.wait()
 
 
 def picked(plane, sign, own, behind, ahead, parts):
@@ -125,7 +135,13 @@
     return pl.pallas_call(
         pick_kernel,
         in_specs=[pl.BlockSpec(memory_space=pltpu.SMEM)] + [pl.BlockSpec(memory_space=pltpu.VMEM)] * 3,
+        out_specs=[pl.BlockSpec(memory_space=pltpu.HBM)] * len(shapes),
         out_shape=[jax.ShapeDtypeStruct(shape, BF16) for shape in shapes],
+        scratch_shapes=[
+            pltpu.VMEM(shapes[0], BF16),
+            pltpu.VMEM((sum(CUTS), width), BF16),
+            pltpu.SemaphoreType.DMA((parts * len(shapes),)),
+        ],
         compiler_params=SMALL,
     )(jnp.stack([plane, sign]).astype(jnp.int32), own, behind, ahead)
 
@@ -189,26 +205,25 @@
     return (same & (real[:, None] > 0)).astype(BF16)
 
 
-def cut_kernel(in_ref, up_ref, down_ref):
+def cut_kernel(in_ref, up_ref, down_ref, sems):
     half = up_ref.shape[1]
-    up_ref[...] = in_ref[:, :half]
-    down_ref[...] = in_ref[:, half:]
+    up = pltpu.make_async_copy(in_ref.at[:, pl.ds(0, half)], up_ref, sems.at[0])
+    down = pltpu.make_async_copy(in_ref.at[:, pl.ds(half, half)], down_ref, sems.at[1])
+    up.start()
+    down.start()
+    up.wait()
+    down.wait()
 
 
 def halves(array):
     count, rows, width = array.shape
-    steps = 4
-
-    def spec(size):
-        return pl.BlockSpec((count // steps, size, width), lambda i: (i, 0, 0))
-
     shape = jax.ShapeDtypeStruct((count, rows // 2, width), array.dtype)
     return pl.pallas_call(
         cut_kernel,
-        grid=(steps,),
-        in_specs=[spec(rows)],
-        out_specs=[spec(rows // 2)] * 2,
+        in_specs=[pl.BlockSpec(memory_space=pltpu.VMEM)],
+        out_specs=[pl.BlockSpec(memory_space=pltpu.HBM)] * 2,
         out_shape=[shape] * 2,
+        scratch_shapes=[pltpu.SemaphoreType.DMA((2,))],
         compiler_params=SMALL,
     )(array)
 
@@ -250,12 +265,13 @@
     reduced = jnp.dot(hidden_act[0, 0], basis, preferred_element_type=F32).astype(BF16)
     reduced = gathered(reduced, "dp")
 
-    near, stay, up2, down2, up3 = picked(plane, sign, own, behind, ahead, parts)
-    up2, down2, up3 = shift(up2, 2), shift(down2, -2), shift(up3, 3)
+    near, stay, up2, down2, up3, down3, up4 = picked(plane, sign, own, behind, ahead, parts)
+    up2, down2 = shift(up2, 2), shift(down2, -2)
+    up3, down3, up4 = shift(up3, 3), shift(down3, -3), shift(up4, 4)
     near, reduced = lax.optimization_barrier((near, reduced))
     near = exchanged(near)
     factors = ordered(moves, reduced)
-    far = join([stay, up2, down2, up3], parts)
+    far = join([stay, up2, down2, up3, down3, up4], parts)
     up1, down1 = halves(near)
     far, up1 = lax.optimization_barrier((far, up1))
     far = exchanged(far)

time: 141 us -> 142 us (level)
  waiting for transfers between devices: 59.9 us -> 45.5 us
  starting transfers between devices: 62.1 us -> 76.2 us
    ppermute x7 -> x9, waiting for transfers between devices: 48.6 us -> 37.9 us  [shift(): return lax.ppermute(array, ('z', 'core'), pairs)]
    ppermute x7 -> x9, starting transfers between devices: 38.5 us -> 45.8 us  [shift(): return lax.ppermute(array, ('z', 'core'), pairs)]
    all_to_all x2, starting transfers between devices: 14.9 us -> 21.8 us  [exchanged(): lax.all_to_all(array, ('dp', 'x', 'core'), split_axis=0, concat_axis=0, t...]
    all_to_all x2, waiting for transfers between devices: 4.48 us -> 0.78 us  [exchanged(): lax.all_to_all(array, ('dp', 'x', 'core'), split_axis=0, concat_axis=0, t...]
  transfers between devices with their start and end apart: 11 -> 13, of which waited for: 7 -> 9; matrix products, arithmetic and copies ran while one was open for 2% -> 2% of each run, Pallas kernels for 4% -> 5%
where the time goes in v5:
time: 142 us; the launch traced here: 141 us
  starting transfers between devices  76.2 us (54%)
  waiting for transfers between devices  45.5 us (32%)
  Pallas kernels  7.23 us (5%)
  local copies, waits for them, and re-layouts  6.58 us (5%)
  matrix products  5.12 us (4%)
    ppermute x9, starting transfers between devices, shift(): return lax.ppermute(array, ('z', 'core'), pairs)  45.8 us
    ppermute x9, waiting for transfers between devices, shift(): return lax.ppermute(array, ('z', 'core'), pairs)  37.9 us
    all_to_all x2, starting transfers between devices, exchanged(): lax.all_to_all(array, ('dp', 'x', 'core'), split_axis=0, concat_axis=0, t...  21.8 us
    all_to_all x2, starting transfers between devices, gathered(): return lax.all_to_all(copies, axis, split_axis=0, concat_axis=0, tiled=True)  8.6 us
    all_to_all x2, waiting for transfers between devices, gathered(): return lax.all_to_all(copies, axis, split_axis=0, concat_axis=0, tiled=True)  6.81 us
    dot_general x4, matrix products, layer(): lax.dot_general(piece.reshape(-1, piece.shape[2]), factor.reshape(-1, ran...  4.71 us
    unnamed x16, local copies, waits for them, and re-layouts  3.72 us
    pallas_call x1, Pallas kernels, picked(): pl.pallas_call(pick_kernel, in_specs=[pl.BlockSpec(memory_space=pltpu.SME...  3.58 us
  transfers between devices with their start and end apart: 13, of which 9 were waited for; matrix products, arithmetic and copies ran while one was open for 2% of the time, Pallas kernels for 5%

profile of v5, /device:TPU:1, one launch (start us, length us, event | category | flops | bytes accessed | tf_op | source)
XLA Modules:
  0.0 141.0 jit_solution(11373989561874171551)
XLA Ops:
  0.0 1.9 %broadcast_in_dim.9 = bf16[4,384,256]{2,1,0:T(8,128)(2,1)} broadcast(bf16[384,256]{1,0:T(8,128)(2,1)} %bitcast.40), dimensions={1,2} | broadcast | bytes 983040 | tf_op jit(solution)/shard_map/broadcast_in_dim | solution.py:182
  1.9 5.1 %all-to-all-start = ((bf16[4,384,256]{2,1,0:T(8,128)(2,1)}), bf16[4,384,256]{2,1,0:T(8,128)(2,1)S(1)}, u32[]{:S(2)}, u32[]{:S(2)}) async-start(bf16[4,384,256]{2,1,0:T(8,128)(2,1)} %broadcast_in_dim.9), calls=%async_computation | async-start | bytes 1572864 | tf_op jit(solution)/shard_map/all_to_all | solution.py:183
  7.1 0.7 copy-done.5
  7.8 0.0 copy-done.4
  7.8 0.6 copy-done.7
  8.4 0.2 fusion.8.move_ref
  8.6 6.8 %all-to-all-done = bf16[4,384,256]{2,1,0:T(8,128)(2,1)S(1)} async-done(((bf16[4,384,256]{2,1,0:T(8,128)(2,1)}), bf16[4,384,256]{2,1,0:T(8,128)(2,1)S(1)}, u32[]{:S(2)}, u32[]{:S(2)}) %all-to-all-start) | async-done | bytes 786464 | tf_op jit(solution)/shard_map/all_to_all | solution.py:183
  15.4 0.4 fusion.3
  15.8 0.1 copy.10
  15.9 0.8 broadcast_in_dim.20
  16.8 3.5 %all-to-all-start.1 = ((bf16[4,256,256]{2,1,0:T(8,128)(2,1)}), bf16[4,256,256]{2,1,0:T(8,128)(2,1)S(1)}, u32[]{:S(2)}, u32[]{:S(2)}) async-start(bf16[4,256,256]{2,1,0:T(8,128)(2,1)} %broadcast_in_dim.20), calls=%async_computation.1 | async-start | bytes 1048576 | tf_op jit(solution)/shard_map/all_to_all | solution.py:183
  20.3 1.8 %shard_map.91.own_ref = bf16[32,4224]{1,0:T(8,128)(2,1)} custom-call(bf16[32,4096]{1,0:T(8,128)(2,1)} %grad_ref.1, s32[8,32]{1,0:T(8,128)} %bitcast.41, f32[8,32]{1,0:T(8,128)} %bitcast.42), custom_call_target="tpu_custom_call" | custom-call | tf_op jit(solution)/shard_map/pallas_call | solution.py:256
  22.0 11.9 %collective-permute-start.1 = (bf16[32,4224]{1,0:T(8,128)(2,1)}, bf16[32,4224]{1,0:T(8,128)(2,1)S(1)}, u32[]{:S(2)}, u32[]{:S(2)}) collective-permute-start(bf16[32,4224]{1,0:T(8,128)(2,1)} %shard_map.91.own_ref), channel_id=1, source_target_pairs={{0,96},{1,33},{8,104},{9,41},{16,112},{17,49},{24,120},{25,57},{32... | collective-permute-start | bytes 811016 | tf_op jit(solution)/shard_map/ppermute | solution.py:177
  34.0 5.6 %collective-permute-start = (bf16[32,4224]{1,0:T(8,128)(2,1)}, bf16[32,4224]{1,0:T(8,128)(2,1)S(1)}, u32[]{:S(2)}, u32[]{:S(2)}) collective-permute-start(bf16[32,4224]{1,0:T(8,128)(2,1)} %shard_map.91.own_ref), channel_id=1, source_target_pairs={{0,32},{1,97},{8,40},{9,105},{16,48},{17,113},{24,56},{25,121},{32... | collective-permute-start | bytes 811016 | tf_op jit(solution)/shard_map/ppermute | solution.py:177
  39.5 0.1 pad_add_fusion.place_ref
  39.6 2.5 %collective-permute-done.1.ahead_ref = bf16[32,4224]{1,0:T(8,128)(2,1)S(1)} collective-permute-done((bf16[32,4224]{1,0:T(8,128)(2,1)}, bf16[32,4224]{1,0:T(8,128)(2,1)S(1)}, u32[]{:S(2)}, u32[]{:S(2)}) %collective-permute-start.1) | collective-permute-done | bytes 270368 | tf_op jit(solution)/shard_map/ppermute | solution.py:177
  42.1 19.0 %collective-permute-done.behind_ref = bf16[32,4224]{1,0:T(8,128)(2,1)S(1)} collective-permute-done((bf16[32,4224]{1,0:T(8,128)(2,1)}, bf16[32,4224]{1,0:T(8,128)(2,1)S(1)}, u32[]{:S(2)}, u32[]{:S(2)}) %collective-permute-start) | collective-permute-done | bytes 270368 | tf_op jit(solution)/shard_map/ppermute | solution.py:177
  61.1 1.0 copy-done.1
  62.1 3.6 %shard_map.92 = (bf16[4,128,1024]{2,1,0:T(8,128)(2,1)}, bf16[16,4096]{1,0:T(8,128)(2,1)S(1)}, bf16[32,4096]{1,0:T(8,128)(2,1)S(1)}, bf16[32,4096]{1,0:T(8,128)(2...) custom-call(s32[2]{0:T(128)S(1)} %pad_add_fusion.place_ref, ...), custom_call_target="tpu_custom_call" | custom-call | tf_op jit(solution)/shard_map/pallas_call | solution.py:135
  65.6 0.6 copy-done.3
  66.3 0.0 all-to-all-done.1.reduced_ref
  66.3 11.6 %all-to-all-start.2 = ((bf16[32,16,1024]{2,1,0:T(8,128)(2,1)}), bf16[32,16,1024]{2,1,0:T(8,128)(2,1)S(1)}, u32[]{:S(2)}, u32[]{:S(2)}) async-start(bf16[32,16,1024]{2,1,0:T(8,128)(2,1)} %bitcast.8), calls=%async_computation.2 | async-start | bytes 2097152 | tf_op jit(solution)/shard_map/all_to_all | solution.py:188
  77.9 2.8 %collective-permute-start.2 = (bf16[32,4096]{1,0:T(8,128)(2,1)S(1)}, bf16[32,4096]{1,0:T(8,128)(2,1)S(1)}, u32[]{:S(2)}, u32[]{:S(2)}) collective-permute-start(bf16[32,4096]{1,0:T(8,128)(2,1)S(1)} %get-tuple-element.31), channel_id=1, source_target_pairs={{0,16},{1,113},{8,24},{9,121},{16,32},{17,1},{24,40},{25,9},{32,48... | collective-permute-start | bytes 786440 | tf_op jit(solution)/shard_map/ppermute | solution.py:177
  80.8 3.4 %collective-permute-start.3 = (bf16[32,4096]{1,0:T(8,128)(2,1)S(1)}, bf16[32,4096]{1,0:T(8,128)(2,1)S(1)}, u32[]{:S(2)}, u32[]{:S(2)}) collective-permute-start(bf16[32,4096]{1,0:T(8,128)(2,1)S(1)} %get-tuple-element.32), channel_id=1, source_target_pairs={{0,112},{1,17},{8,120},{9,25},{16,0},{17,33},{24,8},{25,41},{32,16... | collective-permute-start | bytes 786440 | tf_op jit(solution)/shard_map/ppermute | solution.py:177
  84.1 4.5 %collective-permute-start.4 = (bf16[16,4096]{1,0:T(8,128)(2,1)}, bf16[16,4096]{1,0:T(8,128)(2,1)S(1)}, u32[]{:S(2)}, u32[]{:S(2)}) collective-permute-start(bf16[16,4096]{1,0:T(8,128)(2,1)} %copy-done.3), channel_id=1, source_target_pairs={{0,24},{1,105},{8,32},{9,113},{16,40},{17,121},{24,48},{25,1},{32,... | collective-permute-start | bytes 393224 | tf_op jit(solution)/shard_map/ppermute | solution.py:177
  88.7 2.6 %collective-permute-start.5 = (bf16[16,4096]{1,0:T(8,128)(2,1)S(1)}, bf16[16,4096]{1,0:T(8,128)(2,1)S(1)}, u32[]{:S(2)}, u32[]{:S(2)}) collective-permute-start(bf16[16,4096]{1,0:T(8,128)(2,1)S(1)} %get-tuple-element.34), channel_id=1, source_target_pairs={{0,104},{1,25},{8,112},{9,33},{16,120},{17,41},{24,0},{25,49},{32,... | collective-permute-start | bytes 393224 | tf_op jit(solution)/shard_map/ppermute | solution.py:177
  91.2 6.3 %collective-permute-start.6 = (bf16[16,4096]{1,0:T(8,128)(2,1)S(1)}, bf16[16,4096]{1,0:T(8,128)(2,1)S(1)}, u32[]{:S(2)}, u32[]{:S(2)}) collective-permute-start(bf16[16,4096]{1,0:T(8,128)(2,1)S(1)} %get-tuple-element.35), channel_id=1, source_target_pairs={{0,32},{1,97},{8,40},{9,105},{16,48},{17,113},{24,56},{25,121},{32... | collective-permute-start | bytes 393224 | tf_op jit(solution)/shard_map/ppermute | solution.py:177
  97.6 0.8 collective-permute-done.4.refs_3_
  98.4 7.1 %collective-permute-done.5.refs_4_ = bf16[16,4096]{1,0:T(8,128)(2,1)S(1)} collective-permute-done((bf16[16,4096]{1,0:T(8,128)(2,1)S(1)}, bf16[16,4096]{1,0:T(8,128)(2,1)S(1)}, u32[]{:S(2)}, u32[]{:S(2)}) %collective-permute-start.5) | collective-permute-done | bytes 131104 | tf_op jit(solution)/shard_map/ppermute | solution.py:177
  105.5 1.1 collective-permute-done.6.refs_5_
  106.6 0.0 collective-permute-done.2.refs_1_
  106.6 0.0 collective-permute-done.3.refs_2_
  106.6 1.4 shard_map.94
  108.0 0.0 all-to-all-done.2.in_ref
  108.0 0.1 shard_map.95
  108.1 0.0 copy-start.2
  108.1 0.8 copy-done.2
  108.9 10.1 %all-to-all-start.3 = ((bf16[32,16,1024]{2,1,0:T(8,128)(2,1)}), bf16[32,16,1024]{2,1,0:T(8,128)(2,1)}, u32[]{:S(2)}, u32[]{:S(2)}) async-start(bf16[32,16,1024]{2,1,0:T(8,128)(2,1)} %bitcast.15), calls=%async_computation.3 | async-start | bytes 2097152 | tf_op jit(solution)/shard_map/all_to_all | solution.py:188
  119.0 6.8 %collective-permute-start.7 = (bf16[32,8,1024]{2,1,0:T(8,128)(2,1)}, bf16[32,8,1024]{2,1,0:T(8,128)(2,1)S(1)}, u32[]{:S(2)}, u32[]{:S(2)}) collective-permute-start(bf16[32,8,1024]{2,1,0:T(8,128)(2,1)} %copy-done.2), channel_id=1, source_target_pairs={{0,8},{1,121},{8,16},{9,1},{16,24},{17,9},{24,32},{25,17},{32,40},... | collective-permute-start | bytes 1572872 | tf_op jit(solution)/shard_map/ppermute | solution.py:177
  125.8 0.4 shard_map.93
  126.2 1.9 %collective-permute-start.8 = (bf16[32,8,1024]{2,1,0:T(8,128)(2,1)S(1)}, bf16[32,8,1024]{2,1,0:T(8,128)(2,1)}, u32[]{:S(2)}, u32[]{:S(2)}) collective-permute-start(bf16[32,8,1024]{2,1,0:T(8,128)(2,1)S(1)} %get-tuple-element.39), channel_id=1, source_target_pairs={{0,120},{1,9},{8,0},{9,17},{16,8},{17,25},{24,16},{25,33},{32,24},... | collective-permute-start | bytes 1572872 | tf_op jit(solution)/shard_map/ppermute | solution.py:177
  128.2 0.5 fusion.12
  128.6 6.4 %collective-permute-done.7 = bf16[32,8,1024]{2,1,0:T(8,128)(2,1)S(1)} collective-permute-done((bf16[32,8,1024]{2,1,0:T(8,128)(2,1)}, bf16[32,8,1024]{2,1,0:T(8,128)(2,1)S(1)}, u32[]{:S(2)}, u32[]{:S(2)}) %collective-permute-start.7) | collective-permute-done | bytes 524320 | tf_op jit(solution)/shard_map/ppermute | solution.py:177
  135.0 0.3 convolution_add_fusion.1
  135.4 0.8 all-to-all-done.3
  136.1 1.7 %fusion.13 = f32[1024,256]{1,0:T(8,128)S(1)} fusion(bf16[512,1024]{1,0:T(8,128)(2,1)} %bitcast.16, bf16[512,256]{1,0:T(8,128)(2,1)S(1)} %bitcast.35), kind=kOutput, calls=%fused_computation.21 | convolution fusion | flops 268435456 | bytes 2359296 | tf_op jit(solution)/shard_map/dot_general | solution.py:281
  137.8 1.0 collective-permute-done.8
  138.8 2.2 %fusion.2 = bf16[1,1024,256]{2,1,0:T(8,128)(2,1)} fusion(f32[1024,256]{1,0:T(8,128)S(1)} %fusion.13, f32[1024,256]{1,0:T(8,128)S(1)} %convolution_add_fusion.1, bf16[256,256]{1,0:T(8,128)(2,1)S(1)} %bitcast.37, bf16[32,8,1024]{2,1,0:T(8,128)(2,1)} %collective-permute-done.8), kind=kOutput, calls=%fused_computation.4 | convolution fusion | flops 135004160 | bytes 3276800 | tf_op jit(solution)/shard_map/dot_general | solution.py:281
  (10 shorter events, 0.0 us)
Async XLA Ops:
  0.0 15.4 %copy-start = (bf16[1,1,256,1536]{3,2,1,0:T(8,128)(2,1)S(1)}, bf16[1,1,256,1536]{3,2,1,0:T(8,128)(2,1)}, u32[]{:S(2)}) copy-start(bf16[1,1,256,1536]{3,2,1,0:T(8,128)(2,1)} %param.12) | copy-start | bytes 2359300
  1.9 5.1 %copy-start.6 = (s32[384]{0:T(512)S(1)}, s32[384]{0:T(512)}, u32[]{:S(2)}) copy-start(s32[384]{0:T(512)} %constant.40.clone) | copy-start | bytes 4612
  1.9 13.5 %all-to-all-start = ((bf16[4,384,256]{2,1,0:T(8,128)(2,1)}), bf16[4,384,256]{2,1,0:T(8,128)(2,1)S(1)}, u32[]{:S(2)}, u32[]{:S(2)}) async-start(bf16[4,384,256]{2,1,0:T(8,128)(2,1)} %broadcast_in_dim.9), calls=%async_computation | async-start | bytes 1572864 | tf_op jit(solution)/shard_map/all_to_all | solution.py:183
  7.1 0.7 copy-start.5
  7.1 0.7 copy-start.4
  7.8 0.7 copy-start.7
  16.8 49.5 %all-to-all-start.1 = ((bf16[4,256,256]{2,1,0:T(8,128)(2,1)}), bf16[4,256,256]{2,1,0:T(8,128)(2,1)S(1)}, u32[]{:S(2)}, u32[]{:S(2)}) async-start(bf16[4,256,256]{2,1,0:T(8,128)(2,1)} %broadcast_in_dim.20), calls=%async_computation.1 | async-start | bytes 1048576 | tf_op jit(solution)/shard_map/all_to_all | solution.py:183
  22.0 20.0 %collective-permute-start.1 = (bf16[32,4224]{1,0:T(8,128)(2,1)}, bf16[32,4224]{1,0:T(8,128)(2,1)S(1)}, u32[]{:S(2)}, u32[]{:S(2)}) collective-permute-start(bf16[32,4224]{1,0:T(8,128)(2,1)} %shard_map.91.own_ref), channel_id=1, source_target_pairs={{0,96},{1,33},{8,104},{9,41},{16,112},{17,49},{24,120},{25,57},{32... | collective-permute-start | bytes 811016 | tf_op jit(solution)/shard_map/ppermute | solution.py:177
  34.0 27.2 %collective-permute-start = (bf16[32,4224]{1,0:T(8,128)(2,1)}, bf16[32,4224]{1,0:T(8,128)(2,1)S(1)}, u32[]{:S(2)}, u32[]{:S(2)}) collective-permute-start(bf16[32,4224]{1,0:T(8,128)(2,1)} %shard_map.91.own_ref), channel_id=1, source_target_pairs={{0,32},{1,97},{8,40},{9,105},{16,48},{17,113},{24,56},{25,121},{32... | collective-permute-start | bytes 811016 | tf_op jit(solution)/shard_map/ppermute | solution.py:177
  61.1 1.0 copy-start.1
  65.6 0.6 copy-start.3
  66.3 41.7 %all-to-all-start.2 = ((bf16[32,16,1024]{2,1,0:T(8,128)(2,1)}), bf16[32,16,1024]{2,1,0:T(8,128)(2,1)S(1)}, u32[]{:S(2)}, u32[]{:S(2)}) async-start(bf16[32,16,1024]{2,1,0:T(8,128)(2,1)} %bitcast.8), calls=%async_computation.2 | async-start | bytes 2097152 | tf_op jit(solution)/shard_map/all_to_all | solution.py:188
  77.9 28.6 %collective-permute-start.2 = (bf16[32,4096]{1,0:T(8,128)(2,1)S(1)}, bf16[32,4096]{1,0:T(8,128)(2,1)S(1)}, u32[]{:S(2)}, u32[]{:S(2)}) collective-permute-start(bf16[32,4096]{1,0:T(8,128)(2,1)S(1)} %get-tuple-element.31), channel_id=1, source_target_pairs={{0,16},{1,113},{8,24},{9,121},{16,32},{17,1},{24,40},{25,9},{32,48... | collective-permute-start | bytes 786440 | tf_op jit(solution)/shard_map/ppermute | solution.py:177
  80.8 25.8 %collective-permute-start.3 = (bf16[32,4096]{1,0:T(8,128)(2,1)S(1)}, bf16[32,4096]{1,0:T(8,128)(2,1)S(1)}, u32[]{:S(2)}, u32[]{:S(2)}) collective-permute-start(bf16[32,4096]{1,0:T(8,128)(2,1)S(1)} %get-tuple-element.32), channel_id=1, source_target_pairs={{0,112},{1,17},{8,120},{9,25},{16,0},{17,33},{24,8},{25,41},{32,16... | collective-permute-start | bytes 786440 | tf_op jit(solution)/shard_map/ppermute | solution.py:177
  84.1 14.3 %collective-permute-start.4 = (bf16[16,4096]{1,0:T(8,128)(2,1)}, bf16[16,4096]{1,0:T(8,128)(2,1)S(1)}, u32[]{:S(2)}, u32[]{:S(2)}) collective-permute-start(bf16[16,4096]{1,0:T(8,128)(2,1)} %copy-done.3), channel_id=1, source_target_pairs={{0,24},{1,105},{8,32},{9,113},{16,40},{17,121},{24,48},{25,1},{32,... | collective-permute-start | bytes 393224 | tf_op jit(solution)/shard_map/ppermute | solution.py:177
  88.7 16.8 %collective-permute-start.5 = (bf16[16,4096]{1,0:T(8,128)(2,1)S(1)}, bf16[16,4096]{1,0:T(8,128)(2,1)S(1)}, u32[]{:S(2)}, u32[]{:S(2)}) collective-permute-start(bf16[16,4096]{1,0:T(8,128)(2,1)S(1)} %get-tuple-element.34), channel_id=1, source_target_pairs={{0,104},{1,25},{8,112},{9,33},{16,120},{17,41},{24,0},{25,49},{32,... | collective-permute-start | bytes 393224 | tf_op jit(solution)/shard_map/ppermute | solution.py:177
  91.2 15.3 %collective-permute-start.6 = (bf16[16,4096]{1,0:T(8,128)(2,1)S(1)}, bf16[16,4096]{1,0:T(8,128)(2,1)S(1)}, u32[]{:S(2)}, u32[]{:S(2)}) collective-permute-start(bf16[16,4096]{1,0:T(8,128)(2,1)S(1)} %get-tuple-element.35), channel_id=1, source_target_pairs={{0,32},{1,97},{8,40},{9,105},{16,48},{17,113},{24,56},{25,121},{32... | collective-permute-start | bytes 393224 | tf_op jit(solution)/shard_map/ppermute | solution.py:177
  108.1 0.8 copy-start.2
  108.9 27.3 %all-to-all-start.3 = ((bf16[32,16,1024]{2,1,0:T(8,128)(2,1)}), bf16[32,16,1024]{2,1,0:T(8,128)(2,1)}, u32[]{:S(2)}, u32[]{:S(2)}) async-start(bf16[32,16,1024]{2,1,0:T(8,128)(2,1)} %bitcast.15), calls=%async_computation.3 | async-start | bytes 2097152 | tf_op jit(solution)/shard_map/all_to_all | solution.py:188
  119.0 16.0 %collective-permute-start.7 = (bf16[32,8,1024]{2,1,0:T(8,128)(2,1)}, bf16[32,8,1024]{2,1,0:T(8,128)(2,1)S(1)}, u32[]{:S(2)}, u32[]{:S(2)}) collective-permute-start(bf16[32,8,1024]{2,1,0:T(8,128)(2,1)} %copy-done.2), channel_id=1, source_target_pairs={{0,8},{1,121},{8,16},{9,1},{16,24},{17,9},{24,32},{25,17},{32,40},... | collective-permute-start | bytes 1572872 | tf_op jit(solution)/shard_map/ppermute | solution.py:177
  126.2 12.6 %collective-permute-start.8 = (bf16[32,8,1024]{2,1,0:T(8,128)(2,1)S(1)}, bf16[32,8,1024]{2,1,0:T(8,128)(2,1)}, u32[]{:S(2)}, u32[]{:S(2)}) collective-permute-start(bf16[32,8,1024]{2,1,0:T(8,128)(2,1)S(1)} %get-tuple-element.39), channel_id=1, source_target_pairs={{0,120},{1,9},{8,0},{9,17},{16,8},{17,25},{24,16},{25,33},{32,24},... | collective-permute-start | bytes 1572872 | tf_op jit(solution)/shard_map/ppermute | solution.py:177

commit v6 on v4

--- a/solution.py
+++ b/solution.py
@@ -18,9 +18,10 @@
 SMALL = pltpu.CompilerParams(vmem_limit_bytes=12 * 1024 * 1024)
 
 START = (0, -LEAP, LEAP)
-NEAR = ((1, 0), (1, 1), (1, 2), (0, 0), (-1, 0), (-1, 1), (-1, 2), (0, 1))
-FAR = ((0, 2), (2, 0), (2, 1), (2, 2), (-2, 0), (-2, 1), (-2, 2), (3, 1))
+NEAR = ((2, 0), (2, 1), (2, 2), (0, 0), (-2, 0), (-2, 1), (-2, 2), (0, 1))
+FAR = ((0, 2), (1, 0), (1, 1), (1, 2), (-1, 0), (-1, 1), (-1, 2), (3, 1))
 CUTS = (GROUP, 3 * GROUP, 3 * GROUP, GROUP)
+HALVES = ((0, 3), (4, 7))
 
 
 def origins(table, moved):
@@ -29,8 +30,8 @@
 
 SLOTS = (
     origins(NEAR, 0)
-    + origins(NEAR[:4], 1)
-    + origins(NEAR[4:], -1)
+    + origins(NEAR[slice(*HALVES[0])], 2)
+    + origins(NEAR[slice(*HALVES[1])], -2)
     + [(START[block] - step, 0) for step, block in FAR]
 )
 
@@ -174,7 +175,7 @@
 
 def factor_moves(plane, sign, slots):
     moves = []
-    for low, high in ((0, 8), (8, 12), (12, 16), (16, 24)):
+    for low, high in ((0, 8), (8, 11), (11, 14), (14, 22)):
         span = SLOTS[low:high]
         size = len(span)
         to = np.arange(SEATS * size * 2)
@@ -190,27 +191,30 @@
 
 
 def cut_kernel(in_ref, up_ref, down_ref):
-    half = up_ref.shape[1]
-    up_ref[...] = in_ref[:, :half]
-    down_ref[...] = in_ref[:, half:]
+    steps = 2
+    chunk = in_ref.shape[0] // steps
+    for ref, (low, high) in zip((up_ref, down_ref), HALVES, strict=True):
+        size = 2 * (high - low)
+        count = chunk // GROUP * size
+        row = lax.broadcasted_iota(jnp.int32, (count, chunk), 0)
+        goal = lax.broadcasted_iota(jnp.int32, (count, chunk), 1)
+        source = (row * (65536 // size + 1)) >> 16
+        move = (goal == source * GROUP + 2 * low + row - source * size).astype(F32).astype(BF16)
+        for step in range(steps):
+            rows = jnp.dot(
+                move, in_ref[step * chunk : (step + 1) * chunk], preferred_element_type=F32
+            )
+            ref[step * count : (step + 1) * count] = rows.astype(BF16)
 
 
 def halves(array):
     count, rows, width = array.shape
-    steps = 4
-
-    def spec(size):
-        return pl.BlockSpec((count // steps, size, width), lambda i: (i, 0, 0))
-
-    shape = jax.ShapeDtypeStruct((count, rows // 2, width), array.dtype)
-    return pl.pallas_call(
-        cut_kernel,
-        grid=(steps,),
-        in_specs=[spec(rows)],
-        out_specs=[spec(rows // 2)] * 2,
-        out_shape=[shape] * 2,
-        compiler_params=SMALL,
-    )(array)
+    shapes = [
+        jax.ShapeDtypeStruct((count * 2 * (high - low), width), array.dtype) for low, high in HALVES
+    ]
+    return pl.pallas_call(cut_kernel, out_shape=shapes, compiler_params=SMALL)(
+        array.reshape(count * rows, width)
+    )
 
 
 def order_kernel(move_ref, reduced_ref, *out_refs):
@@ -224,7 +228,7 @@
 
 def ordered(moves, reduced):
     replicas, _, rank = reduced.shape
-    sizes = [2 * SEATS * count for count in (8, 4, 4, 8)]
+    sizes = [2 * SEATS * count for count in (8, 3, 3, 8)]
     return pl.pallas_call(
         order_kernel,
         out_shape=[jax.ShapeDtypeStruct((replicas, size, rank), BF16) for size in sizes],
@@ -250,20 +254,19 @@
     reduced = jnp.dot(hidden_act[0, 0], basis, preferred_element_type=F32).astype(BF16)
     reduced = gathered(reduced, "dp")
 
-    near, stay, up2, down2, up3 = picked(plane, sign, own, behind, ahead, parts)
-    up2, down2, up3 = shift(up2, 2), shift(down2, -2), shift(up3, 3)
+    near, stay, up1, down1, up3 = picked(plane, sign, own, behind, ahead, parts)
+    up1, down1, up3 = shift(up1, 1), shift(down1, -1), shift(up3, 3)
     near, reduced = lax.optimization_barrier((near, reduced))
     near = exchanged(near)
     factors = ordered(moves, reduced)
-    far = join([stay, up2, down2, up3], parts)
-    up1, down1 = halves(near)
-    far, up1 = lax.optimization_barrier((far, up1))
+    far = join([stay, up1, down1, up3], parts)
     far = exchanged(far)
-    up1, down1 = shift(up1, 1), shift(down1, -1)
+    up2, down2 = halves(near)
+    up2, down2 = shift(up2, 2), shift(down2, -2)
     total = None
-    for piece, factor in zip((near, up1, down1, far), factors, strict=True):
+    for piece, factor in zip((near, up2, down2, far), factors, strict=True):
         share = lax.dot_general(
-            piece.reshape(-1, piece.shape[2]),
+            piece.reshape(-1, piece.shape[-1]),
             factor.reshape(-1, rank),
             (((0,), (0,)), ((), ())),
             preferred_element_type=F32,

time: 141 us -> 144 us (1.021)
  waiting for transfers between devices: 59.9 us -> 64.2 us
  starting transfers between devices: 62.1 us -> 59.5 us
    all_to_all x2, waiting for transfers between devices: 4.48 us -> 13.3 us  [exchanged(): lax.all_to_all(array, ('dp', 'x', 'core'), split_axis=0, concat_axis=0, t...]
    ppermute x7, starting transfers between devices: 38.5 us -> 33.9 us  [shift(): return lax.ppermute(array, ('z', 'core'), pairs)]
    ppermute x7, waiting for transfers between devices: 48.6 us -> 44 us  [shift(): return lax.ppermute(array, ('z', 'core'), pairs)]
    all_to_all x2, starting transfers between devices: 14.9 us -> 17 us  [exchanged(): lax.all_to_all(array, ('dp', 'x', 'core'), split_axis=0, concat_axis=0, t...]
    unnamed x16 -> x14, local copies, waits for them, and re-layouts: 3.73 us -> 2.96 us
  transfers between devices with their start and end apart: 11 -> 11, of which waited for: 7 -> 7; matrix products, arithmetic and copies ran while one was open for 2% -> 3% of each run, Pallas kernels for 4% -> 5%
where the time goes in v6:
time: 144 us; the launch traced here: 142 us
  waiting for transfers between devices  64.2 us (45%)
  starting transfers between devices  59.5 us (41%)
  Pallas kernels  7.23 us (5%)
  local copies, waits for them, and re-layouts  5.81 us (4%)
  matrix products  5.07 us (4%)
    ppermute x7, waiting for transfers between devices, shift(): return lax.ppermute(array, ('z', 'core'), pairs)  44 us
    ppermute x7, starting transfers between devices, shift(): return lax.ppermute(array, ('z', 'core'), pairs)  33.9 us
    all_to_all x2, starting transfers between devices, exchanged(): lax.all_to_all(array, ('dp', 'x', 'core'), split_axis=0, concat_axis=0, t...  17 us
    all_to_all x2, waiting for transfers between devices, exchanged(): lax.all_to_all(array, ('dp', 'x', 'core'), split_axis=0, concat_axis=0, t...  13.3 us
    all_to_all x2, starting transfers between devices, gathered(): return lax.all_to_all(copies, axis, split_axis=0, concat_axis=0, tiled=True)  8.6 us
    all_to_all x2, waiting for transfers between devices, gathered(): return lax.all_to_all(copies, axis, split_axis=0, concat_axis=0, tiled=True)  6.82 us
    dot_general x4, matrix products, layer(): lax.dot_general(piece.reshape(-1, piece.shape[-1]), factor.reshape(-1, ra...  4.65 us
    unnamed x14, local copies, waits for them, and re-layouts  2.96 us
  transfers between devices with their start and end apart: 11, of which 7 were waited for; matrix products, arithmetic and copies ran while one was open for 3% of the time, Pallas kernels for 5%

profile of v6, /device:TPU:1, one launch (start us, length us, event | category | flops | bytes accessed | tf_op | source)
XLA Modules:
  0.0 142.3 jit_solution(17979017320502967372)
XLA Ops:
  0.0 0.0 copy-start
  0.0 1.9 %broadcast_in_dim.9 = bf16[4,384,256]{2,1,0:T(8,128)(2,1)} broadcast(bf16[384,256]{1,0:T(8,128)(2,1)} %bitcast.37), dimensions={1,2} | broadcast | bytes 983040 | tf_op jit(solution)/shard_map/broadcast_in_dim | solution.py:167
  1.9 0.0 copy-start.5
  1.9 5.1 %all-to-all-start = ((bf16[4,384,256]{2,1,0:T(8,128)(2,1)}), bf16[4,384,256]{2,1,0:T(8,128)(2,1)S(1)}, u32[]{:S(2)}, u32[]{:S(2)}) async-start(bf16[4,384,256]{2,1,0:T(8,128)(2,1)} %broadcast_in_dim.9), calls=%async_computation | async-start | bytes 1572864 | tf_op jit(solution)/shard_map/all_to_all | solution.py:168
  7.1 0.0 copy-start.4
  7.1 0.0 copy-start.3
  7.1 0.0 copy-done.5
  7.1 0.7 copy-done.4
  7.8 0.0 copy-done.3
  7.8 0.6 copy-done.6
  8.4 0.2 fusion.6.move_ref
  8.6 6.8 %all-to-all-done = bf16[4,384,256]{2,1,0:T(8,128)(2,1)S(1)} async-done(((bf16[4,384,256]{2,1,0:T(8,128)(2,1)}), bf16[4,384,256]{2,1,0:T(8,128)(2,1)S(1)}, u32[]{:S(2)}, u32[]{:S(2)}) %all-to-all-start) | async-done | bytes 786464 | tf_op jit(solution)/shard_map/all_to_all | solution.py:168
  15.4 0.0 copy-done
  15.4 0.4 fusion.3
  15.8 0.1 copy.10
  15.9 0.8 broadcast_in_dim.20
  16.8 3.5 %all-to-all-start.1 = ((bf16[4,256,256]{2,1,0:T(8,128)(2,1)}), bf16[4,256,256]{2,1,0:T(8,128)(2,1)S(1)}, u32[]{:S(2)}, u32[]{:S(2)}) async-start(bf16[4,256,256]{2,1,0:T(8,128)(2,1)} %broadcast_in_dim.20), calls=%async_computation.1 | async-start | bytes 1048576 | tf_op jit(solution)/shard_map/all_to_all | solution.py:168
  20.2 1.8 %shard_map.91.own_ref = bf16[32,4224]{1,0:T(8,128)(2,1)} custom-call(bf16[32,4096]{1,0:T(8,128)(2,1)} %grad_ref.1, s32[8,32]{1,0:T(8,128)} %bitcast.38, f32[8,32]{1,0:T(8,128)} %bitcast.39), custom_call_target="tpu_custom_call" | custom-call | tf_op jit(solution)/shard_map/pallas_call | solution.py:245
  22.1 13.3 %collective-permute-start.1 = (bf16[32,4224]{1,0:T(8,128)(2,1)}, bf16[32,4224]{1,0:T(8,128)(2,1)S(1)}, u32[]{:S(2)}, u32[]{:S(2)}) collective-permute-start(bf16[32,4224]{1,0:T(8,128)(2,1)} %shard_map.91.own_ref), channel_id=1, source_target_pairs={{0,88},{1,41},{8,96},{9,49},{16,104},{17,57},{24,112},{25,65},{32,... | collective-permute-start | bytes 811016 | tf_op jit(solution)/shard_map/ppermute | solution.py:162
  35.3 5.9 %collective-permute-start = (bf16[32,4224]{1,0:T(8,128)(2,1)}, bf16[32,4224]{1,0:T(8,128)(2,1)S(1)}, u32[]{:S(2)}, u32[]{:S(2)}) collective-permute-start(bf16[32,4224]{1,0:T(8,128)(2,1)} %shard_map.91.own_ref), channel_id=1, source_target_pairs={{0,40},{1,89},{8,48},{9,97},{16,56},{17,105},{24,64},{25,113},{32,... | collective-permute-start | bytes 811016 | tf_op jit(solution)/shard_map/ppermute | solution.py:162
  41.2 0.1 pad_add_fusion.place_ref
  41.3 2.4 %collective-permute-done.1.ahead_ref = bf16[32,4224]{1,0:T(8,128)(2,1)S(1)} collective-permute-done((bf16[32,4224]{1,0:T(8,128)(2,1)}, bf16[32,4224]{1,0:T(8,128)(2,1)S(1)}, u32[]{:S(2)}, u32[]{:S(2)}) %collective-permute-start.1) | collective-permute-done | bytes 270368 | tf_op jit(solution)/shard_map/ppermute | solution.py:162
  43.7 26.5 %collective-permute-done.behind_ref = bf16[32,4224]{1,0:T(8,128)(2,1)S(1)} collective-permute-done((bf16[32,4224]{1,0:T(8,128)(2,1)}, bf16[32,4224]{1,0:T(8,128)(2,1)S(1)}, u32[]{:S(2)}, u32[]{:S(2)}) %collective-permute-start) | collective-permute-done | bytes 270368 | tf_op jit(solution)/shard_map/ppermute | solution.py:162
  70.2 1.0 copy-done.1
  71.2 2.6 %shard_map.92 = (bf16[4,128,1024]{2,1,0:T(8,128)(2,1)}, bf16[16,4096]{1,0:T(8,128)(2,1)S(1)}, bf16[48,4096]{1,0:T(8,128)(2,1)S(1)}, bf16[48,4096]{1,0:T(8,128)(2,1)S(1)}, bf16[16,4096]{1,0:T(8,128)(2,1)S(1)}) custom-call(s32[2]{0:T(128)S(1)} %pad_add_fusion.place_ref, bf16[32,4224]{1,0:T(8,128)(2,1)S(1)} %copy-done.1, ...), custom_call_target="tpu_custom_call" | custom-call | tf_op jit(solution)/shard_map/pallas_call | solution.py:126
  73.7 0.7 copy-done.2
  74.4 0.0 all-to-all-done.1.reduced_ref
  74.4 7.6 %all-to-all-start.2 = ((bf16[32,16,1024]{2,1,0:T(8,128)(2,1)}), bf16[32,16,1024]{2,1,0:T(8,128)(2,1)S(1)}, u32[]{:S(2)}, u32[]{:S(2)}) async-start(bf16[32,16,1024]{2,1,0:T(8,128)(2,1)} %bitcast.8), calls=%async_computation.2 | async-start | bytes 2097152 | tf_op jit(solution)/shard_map/all_to_all | solution.py:173
  82.0 2.9 %collective-permute-start.4 = (bf16[48,4096]{1,0:T(8,128)(2,1)S(1)}, bf16[48,4096]{1,0:T(8,128)(2,1)S(1)}, u32[]{:S(2)}, u32[]{:S(2)}) collective-permute-start(bf16[48,4096]{1,0:T(8,128)(2,1)S(1)} %get-tuple-element.31), channel_id=1, source_target_pairs={{0,8},{1,121},{8,16},{9,1},{16,24},{17,9},{24,32},{25,17},{32,40},... | collective-permute-start | bytes 1179656 | tf_op jit(solution)/shard_map/ppermute | solution.py:162
  84.9 2.4 %collective-permute-start.5 = (bf16[48,4096]{1,0:T(8,128)(2,1)S(1)}, bf16[48,4096]{1,0:T(8,128)(2,1)S(1)}, u32[]{:S(2)}, u32[]{:S(2)}) collective-permute-start(bf16[48,4096]{1,0:T(8,128)(2,1)S(1)} %get-tuple-element.32), channel_id=1, source_target_pairs={{0,120},{1,9},{8,0},{9,17},{16,8},{17,25},{24,16},{25,33},{32,24},... | collective-permute-start | bytes 1179656 | tf_op jit(solution)/shard_map/ppermute | solution.py:162
  87.3 5.3 %collective-permute-start.6 = (bf16[16,4096]{1,0:T(8,128)(2,1)}, bf16[16,4096]{1,0:T(8,128)(2,1)S(1)}, u32[]{:S(2)}, u32[]{:S(2)}) collective-permute-start(bf16[16,4096]{1,0:T(8,128)(2,1)} %copy-done.2), channel_id=1, source_target_pairs={{0,24},{1,105},{8,32},{9,113},{16,40},{17,121},{24,48},{25,1},{32,... | collective-permute-start | bytes 393224 | tf_op jit(solution)/shard_map/ppermute | solution.py:162
  92.6 5.3 %collective-permute-done.6.refs_3_ = bf16[16,4096]{1,0:T(8,128)(2,1)S(1)} collective-permute-done((bf16[16,4096]{1,0:T(8,128)(2,1)}, bf16[16,4096]{1,0:T(8,128)(2,1)S(1)}, u32[]{:S(2)}, u32[]{:S(2)}) %collective-permute-start.6) | collective-permute-done | bytes 131104 | tf_op jit(solution)/shard_map/ppermute | solution.py:162
  97.9 0.0 collective-permute-done.4.refs_1_
  97.9 2.8 %collective-permute-done.5.refs_2_ = bf16[48,4096]{1,0:T(8,128)(2,1)S(1)} collective-permute-done((bf16[48,4096]{1,0:T(8,128)(2,1)S(1)}, bf16[48,4096]{1,0:T(8,128)(2,1)S(1)}, u32[]{:S(2)}, u32[]{:S(2)}) %collective-permute-start.5) | collective-permute-done | bytes 393248 | tf_op jit(solution)/shard_map/ppermute | solution.py:162
  100.7 1.4 shard_map.95
  102.1 0.0 all-to-all-done.2
  102.1 9.4 %all-to-all-start.3 = ((bf16[32,16,1024]{2,1,0:T(8,128)(2,1)}), bf16[32,16,1024]{2,1,0:T(8,128)(2,1)}, u32[]{:S(2)}, u32[]{:S(2)}) async-start(bf16[32,16,1024]{2,1,0:T(8,128)(2,1)} %bitcast.13), calls=%async_computation.3 | async-start | bytes 2097152 | tf_op jit(solution)/shard_map/all_to_all | solution.py:173
  111.5 0.4 shard_map.93
  111.9 1.1 shard_map.94
  113.0 2.3 %collective-permute-start.2 = (bf16[192,1024]{1,0:T(8,128)(2,1)}, bf16[192,1024]{1,0:T(8,128)(2,1)}, u32[]{:S(2)}, u32[]{:S(2)}) collective-permute-start(bf16[192,1024]{1,0:T(8,128)(2,1)} %get-tuple-element.26), channel_id=1, source_target_pairs={{0,16},{1,113},{8,24},{9,121},{16,32},{17,1},{24,40},{25,9},{32,48... | collective-permute-start | bytes 1179656 | tf_op jit(solution)/shard_map/ppermute | solution.py:162
  115.3 13.3 %all-to-all-done.3 = bf16[32,16,1024]{2,1,0:T(8,128)(2,1)} async-done(((bf16[32,16,1024]{2,1,0:T(8,128)(2,1)}), bf16[32,16,1024]{2,1,0:T(8,128)(2,1)}, u32[]{:S(2)}, u32[]{:S(2)}) %all-to-all-start.3) | async-done | bytes 1048608 | tf_op jit(solution)/shard_map/all_to_all | solution.py:173
  128.6 1.7 %fusion.11 = f32[1024,256]{1,0:T(8,128)S(1)} fusion(bf16[512,1024]{1,0:T(8,128)(2,1)} %bitcast.14, bf16[512,256]{1,0:T(8,128)(2,1)S(1)} %bitcast.33), kind=kOutput, calls=%fused_computation.19 | convolution fusion | flops 268435456 | bytes 2359296 | tf_op jit(solution)/shard_map/dot_general | solution.py:268
  130.3 1.9 %collective-permute-start.3 = (bf16[192,1024]{1,0:T(8,128)(2,1)S(1)}, bf16[192,1024]{1,0:T(8,128)(2,1)S(1)}, u32[]{:S(2)}, u32[]{:S(2)}) collective-permute-start(bf16[192,1024]{1,0:T(8,128)(2,1)S(1)} %get-tuple-element.28), channel_id=1, source_target_pairs={{0,112},{1,17},{8,120},{9,25},{16,0},{17,33},{24,8},{25,41},{32,16... | collective-permute-start | bytes 1179656 | tf_op jit(solution)/shard_map/ppermute | solution.py:162
  132.3 0.5 fusion.10
  132.7 0.0 collective-permute-done.2
  132.8 1.3 convolution_add_fusion.1
  134.1 7.0 %collective-permute-done.3 = bf16[192,1024]{1,0:T(8,128)(2,1)S(1)} collective-permute-done((bf16[192,1024]{1,0:T(8,128)(2,1)S(1)}, bf16[192,1024]{1,0:T(8,128)(2,1)S(1)}, u32[]{:S(2)}, u32[]{:S(2)}) %collective-permute-start.3) | collective-permute-done | bytes 393248 | tf_op jit(solution)/shard_map/ppermute | solution.py:162
  141.1 1.1 fusion.2
  (4 shorter events, 0.0 us)
Async XLA Ops:
  0.0 15.4 %copy-start = (bf16[1,1,256,1536]{3,2,1,0:T(8,128)(2,1)S(1)}, bf16[1,1,256,1536]{3,2,1,0:T(8,128)(2,1)}, u32[]{:S(2)}) copy-start(bf16[1,1,256,1536]{3,2,1,0:T(8,128)(2,1)} %param.12) | copy-start | bytes 2359300
  1.9 5.1 %copy-start.5 = (s32[352]{0:T(512)S(1)}, s32[352]{0:T(512)}, u32[]{:S(2)}) copy-start(s32[352]{0:T(512)} %constant.40.clone) | copy-start | bytes 4228
  1.9 13.5 %all-to-all-start = ((bf16[4,384,256]{2,1,0:T(8,128)(2,1)}), bf16[4,384,256]{2,1,0:T(8,128)(2,1)S(1)}, u32[]{:S(2)}, u32[]{:S(2)}) async-start(bf16[4,384,256]{2,1,0:T(8,128)(2,1)} %broadcast_in_dim.9), calls=%async_computation | async-start | bytes 1572864 | tf_op jit(solution)/shard_map/all_to_all | solution.py:168
  7.1 0.7 copy-start.4
  7.1 0.7 copy-start.3
  7.8 0.7 copy-start.6
  16.8 57.6 %all-to-all-start.1 = ((bf16[4,256,256]{2,1,0:T(8,128)(2,1)}), bf16[4,256,256]{2,1,0:T(8,128)(2,1)S(1)}, u32[]{:S(2)}, u32[]{:S(2)}) async-start(bf16[4,256,256]{2,1,0:T(8,128)(2,1)} %broadcast_in_dim.20), calls=%async_computation.1 | async-start | bytes 1048576 | tf_op jit(solution)/shard_map/all_to_all | solution.py:168
  22.1 21.6 %collective-permute-start.1 = (bf16[32,4224]{1,0:T(8,128)(2,1)}, bf16[32,4224]{1,0:T(8,128)(2,1)S(1)}, u32[]{:S(2)}, u32[]{:S(2)}) collective-permute-start(bf16[32,4224]{1,0:T(8,128)(2,1)} %shard_map.91.own_ref), channel_id=1, source_target_pairs={{0,88},{1,41},{8,96},{9,49},{16,104},{17,57},{24,112},{25,65},{32,... | collective-permute-start | bytes 811016 | tf_op jit(solution)/shard_map/ppermute | solution.py:162
  35.3 34.9 %collective-permute-start = (bf16[32,4224]{1,0:T(8,128)(2,1)}, bf16[32,4224]{1,0:T(8,128)(2,1)S(1)}, u32[]{:S(2)}, u32[]{:S(2)}) collective-permute-start(bf16[32,4224]{1,0:T(8,128)(2,1)} %shard_map.91.own_ref), channel_id=1, source_target_pairs={{0,40},{1,89},{8,48},{9,97},{16,56},{17,105},{24,64},{25,113},{32,... | collective-permute-start | bytes 811016 | tf_op jit(solution)/shard_map/ppermute | solution.py:162
  70.2 1.0 copy-start.1
  73.7 0.7 copy-start.2
  74.4 27.7 %all-to-all-start.2 = ((bf16[32,16,1024]{2,1,0:T(8,128)(2,1)}), bf16[32,16,1024]{2,1,0:T(8,128)(2,1)S(1)}, u32[]{:S(2)}, u32[]{:S(2)}) async-start(bf16[32,16,1024]{2,1,0:T(8,128)(2,1)} %bitcast.8), calls=%async_computation.2 | async-start | bytes 2097152 | tf_op jit(solution)/shard_map/all_to_all | solution.py:173
  82.0 15.9 %collective-permute-start.4 = (bf16[48,4096]{1,0:T(8,128)(2,1)S(1)}, bf16[48,4096]{1,0:T(8,128)(2,1)S(1)}, u32[]{:S(2)}, u32[]{:S(2)}) collective-permute-start(bf16[48,4096]{1,0:T(8,128)(2,1)S(1)} %get-tuple-element.31), channel_id=1, source_target_pairs={{0,8},{1,121},{8,16},{9,1},{16,24},{17,9},{24,32},{25,17},{32,40},... | collective-permute-start | bytes 1179656 | tf_op jit(solution)/shard_map/ppermute | solution.py:162
  84.9 15.8 %collective-permute-start.5 = (bf16[48,4096]{1,0:T(8,128)(2,1)S(1)}, bf16[48,4096]{1,0:T(8,128)(2,1)S(1)}, u32[]{:S(2)}, u32[]{:S(2)}) collective-permute-start(bf16[48,4096]{1,0:T(8,128)(2,1)S(1)} %get-tuple-element.32), channel_id=1, source_target_pairs={{0,120},{1,9},{8,0},{9,17},{16,8},{17,25},{24,16},{25,33},{32,24},... | collective-permute-start | bytes 1179656 | tf_op jit(solution)/shard_map/ppermute | solution.py:162
  87.3 10.6 %collective-permute-start.6 = (bf16[16,4096]{1,0:T(8,128)(2,1)}, bf16[16,4096]{1,0:T(8,128)(2,1)S(1)}, u32[]{:S(2)}, u32[]{:S(2)}) collective-permute-start(bf16[16,4096]{1,0:T(8,128)(2,1)} %copy-done.2), channel_id=1, source_target_pairs={{0,24},{1,105},{8,32},{9,113},{16,40},{17,121},{24,48},{25,1},{32,... | collective-permute-start | bytes 393224 | tf_op jit(solution)/shard_map/ppermute | solution.py:162
  102.1 26.5 %all-to-all-start.3 = ((bf16[32,16,1024]{2,1,0:T(8,128)(2,1)}), bf16[32,16,1024]{2,1,0:T(8,128)(2,1)}, u32[]{:S(2)}, u32[]{:S(2)}) async-start(bf16[32,16,1024]{2,1,0:T(8,128)(2,1)} %bitcast.13), calls=%async_computation.3 | async-start | bytes 2097152 | tf_op jit(solution)/shard_map/all_to_all | solution.py:173
  113.0 19.8 %collective-permute-start.2 = (bf16[192,1024]{1,0:T(8,128)(2,1)}, bf16[192,1024]{1,0:T(8,128)(2,1)}, u32[]{:S(2)}, u32[]{:S(2)}) collective-permute-start(bf16[192,1024]{1,0:T(8,128)(2,1)} %get-tuple-element.26), channel_id=1, source_target_pairs={{0,16},{1,113},{8,24},{9,121},{16,32},{17,1},{24,40},{25,9},{32,48... | collective-permute-start | bytes 1179656 | tf_op jit(solution)/shard_map/ppermute | solution.py:162
  130.3 10.8 %collective-permute-start.3 = (bf16[192,1024]{1,0:T(8,128)(2,1)S(1)}, bf16[192,1024]{1,0:T(8,128)(2,1)S(1)}, u32[]{:S(2)}, u32[]{:S(2)}) collective-permute-start(bf16[192,1024]{1,0:T(8,128)(2,1)S(1)} %get-tuple-element.28), channel_id=1, source_target_pairs={{0,112},{1,17},{8,120},{9,25},{16,0},{17,33},{24,8},{25,41},{32,16... | collective-permute-start | bytes 1179656 | tf_op jit(solution)/shard_map/ppermute | solution.py:162

commit v7 on v6

--- a/solution.py
+++ b/solution.py
@@ -18,8 +18,8 @@
 SMALL = pltpu.CompilerParams(vmem_limit_bytes=12 * 1024 * 1024)
 
 START = (0, -LEAP, LEAP)
-NEAR = ((2, 0), (2, 1), (2, 2), (0, 0), (-2, 0), (-2, 1), (-2, 2), (0, 1))
-FAR = ((0, 2), (1, 0), (1, 1), (1, 2), (-1, 0), (-1, 1), (-1, 2), (3, 1))
+NEAR = ((1, 0), (1, 1), (1, 2), (0, 0), (-1, 0), (-1, 1), (-1, 2), (0, 1))
+FAR = ((0, 2), (2, 0), (2, 1), (2, 2), (-2, 0), (-2, 1), (-2, 2), (3, 1))
 CUTS = (GROUP, 3 * GROUP, 3 * GROUP, GROUP)
 HALVES = ((0, 3), (4, 7))
 
@@ -30,8 +30,8 @@
 
 SLOTS = (
     origins(NEAR, 0)
-    + origins(NEAR[slice(*HALVES[0])], 2)
-    + origins(NEAR[slice(*HALVES[1])], -2)
+    + origins(NEAR[slice(*HALVES[0])], 1)
+    + origins(NEAR[slice(*HALVES[1])], -1)
     + [(START[block] - step, 0) for step, block in FAR]
 )
 
@@ -254,24 +254,26 @@
     reduced = jnp.dot(hidden_act[0, 0], basis, preferred_element_type=F32).astype(BF16)
     reduced = gathered(reduced, "dp")
 
-    near, stay, up1, down1, up3 = picked(plane, sign, own, behind, ahead, parts)
-    up1, down1, up3 = shift(up1, 1), shift(down1, -1), shift(up3, 3)
+    near, stay, up2, down2, up3 = picked(plane, sign, own, behind, ahead, parts)
+    up2, down2, up3 = shift(up2, 2), shift(down2, -2), shift(up3, 3)
     near, reduced = lax.optimization_barrier((near, reduced))
     near = exchanged(near)
     factors = ordered(moves, reduced)
-    far = join([stay, up1, down1, up3], parts)
+    far = join([stay, up2, down2, up3], parts)
     far = exchanged(far)
-    up2, down2 = halves(near)
-    up2, down2 = shift(up2, 2), shift(down2, -2)
-    total = None
-    for piece, factor in zip((near, up2, down2, far), factors, strict=True):
+    up1, down1 = halves(near)
+    up1, down1 = shift(up1, 1), shift(down1, -1)
+    shares = []
+    for piece, factor in zip((near, up1, down1, far), factors, strict=True):
         share = lax.dot_general(
             piece.reshape(-1, piece.shape[-1]),
             factor.reshape(-1, rank),
             (((0,), (0,)), ((), ())),
             preferred_element_type=F32,
         )
-        total = share if total is None else total + share
+        shares.append(share)
+    early = lax.optimization_barrier(shares[0] + shares[1] + shares[2])
+    total = shares[3] + early
     return total.astype(BF16)[None]
 
 

time: 144 us -> 139 us (0.965)
  waiting for transfers between devices: 64.2 us -> 59.1 us
  starting transfers between devices: 59.5 us -> 62.1 us
    all_to_all x2, waiting for transfers between devices: 13.3 us -> 1.56 us  [exchanged(): lax.all_to_all(array, ('dp', 'x', 'core'), split_axis=0, concat_axis=0, t...]
    ppermute x7, waiting for transfers between devices: 44 us -> 50.7 us  [shift(): return lax.ppermute(array, ('z', 'core'), pairs)]
    ppermute x7, starting transfers between devices: 33.9 us -> 38.5 us  [shift(): return lax.ppermute(array, ('z', 'core'), pairs)]
    all_to_all x2, starting transfers between devices: 17 us -> 14.9 us  [exchanged(): lax.all_to_all(array, ('dp', 'x', 'core'), split_axis=0, concat_axis=0, t...]
  transfers between devices with their start and end apart: 11 -> 11, of which waited for: 7 -> 8; matrix products, arithmetic and copies ran while one was open for 3% -> 1% of each run, Pallas kernels for 5% -> 5%
where the time goes in v7:
time: 139 us; the launch traced here: 138 us
  starting transfers between devices  62.1 us (45%)
  waiting for transfers between devices  59.1 us (43%)
  Pallas kernels  6.61 us (5%)
  local copies, waits for them, and re-layouts  5.81 us (4%)
  matrix products  4.09 us (3%)
    ppermute x7, waiting for transfers between devices, shift(): return lax.ppermute(array, ('z', 'core'), pairs)  50.7 us
    ppermute x7, starting transfers between devices, shift(): return lax.ppermute(array, ('z', 'core'), pairs)  38.5 us
    all_to_all x2, starting transfers between devices, exchanged(): lax.all_to_all(array, ('dp', 'x', 'core'), split_axis=0, concat_axis=0, t...  14.9 us
    all_to_all x2, starting transfers between devices, gathered(): return lax.all_to_all(copies, axis, split_axis=0, concat_axis=0, tiled=True)  8.6 us
    all_to_all x2, waiting for transfers between devices, gathered(): return lax.all_to_all(copies, axis, split_axis=0, concat_axis=0, tiled=True)  6.82 us
    dot_general x4, matrix products, layer(): lax.dot_general(piece.reshape(-1, piece.shape[-1]), factor.reshape(-1, ra...  3.68 us
    unnamed x14, local copies, waits for them, and re-layouts  2.96 us
  transfers between devices with their start and end apart: 11, of which 8 were waited for; matrix products, arithmetic and copies ran while one was open for 1% of the time, Pallas kernels for 5%

profile of v7, /device:TPU:1, one launch (start us, length us, event | category | flops | bytes accessed | tf_op | source)
XLA Modules:
  0.0 138.1 jit_solution(2261977058110822347)
XLA Ops:
  0.0 0.0 copy-start
  0.0 1.9 %broadcast_in_dim.9 = bf16[4,384,256]{2,1,0:T(8,128)(2,1)} broadcast(bf16[384,256]{1,0:T(8,128)(2,1)} %bitcast.37), dimensions={1,2} | broadcast | bytes 983040 | tf_op jit(solution)/shard_map/broadcast_in_dim | solution.py:167
  1.9 0.0 copy-start.5
  1.9 5.1 %all-to-all-start.1 = ((bf16[4,384,256]{2,1,0:T(8,128)(2,1)}), bf16[4,384,256]{2,1,0:T(8,128)(2,1)S(1)}, u32[]{:S(2)}, u32[]{:S(2)}) async-start(bf16[4,384,256]{2,1,0:T(8,128)(2,1)} %broadcast_in_dim.9), calls=%async_computation.1 | async-start | bytes 1572864 | tf_op jit(solution)/shard_map/all_to_all | solution.py:168
  7.1 0.0 copy-start.4
  7.1 0.0 copy-start.3
  7.1 0.0 copy-done.5
  7.1 0.7 copy-done.4
  7.8 0.0 copy-done.3
  7.8 0.6 copy-done.6
  8.4 0.2 fusion.5.move_ref
  8.6 6.8 %all-to-all-done.1 = bf16[4,384,256]{2,1,0:T(8,128)(2,1)S(1)} async-done(((bf16[4,384,256]{2,1,0:T(8,128)(2,1)}), bf16[4,384,256]{2,1,0:T(8,128)(2,1)S(1)}, u32[]{:S(2)}, u32[]{:S(2)}) %all-to-all-start.1) | async-done | bytes 786464 | tf_op jit(solution)/shard_map/all_to_all | solution.py:168
  15.4 0.0 copy-done
  15.4 0.4 fusion.2
  15.8 0.1 copy.10
  15.9 0.8 broadcast_in_dim.20
  16.8 3.5 %all-to-all-start.2 = ((bf16[4,256,256]{2,1,0:T(8,128)(2,1)}), bf16[4,256,256]{2,1,0:T(8,128)(2,1)S(1)}, u32[]{:S(2)}, u32[]{:S(2)}) async-start(bf16[4,256,256]{2,1,0:T(8,128)(2,1)} %broadcast_in_dim.20), calls=%async_computation.2 | async-start | bytes 1048576 | tf_op jit(solution)/shard_map/all_to_all | solution.py:168
  20.2 1.8 %shard_map.91.own_ref = bf16[32,4224]{1,0:T(8,128)(2,1)} custom-call(bf16[32,4096]{1,0:T(8,128)(2,1)} %grad_ref.1, s32[8,32]{1,0:T(8,128)} %bitcast.38, f32[8,32]{1,0:T(8,128)} %bitcast.39), custom_call_target="tpu_custom_call" | custom-call | tf_op jit(solution)/shard_map/pallas_call | solution.py:245
  22.1 13.3 %collective-permute-start.1 = (bf16[32,4224]{1,0:T(8,128)(2,1)}, bf16[32,4224]{1,0:T(8,128)(2,1)S(1)}, u32[]{:S(2)}, u32[]{:S(2)}) collective-permute-start(bf16[32,4224]{1,0:T(8,128)(2,1)} %shard_map.91.own_ref), channel_id=1, source_target_pairs={{0,88},{1,41},{8,96},{9,49},{16,104},{17,57},{24,112},{25,65},{32,... | collective-permute-start | bytes 811016 | tf_op jit(solution)/shard_map/ppermute | solution.py:162
  35.3 5.9 %collective-permute-start = (bf16[32,4224]{1,0:T(8,128)(2,1)}, bf16[32,4224]{1,0:T(8,128)(2,1)S(1)}, u32[]{:S(2)}, u32[]{:S(2)}) collective-permute-start(bf16[32,4224]{1,0:T(8,128)(2,1)} %shard_map.91.own_ref), channel_id=1, source_target_pairs={{0,40},{1,89},{8,48},{9,97},{16,56},{17,105},{24,64},{25,113},{32,... | collective-permute-start | bytes 811016 | tf_op jit(solution)/shard_map/ppermute | solution.py:162
  41.2 0.1 pad_add_fusion.place_ref
  41.3 2.4 %collective-permute-done.1.ahead_ref = bf16[32,4224]{1,0:T(8,128)(2,1)S(1)} collective-permute-done((bf16[32,4224]{1,0:T(8,128)(2,1)}, bf16[32,4224]{1,0:T(8,128)(2,1)S(1)}, u32[]{:S(2)}, u32[]{:S(2)}) %collective-permute-start.1) | collective-permute-done | bytes 270368 | tf_op jit(solution)/shard_map/ppermute | solution.py:162
  43.7 26.5 %collective-permute-done.behind_ref = bf16[32,4224]{1,0:T(8,128)(2,1)S(1)} collective-permute-done((bf16[32,4224]{1,0:T(8,128)(2,1)}, bf16[32,4224]{1,0:T(8,128)(2,1)S(1)}, u32[]{:S(2)}, u32[]{:S(2)}) %collective-permute-start) | collective-permute-done | bytes 270368 | tf_op jit(solution)/shard_map/ppermute | solution.py:162
  70.2 1.0 copy-done.1
  71.2 2.6 %shard_map.92 = (bf16[4,128,1024]{2,1,0:T(8,128)(2,1)}, bf16[16,4096]{1,0:T(8,128)(2,1)S(1)}, bf16[48,4096]{1,0:T(8,128)(2,1)S(1)}, bf16[48,4096]{1,0:T(8,128)(2,1)S(1)}, bf16[16,4096]{1,0:T(8,128)(2,1)S(1)}) custom-call(s32[2]{0:T(128)S(1)} %pad_add_fusion.place_ref, bf16[32,4224]{1,0:T(8,128)(2,1)S(1)} %copy-done.1, ...), custom_call_target="tpu_custom_call" | custom-call | tf_op jit(solution)/shard_map/pallas_call | solution.py:126
  73.7 0.7 copy-done.2
  74.4 0.0 all-to-all-done.2.reduced_ref
  74.4 7.6 %all-to-all-start.3 = ((bf16[32,16,1024]{2,1,0:T(8,128)(2,1)}), bf16[32,16,1024]{2,1,0:T(8,128)(2,1)S(1)}, u32[]{:S(2)}, u32[]{:S(2)}) async-start(bf16[32,16,1024]{2,1,0:T(8,128)(2,1)} %bitcast.11), calls=%async_computation.3 | async-start | bytes 2097152 | tf_op jit(solution)/shard_map/all_to_all | solution.py:173
  82.0 4.8 %collective-permute-start.2 = (bf16[48,4096]{1,0:T(8,128)(2,1)S(1)}, bf16[48,4096]{1,0:T(8,128)(2,1)S(1)}, u32[]{:S(2)}, u32[]{:S(2)}) collective-permute-start(bf16[48,4096]{1,0:T(8,128)(2,1)S(1)} %get-tuple-element.21), channel_id=1, source_target_pairs={{0,16},{1,113},{8,24},{9,121},{16,32},{17,1},{24,40},{25,9},{32,48... | collective-permute-start | bytes 1179656 | tf_op jit(solution)/shard_map/ppermute | solution.py:162
  86.8 1.9 %collective-permute-start.3 = (bf16[48,4096]{1,0:T(8,128)(2,1)S(1)}, bf16[48,4096]{1,0:T(8,128)(2,1)S(1)}, u32[]{:S(2)}, u32[]{:S(2)}) collective-permute-start(bf16[48,4096]{1,0:T(8,128)(2,1)S(1)} %get-tuple-element.22), channel_id=1, source_target_pairs={{0,112},{1,17},{8,120},{9,25},{16,0},{17,33},{24,8},{25,41},{32,16... | collective-permute-start | bytes 1179656 | tf_op jit(solution)/shard_map/ppermute | solution.py:162
  88.8 7.4 %collective-permute-start.4 = (bf16[16,4096]{1,0:T(8,128)(2,1)}, bf16[16,4096]{1,0:T(8,128)(2,1)S(1)}, u32[]{:S(2)}, u32[]{:S(2)}) collective-permute-start(bf16[16,4096]{1,0:T(8,128)(2,1)} %copy-done.2), channel_id=1, source_target_pairs={{0,24},{1,105},{8,32},{9,113},{16,40},{17,121},{24,48},{25,1},{32,... | collective-permute-start | bytes 393224 | tf_op jit(solution)/shard_map/ppermute | solution.py:162
  96.2 10.5 %collective-permute-done.4.refs_3_ = bf16[16,4096]{1,0:T(8,128)(2,1)S(1)} collective-permute-done((bf16[16,4096]{1,0:T(8,128)(2,1)}, bf16[16,4096]{1,0:T(8,128)(2,1)S(1)}, u32[]{:S(2)}, u32[]{:S(2)}) %collective-permute-start.4) | collective-permute-done | bytes 131104 | tf_op jit(solution)/shard_map/ppermute | solution.py:162
  106.7 0.0 collective-permute-done.2.refs_1_
  106.7 3.0 %collective-permute-done.3.refs_2_ = bf16[48,4096]{1,0:T(8,128)(2,1)S(1)} collective-permute-done((bf16[48,4096]{1,0:T(8,128)(2,1)S(1)}, bf16[48,4096]{1,0:T(8,128)(2,1)S(1)}, u32[]{:S(2)}, u32[]{:S(2)}) %collective-permute-start.3) | collective-permute-done | bytes 393248 | tf_op jit(solution)/shard_map/ppermute | solution.py:162
  109.7 1.4 %shard_map.93 = bf16[4,128,1024]{2,1,0:T(8,128)(2,1)} custom-call(bf16[16,4096]{1,0:T(8,128)(2,1)S(1)} %get-tuple-element.20.refs_0_, bf16[48,4096]{1,0:T(8,128)(2,1)S(1)} %collective-permute-done.2.refs_1_, bf16[48,4096]{1,0:T(8,128)(2,1)S(1)} %collective-permute-done.3.refs_2_, bf16[16,4096]{1,0:T(8,128)(2,1)S(1)} %collective-permute-done.4.refs_3_), custom_call_target="tpu_custom_call" | custom-call | tf_op jit(solution)/shard_map/pallas_call | solution.py:149
  111.1 0.0 all-to-all-done.3
  111.1 7.3 %all-to-all-start = ((bf16[32,16,1024]{2,1,0:T(8,128)(2,1)}), bf16[32,16,1024]{2,1,0:T(8,128)(2,1)}, u32[]{:S(2)}, u32[]{:S(2)}) async-start(bf16[32,16,1024]{2,1,0:T(8,128)(2,1)} %bitcast.4), calls=%async_computation | async-start | bytes 2097152 | tf_op jit(solution)/shard_map/all_to_all | solution.py:173
  118.5 0.5 shard_map.95
  118.9 1.9 %collective-permute-start.5 = (bf16[192,1024]{1,0:T(8,128)(2,1)S(1)}, bf16[192,1024]{1,0:T(8,128)(2,1)S(1)}, u32[]{:S(2)}, u32[]{:S(2)}) collective-permute-start(bf16[192,1024]{1,0:T(8,128)(2,1)S(1)} %get-tuple-element.31), channel_id=1, source_target_pairs={{0,8},{1,121},{8,16},{9,1},{16,24},{17,9},{24,32},{25,17},{32,40},... | collective-permute-start | bytes 1179656 | tf_op jit(solution)/shard_map/ppermute | solution.py:162
  120.8 0.4 shard_map.94
  121.2 3.4 %collective-permute-start.6 = (bf16[192,1024]{1,0:T(8,128)(2,1)S(1)}, bf16[192,1024]{1,0:T(8,128)(2,1)S(1)}, u32[]{:S(2)}, u32[]{:S(2)}) collective-permute-start(bf16[192,1024]{1,0:T(8,128)(2,1)S(1)} %get-tuple-element.33), channel_id=1, source_target_pairs={{0,120},{1,9},{8,0},{9,17},{16,8},{17,25},{24,16},{25,33},{32,24},... | collective-permute-start | bytes 1179656 | tf_op jit(solution)/shard_map/ppermute | solution.py:162
  124.6 0.5 fusion.9
  125.1 2.9 %collective-permute-done.5 = bf16[192,1024]{1,0:T(8,128)(2,1)S(1)} collective-permute-done((bf16[192,1024]{1,0:T(8,128)(2,1)S(1)}, bf16[192,1024]{1,0:T(8,128)(2,1)S(1)}, u32[]{:S(2)}, u32[]{:S(2)}) %collective-permute-start.5) | collective-permute-done | bytes 393248 | tf_op jit(solution)/shard_map/ppermute | solution.py:162
  128.0 0.3 convolution_add_fusion.1
  128.3 5.3 %collective-permute-done.6 = bf16[192,1024]{1,0:T(8,128)(2,1)S(1)} collective-permute-done((bf16[192,1024]{1,0:T(8,128)(2,1)S(1)}, bf16[192,1024]{1,0:T(8,128)(2,1)S(1)}, u32[]{:S(2)}, u32[]{:S(2)}) %collective-permute-start.6) | collective-permute-done | bytes 393248 | tf_op jit(solution)/shard_map/ppermute | solution.py:162
  133.6 0.3 convolution_add_fusion
  134.0 1.6 %all-to-all-done = bf16[32,16,1024]{2,1,0:T(8,128)(2,1)} async-done(((bf16[32,16,1024]{2,1,0:T(8,128)(2,1)}), bf16[32,16,1024]{2,1,0:T(8,128)(2,1)}, u32[]{:S(2)}, u32[]{:S(2)}) %all-to-all-start) | async-done | bytes 1048608 | tf_op jit(solution)/shard_map/all_to_all | solution.py:173
  135.5 2.5 %fusion.1 = bf16[1,1024,256]{2,1,0:T(8,128)(2,1)} fusion(f32[1024,256]{1,0:T(8,128)S(1)} %convolution_add_fusion, bf16[512,1024]{1,0:T(8,128)(2,1)} %bitcast.5, bf16[512,256]{1,0:T(8,128)(2,1)S(1)} %bitcast.33), kind=kOutput, calls=%fused_computation.4 | convolution fusion | flops 268959744 | bytes 2883584 | tf_op jit(solution)/shard_map/dot_general | solution.py:268
  (4 shorter events, 0.0 us)
Async XLA Ops:
  0.0 15.4 %copy-start = (bf16[1,1,256,1536]{3,2,1,0:T(8,128)(2,1)S(1)}, bf16[1,1,256,1536]{3,2,1,0:T(8,128)(2,1)}, u32[]{:S(2)}) copy-start(bf16[1,1,256,1536]{3,2,1,0:T(8,128)(2,1)} %param.12) | copy-start | bytes 2359300
  1.9 5.1 %copy-start.5 = (s32[352]{0:T(512)S(1)}, s32[352]{0:T(512)}, u32[]{:S(2)}) copy-start(s32[352]{0:T(512)} %constant.40.clone) | copy-start | bytes 4228
  1.9 13.5 %all-to-all-start.1 = ((bf16[4,384,256]{2,1,0:T(8,128)(2,1)}), bf16[4,384,256]{2,1,0:T(8,128)(2,1)S(1)}, u32[]{:S(2)}, u32[]{:S(2)}) async-start(bf16[4,384,256]{2,1,0:T(8,128)(2,1)} %broadcast_in_dim.9), calls=%async_computation.1 | async-start | bytes 1572864 | tf_op jit(solution)/shard_map/all_to_all | solution.py:168
  7.1 0.7 copy-start.4
  7.1 0.7 copy-start.3
  7.8 0.7 copy-start.6
  16.8 57.6 %all-to-all-start.2 = ((bf16[4,256,256]{2,1,0:T(8,128)(2,1)}), bf16[4,256,256]{2,1,0:T(8,128)(2,1)S(1)}, u32[]{:S(2)}, u32[]{:S(2)}) async-start(bf16[4,256,256]{2,1,0:T(8,128)(2,1)} %broadcast_in_dim.20), calls=%async_computation.2 | async-start | bytes 1048576 | tf_op jit(solution)/shard_map/all_to_all | solution.py:168
  22.1 21.6 %collective-permute-start.1 = (bf16[32,4224]{1,0:T(8,128)(2,1)}, bf16[32,4224]{1,0:T(8,128)(2,1)S(1)}, u32[]{:S(2)}, u32[]{:S(2)}) collective-permute-start(bf16[32,4224]{1,0:T(8,128)(2,1)} %shard_map.91.own_ref), channel_id=1, source_target_pairs={{0,88},{1,41},{8,96},{9,49},{16,104},{17,57},{24,112},{25,65},{32,... | collective-permute-start | bytes 811016 | tf_op jit(solution)/shard_map/ppermute | solution.py:162
  35.3 34.9 %collective-permute-start = (bf16[32,4224]{1,0:T(8,128)(2,1)}, bf16[32,4224]{1,0:T(8,128)(2,1)S(1)}, u32[]{:S(2)}, u32[]{:S(2)}) collective-permute-start(bf16[32,4224]{1,0:T(8,128)(2,1)} %shard_map.91.own_ref), channel_id=1, source_target_pairs={{0,40},{1,89},{8,48},{9,97},{16,56},{17,105},{24,64},{25,113},{32,... | collective-permute-start | bytes 811016 | tf_op jit(solution)/shard_map/ppermute | solution.py:162
  70.2 1.0 copy-start.1
  73.7 0.7 copy-start.2
  74.4 36.7 %all-to-all-start.3 = ((bf16[32,16,1024]{2,1,0:T(8,128)(2,1)}), bf16[32,16,1024]{2,1,0:T(8,128)(2,1)S(1)}, u32[]{:S(2)}, u32[]{:S(2)}) async-start(bf16[32,16,1024]{2,1,0:T(8,128)(2,1)} %bitcast.11), calls=%async_computation.3 | async-start | bytes 2097152 | tf_op jit(solution)/shard_map/all_to_all | solution.py:173
  82.0 24.7 %collective-permute-start.2 = (bf16[48,4096]{1,0:T(8,128)(2,1)S(1)}, bf16[48,4096]{1,0:T(8,128)(2,1)S(1)}, u32[]{:S(2)}, u32[]{:S(2)}) collective-permute-start(bf16[48,4096]{1,0:T(8,128)(2,1)S(1)} %get-tuple-element.21), channel_id=1, source_target_pairs={{0,16},{1,113},{8,24},{9,121},{16,32},{17,1},{24,40},{25,9},{32,48... | collective-permute-start | bytes 1179656 | tf_op jit(solution)/shard_map/ppermute | solution.py:162
  86.8 22.9 %collective-permute-start.3 = (bf16[48,4096]{1,0:T(8,128)(2,1)S(1)}, bf16[48,4096]{1,0:T(8,128)(2,1)S(1)}, u32[]{:S(2)}, u32[]{:S(2)}) collective-permute-start(bf16[48,4096]{1,0:T(8,128)(2,1)S(1)} %get-tuple-element.22), channel_id=1, source_target_pairs={{0,112},{1,17},{8,120},{9,25},{16,0},{17,33},{24,8},{25,41},{32,16... | collective-permute-start | bytes 1179656 | tf_op jit(solution)/shard_map/ppermute | solution.py:162
  88.8 18.0 %collective-permute-start.4 = (bf16[16,4096]{1,0:T(8,128)(2,1)}, bf16[16,4096]{1,0:T(8,128)(2,1)S(1)}, u32[]{:S(2)}, u32[]{:S(2)}) collective-permute-start(bf16[16,4096]{1,0:T(8,128)(2,1)} %copy-done.2), channel_id=1, source_target_pairs={{0,24},{1,105},{8,32},{9,113},{16,40},{17,121},{24,48},{25,1},{32,... | collective-permute-start | bytes 393224 | tf_op jit(solution)/shard_map/ppermute | solution.py:162
  111.1 24.4 %all-to-all-start = ((bf16[32,16,1024]{2,1,0:T(8,128)(2,1)}), bf16[32,16,1024]{2,1,0:T(8,128)(2,1)}, u32[]{:S(2)}, u32[]{:S(2)}) async-start(bf16[32,16,1024]{2,1,0:T(8,128)(2,1)} %bitcast.4), calls=%async_computation | async-start | bytes 2097152 | tf_op jit(solution)/shard_map/all_to_all | solution.py:173
  118.9 9.1 %collective-permute-start.5 = (bf16[192,1024]{1,0:T(8,128)(2,1)S(1)}, bf16[192,1024]{1,0:T(8,128)(2,1)S(1)}, u32[]{:S(2)}, u32[]{:S(2)}) collective-permute-start(bf16[192,1024]{1,0:T(8,128)(2,1)S(1)} %get-tuple-element.31), channel_id=1, source_target_pairs={{0,8},{1,121},{8,16},{9,1},{16,24},{17,9},{24,32},{25,17},{32,40},... | collective-permute-start | bytes 1179656 | tf_op jit(solution)/shard_map/ppermute | solution.py:162
  121.2 12.4 %collective-permute-start.6 = (bf16[192,1024]{1,0:T(8,128)(2,1)S(1)}, bf16[192,1024]{1,0:T(8,128)(2,1)S(1)}, u32[]{:S(2)}, u32[]{:S(2)}) collective-permute-start(bf16[192,1024]{1,0:T(8,128)(2,1)S(1)} %get-tuple-element.33), channel_id=1, source_target_pairs={{0,120},{1,9},{8,0},{9,17},{16,8},{17,25},{24,16},{25,33},{32,24},... | collective-permute-start | bytes 1179656 | tf_op jit(solution)/shard_map/ppermute | solution.py:162
